TPU v7x, 512 devices: a whole 4x4x16 slice. The times are simulated.
512 devices in a mesh: seq: 32 (over z, core), table: 16 (over x, y).
Axes of the slice: x: 4, y: 4, z: 16, core: 2. Of those that a mesh axis runs over, the one named last changes fastest.
Arguments:
- columns: bfloat16 [16, 8192, 512], P(None, 'seq', 'table'), may hold values from -6 to 6
- gaps: float32 [16, 8192], P('table', 'seq'), may hold values from 0.2 to 9830.4
- norm_in: float32 [512], replicated, may hold values from 0.1 to 1.9
- w_gate: bfloat16 [512, 1024], replicated, may hold values from -0.25 to 0.25
- w_xbc: bfloat16 [512, 1280], replicated, may hold values from -0.25 to 0.25
- w_step: bfloat16 [512, 16], replicated, may hold values from -0.25 to 0.25
- step_bias: float32 [16], replicated, may hold values from -1 to 1
- conv_weight: float32 [4, 1280], replicated, may hold values from -1 to 1
- conv_bias: float32 [1280], replicated, may hold values from -1.5 to 1.5
- rates: float32 [16], replicated, may hold values from 6.1035156e-06 to 0.04
- norm_out: float32 [1024], replicated, may hold values from 0.1 to 1.9
- w_out: bfloat16 [1024, 512], replicated, may hold values from -0.1875 to 0.1875
Outputs:
- mixed: bfloat16 [16, 8192, 512], P('table', 'seq')
All inputs are finite; a program needn't handle non-finite values.
Results may differ from a plain program's by a relative error of at most 0.02.
Values may be sent and summed in bfloat16 or wider, within the bound.
No kernel may reach another device: no remote copies, remote signals or barrier semaphores. Data moves between devices by JAX's collectives and lax.ppermute only.
A program may use at most 64 MiB of HBM per device.

v0:
```python
import jax
import jax.numpy as jnp
from jax import lax
from jax.sharding import PartitionSpec as P

BLOCK = 256


epsilon = 1e-05


def entering(shard, axis, join, neutral):
    place = lax.axis_index(axis)
    gathered = jax.tree.map(
        lambda a, kind: lax.all_gather(a.astype(kind), axis), shard, (jnp.bfloat16, jnp.bfloat16)
    )
    state = jax.tree.map(lambda a, e: jnp.zeros_like(a) + jnp.asarray(e, a.dtype), shard, neutral)

    def one(step, state):
        return join(
            state,
            jax.tree.map(
                lambda a, own: lax.dynamic_index_in_dim(a, step, 0, False).astype(own.dtype),
                gathered,
                shard,
            ),
        )

    return lax.fori_loop(0, place, one, state)


def passed_along(block, axis, distance):
    devices = range(lax.axis_size(axis))
    route = [(i - distance, i) for i in devices if i - distance in devices]
    return lax.ppermute(block, axis, route)


def rms_rows(values, gain):
    return values * lax.rsqrt(jnp.mean(values * values, axis=-1, keepdims=True) + epsilon) * gain


def block_terms(cx, cb, cc, cdt, cda):
    length = cx.shape[0]
    cs = jnp.cumsum(cda, axis=0)
    scores = jnp.dot(cc, cb.T, preferred_element_type=jnp.float32)
    trail = cs.T
    diff = trail[:, :, None] - trail[:, None, :]
    rows = lax.broadcasted_iota(jnp.int32, (length, length), 0)
    cols = lax.broadcasted_iota(jnp.int32, (length, length), 1)
    factor = jnp.exp(jnp.where((rows >= cols)[None], diff, -jnp.inf))
    mix = (scores[None] * factor * cdt.T[:, None, :]).astype(jnp.bfloat16)
    y_in = jnp.einsum("hts,shp->thp", mix, cx, preferred_element_type=jnp.float32)
    weighted = ((jnp.exp(cs[-1][None, :] - cs) * cdt)[:, :, None] * cx.astype(jnp.float32)).astype(
        jnp.bfloat16
    )
    block_state = jnp.einsum("shp,sn->hpn", weighted, cb, preferred_element_type=jnp.float32)
    return (y_in, block_state, cs)


def local_pass(xs, bm, cm, steps_dt, decay):
    length, heads, head_dim = xs.shape
    state_width = bm.shape[1]
    count = length // BLOCK
    blocks = (
        xs.reshape(count, BLOCK, heads, head_dim),
        bm.reshape(count, BLOCK, state_width),
        cm.reshape(count, BLOCK, state_width),
        steps_dt.reshape(count, BLOCK, heads),
        decay.reshape(count, BLOCK, heads),
    )

    def one_block(block):
        return block_terms(block[0], block[1], block[2], block[3], block[4])

    y_in, states, cs = lax.map(one_block, blocks)
    ends = cs[:, -1, :]

    def walk(state, paired):
        return (jnp.exp(paired[0])[:, None, None] * state + paired[1], state)

    final, entries = lax.scan(walk, jnp.zeros(states.shape[1:], jnp.float32), (ends, states))
    starts = jnp.cumsum(ends, axis=0) - ends
    total = jnp.sum(ends, axis=0)
    return (y_in, cs, entries, starts, final, total)


def carried_output(cm, cs, entries, starts, incoming):
    count, length = (cs.shape[0], cs.shape[1])
    queries = cm.reshape(count, length, cm.shape[1])
    enter = (entries + jnp.exp(starts)[:, :, None, None] * incoming[None]).astype(jnp.bfloat16)
    picked = jnp.einsum("ktn,khpn->kthp", queries, enter, preferred_element_type=jnp.float32)
    return jnp.exp(cs)[..., None] * picked


def carry_in(total_part, final_part):

    def combine(earlier, later):
        return (earlier[0] * later[0], later[0][:, :, None, None] * earlier[1] + later[1])

    identity = (jnp.ones_like(total_part), jnp.zeros_like(final_part))
    prefix = entering((jnp.exp(total_part), final_part), "seq", combine, identity)
    return prefix[1]


def local(
    columns,
    gaps,
    norm_in,
    w_gate,
    w_xbc,
    w_step,
    step_bias,
    conv_weight,
    conv_bias,
    rates,
    norm_out,
    w_out,
):
    inner = w_gate.shape[1]
    heads = w_step.shape[1]
    head_dim = inner // heads
    state_width = (w_xbc.shape[1] - inner) // 2
    reach = conv_weight.shape[0] - 1
    normed = rms_rows(
        lax.all_to_all(columns, "table", split_axis=0, concat_axis=2, tiled=True).astype(
            jnp.float32
        ),
        norm_in,
    ).astype(jnp.bfloat16)
    gate = jnp.einsum("brd,de->bre", normed, w_gate, preferred_element_type=jnp.float32).astype(
        jnp.bfloat16
    )
    xbc = jnp.einsum("brd,de->bre", normed, w_xbc, preferred_element_type=jnp.float32).astype(
        jnp.bfloat16
    )
    step_raw = jnp.einsum("brd,de->bre", normed, w_step, preferred_element_type=jnp.float32)
    gate, xbc, step_raw, normed = (gate, xbc, step_raw, normed)
    hists, length = (xbc.shape[0], xbc.shape[1])
    rim = passed_along(xbc[:, length - reach :, :], "seq", 1)
    padded = jnp.concatenate([rim, xbc], axis=1).astype(jnp.float32)
    conv = conv_bias + conv_weight[0] * padded[:, 0:length]
    for offset in range(1, reach + 1):
        conv = conv + conv_weight[offset] * padded[:, offset : offset + length]
    act = jax.nn.silu(conv).astype(jnp.bfloat16)
    xs = act[:, :, :inner].reshape(hists, length, heads, head_dim)
    bm = act[:, :, inner : inner + state_width]
    cm = act[:, :, inner + state_width :]
    steps_dt = jax.nn.softplus(step_raw + step_bias)
    decay = -rates * steps_dt * gaps[:, :, None]
    y_in, cs, entries, starts, final, total = jax.vmap(local_pass)(xs, bm, cm, steps_dt, decay)
    incoming = carry_in(total, final)
    state_terms = jax.vmap(carried_output)(cm, cs, entries, starts, incoming)
    y = (y_in + state_terms).reshape(hists, length, inner)
    gated = y * jax.nn.silu(gate.astype(jnp.float32))
    out_normed = rms_rows(gated, norm_out).astype(jnp.bfloat16)
    return jnp.einsum("bri,id->brd", out_normed, w_out, preferred_element_type=jnp.float32).astype(
        jnp.bfloat16
    )


def solution(mesh):
    in_specs = (
        P(None, "seq", "table"),
        P("table", "seq"),
        P(),
        P(),
        P(),
        P(),
        P(),
        P(),
        P(),
        P(),
        P(),
        P(),
    )
    out_specs = P("table", "seq", None)
    return jax.shard_map(local, mesh=mesh, in_specs=in_specs, out_specs=out_specs, check_vma=False)
```

profile of v0, /device:TPU:481, one launch (start us, length us, event | category | flops | bytes accessed | tf_op | source)
XLA Modules:
  0.0 161.7 jit_solution(6078095798950816290)
XLA Ops:
  6.5 6.9 %all-to-all-start = ((bf16[16,256,32]{1,2,0:T(8,128)(2,1)}), bf16[16,256,32]{1,2,0:T(8,128)(2,1)S(1)}, u32[]{:S(2)}, u32[]{:S(2)}) async-start(bf16[16,256,32]{1,2,0:T(8,128)(2,1)} %param.14), calls=%async_computation | async-start | bytes 524288 | tf_op jit(solution)/shard_map/all_to_all | solution.py:125
  14.2 1.5 slice_reduce_fusion.5
  15.7 5.2 %all-to-all-done = bf16[16,256,32]{1,2,0:T(8,128)(2,1)S(1)} async-done(((bf16[16,256,32]{1,2,0:T(8,128)(2,1)}), bf16[16,256,32]{1,2,0:T(8,128)(2,1)S(1)}, u32[]{:S(2)}, u32[]{:S(2)}) %all-to-all-start) | async-done | bytes 262176 | tf_op jit(solution)/shard_map/all_to_all | solution.py:125
  24.6 1.3 collective-permute-start
  27.1 2.0 %collective-permute-done = bf16[1,3,1280]{2,1,0:T(4,128)(2,1)S(1)} collective-permute-done((bf16[1,3,1280]{2,1,0:T(4,128)(2,1)S(1)}, bf16[1,3,1280]{2,1,0:T(4,128)(2,1)S(1)}, u32[]{:S(2)}, u32[]{:S(2)}) %collective-permute-start) | collective-permute-done | bytes 7712 | tf_op jit(solution)/shard_map/ppermute | solution.py:35
  29.2 1.2 maximum_convert_fusion
  31.3 0.9 multiply_convert_fusion.6
  32.2 1.3 copy.41
  33.5 1.7 %fusion.14 = bf16[16,64,128]{2,1,0:T(8,128)(2,1)} fusion(bf16[256,16,64]{0,2,1:T(8,128)(2,1)S(1)} %bitcast.113, f32[16]{0:T(128)} %get-tuple-element.112, bf16[1,256,1280]{2,1,0:T(8,128)(2,1)S(1)} %multiply_convert_fusion.4), kind=kOutput, calls=%fused_computation.29 | convolution fusion | flops 67371008 | bytes 852032 | tf_op jit(solution)/shard_map/vmap()/while/body/eval_jaxpr/shp,sn->hpn/dot_general | solution.py:56
  35.4 29.8 %all-gather = bf16[32,1,1,16]{3,2,1,0:T(2,128)(2,1)S(1)} all-gather(bf16[1,1,1,16]{3,2,1,0:T(2,128)(2,1)S(1)} %copy.38), channel_id=2, replica_groups=mesh['seq'=32,'table'=16] {'seq'}, dimensions={0}, use_global_device_ids=true | all-gather | bytes 1056 | tf_op jit(solution)/shard_map/all_gather | solution.py:15
  65.8 2.4 %fusion.8 = f32[256,16,64]{0,2,1:T(8,128)} fusion(bf16[256,16,64]{0,2,1:T(8,128)(2,1)S(1)} %bitcast.114, f32[16,256]{1,0:T(8,128)S(1)} %bitcast.116, f32[16,256]{1,0:T(8,128)S(1)} %bitcast_add_fusion, f32[256,256]{1,0:T(8,128)S(1)} %fusion.29, pred[256,256]{1,0:T(8,128)(4,1)S(1)} %iota_compare_fusion), kind=kOutput, calls=%fused_computation.12 | convolution fusion | flops 139460608 | bytes 1933312 | tf_op jit(solution)/shard_map/vmap()/while/body/eval_jaxpr/hts,shp->thp/dot_general | solution.py:52
  68.3 44.2 %all-gather.4.cloned.1.call-done = bf16[512,64,128]{2,1,0:T(8,128)(2,1)} async-done(((bf16[16,64,128]{2,1,0:T(8,128)(2,1)}), bf16[512,64,128]{2,1,0:T(8,128)(2,1)}) %all-gather.4.cloned.1.call-update) | async-done | bytes 8388624 | tf_op jit(solution)/shard_map/all_gather | solution.py:15
  112.5 35.9 %while.3 = (s32[]{:T(128)}, f32[1,16,64,128]{3,2,1,0:T(8,128)S(1)}, s32[]{:T(128)}, bf16[32,1,16]{2,1,0:T(2,128)(2,1)S(1)}, bf16[32,1,16,64,128]{4,3,2,1,0:T(8,128)(2,1)}, /*index=5*/s32[]{:T(128)}, s32[]{:T(128)}, s32[]{:T(128)}) while((s32[]{:T(128)}, f32[1,16,64,128]{3,2,1,0:T(8,128)S(1)}, s32[]{:T(128)}, bf16[32,1,16]{2,1,0:T(2,128)(2,1)S(1)}, ...), condition=%wide.region_4.5_spmd, body=%wide.region_3.4_spmd.sunk | while | flops 393237 | bytes 1311007 | solution.py:29
  112.5 1.1 convert_add_fusion.2
  113.7 1.1 convert_add_fusion.2
  114.9 1.1 convert_add_fusion.2
  116.0 1.1 convert_add_fusion.2
  117.2 1.1 convert_add_fusion.2
  118.3 1.1 convert_add_fusion.2
  119.5 1.1 convert_add_fusion.2
  120.6 1.1 convert_add_fusion.2
  121.8 1.1 convert_add_fusion.2
  123.0 1.1 convert_add_fusion.2
  124.1 1.1 convert_add_fusion.2
  125.3 1.1 convert_add_fusion.2
  126.4 1.1 convert_add_fusion.2
  127.6 1.1 convert_add_fusion.2
  128.7 1.1 convert_add_fusion.2
  129.9 1.1 convert_add_fusion.2
  131.1 1.1 convert_add_fusion.2
  132.2 1.1 convert_add_fusion.2
  133.4 1.1 convert_add_fusion.2
  134.5 1.1 convert_add_fusion.2
  135.7 1.1 convert_add_fusion.2
  136.8 1.1 convert_add_fusion.2
  138.0 1.1 convert_add_fusion.2
  139.2 1.1 convert_add_fusion.2
  140.3 1.1 convert_add_fusion.2
  141.5 1.1 convert_add_fusion.2
  142.6 1.1 convert_add_fusion.2
  143.8 1.1 convert_add_fusion.2
  145.0 1.1 convert_add_fusion.2
  146.1 1.1 convert_add_fusion.2
  147.3 1.1 convert_add_fusion.2
  148.4 1.6 fusion.9
  150.0 1.3 copy.44
  151.3 2.3 %multiply_reduce_fusion = (f32[256]{0:T(256)S(1)}, f32[256,1024]{1,0:T(8,128)S(1)}) fusion(f32[256,1024]{1,0:T(8,128)} %copy.44, bf16[256,512]{0,1:T(8,128)(2,1)S(1)} %copy-done.3, bf16[512,1024]{1,0:T(8,128)(2,1)} %param.17), kind=kOutput, calls=%fused_computation.37 | convolution fusion | flops 270794496 | bytes 3408896 | tf_op jit(solution)/shard_map/brd,de->bre/dot_general | solution.py:130
  153.7 1.2 fusion.15
  (110 shorter events, 7.5 us)
Async XLA Ops:
  6.5 17.5 %copy-start = (bf16[512,1280]{1,0:T(8,128)(2,1)S(1)}, bf16[512,1280]{1,0:T(8,128)(2,1)}, u32[]{:S(2)}) copy-start(bf16[512,1280]{1,0:T(8,128)(2,1)} %param.18) | copy-start | bytes 3932164
  6.5 15.3 %copy-start.16 = (bf16[512,16]{0,1:T(8,128)(2,1)S(1)}, bf16[512,16]{0,1:T(8,128)(2,1)}, u32[]{:S(2)}) copy-start(bf16[512,16]{0,1:T(8,128)(2,1)} %param.19) | copy-start | bytes 49156
  6.5 15.3 %copy-start.20 = (f32[16]{0:T(128)S(1)}, f32[16]{0:T(128)}, u32[]{:S(2)}) copy-start(f32[16]{0:T(128)} %param.20) | copy-start | bytes 196
  6.5 15.5 %copy-start.19 = (f32[1,256]{1,0:T(1,128)S(1)}, f32[1,256]{1,0:T(1,128)}, u32[]{:S(2)}) copy-start(f32[1,256]{1,0:T(1,128)} %param.15) | copy-start | bytes 3076
  6.5 14.4 %all-to-all-start = ((bf16[16,256,32]{1,2,0:T(8,128)(2,1)}), bf16[16,256,32]{1,2,0:T(8,128)(2,1)S(1)}, u32[]{:S(2)}, u32[]{:S(2)}) async-start(bf16[16,256,32]{1,2,0:T(8,128)(2,1)} %param.14), calls=%async_computation | async-start | bytes 524288 | tf_op jit(solution)/shard_map/all_to_all | solution.py:125
  13.4 99.0 %all-gather.4.cloned.1.call-start = ((), (), s32[]{:S(2)}) async-start(), calls=%async_computation.1 | async-start | bytes 8650752 | tf_op jit(solution)/shard_map/all_gather | solution.py:15
  21.9 2.7 %copy-start.2 = (bf16[256,512]{0,1:T(8,128)(2,1)}, bf16[256,512]{0,1:T(8,128)(2,1)S(1)}, u32[]{:S(2)}) copy-start(bf16[256,512]{0,1:T(8,128)(2,1)S(1)} %fusion.21) | copy-start | bytes 786436
  22.0 3.8 %copy-start.5 = (f32[256,16]{0,1:T(8,128)}, f32[256,16]{0,1:T(8,128)S(1)}, u32[]{:S(2)}) copy-start(f32[256,16]{0,1:T(8,128)S(1)} %compare_select_fusion) | copy-start | bytes 49156
  23.1 2.8 %copy-start.7 = (f32[16,2,128]{2,1,0:T(2,128)}, f32[16,2,128]{2,1,0:T(2,128)S(1)}, u32[]{:S(2)}) copy-start(f32[16,2,128]{2,1,0:T(2,128)S(1)} %broadcast.144) | copy-start | bytes 49156
  23.7 2.2 %copy-start.10 = (f32[1,1,256,16]{2,3,1,0:T(8,128)}, f32[1,1,256,16]{2,3,1,0:T(8,128)S(1)}, u32[]{:S(2)}) copy-start(f32[1,1,256,16]{2,3,1,0:T(8,128)S(1)} %fusion.37) | copy-start | bytes 49156
  24.5 2.2 %copy-start.1 = (bf16[1,256,1280]{2,1,0:T(8,128)(2,1)}, bf16[1,256,1280]{2,1,0:T(8,128)(2,1)S(1)}, u32[]{:S(2)}) copy-start(bf16[1,256,1280]{2,1,0:T(8,128)(2,1)S(1)} %fusion) | copy-start | bytes 1966084
  24.6 4.6 %collective-permute-start = (bf16[1,3,1280]{2,1,0:T(4,128)(2,1)S(1)}, bf16[1,3,1280]{2,1,0:T(4,128)(2,1)S(1)}, u32[]{:S(2)}, u32[]{:S(2)}) collective-permute-start(bf16[1,3,1280]{2,1,0:T(4,128)(2,1)S(1)} %slice.65), channel_id=1, source_target_pairs={{0,16},{16,32},{32,48},{48,64},{64,80},{80,96},{96,112},{112,128},... | collective-permute-start | bytes 23048 | tf_op jit(solution)/shard_map/ppermute | solution.py:35
  27.1 3.3 %copy-start.12 = (f32[1280]{0:T(1024)S(1)}, f32[1280]{0:T(1024)}, u32[]{:S(2)}) copy-start(f32[1280]{0:T(1024)} %get-tuple-element.107) | copy-start | bytes 15364
  27.1 3.3 %copy-start.13 = (f32[1280]{0:T(1024)S(1)}, f32[1280]{0:T(1024)}, u32[]{:S(2)}) copy-start(f32[1280]{0:T(1024)} %get-tuple-element.108) | copy-start | bytes 15364
  27.1 3.3 %copy-start.14 = (f32[1280]{0:T(1024)S(1)}, f32[1280]{0:T(1024)}, u32[]{:S(2)}) copy-start(f32[1280]{0:T(1024)} %get-tuple-element.109) | copy-start | bytes 15364
  27.1 3.3 %copy-start.15 = (f32[1280]{0:T(1024)S(1)}, f32[1280]{0:T(1024)}, u32[]{:S(2)}) copy-start(f32[1280]{0:T(1024)} %get-tuple-element.110) | copy-start | bytes 15364
  27.1 3.3 %copy-start.17 = (f32[1280]{0:T(1024)S(1)}, f32[1280]{0:T(1024)}, u32[]{:S(2)}) copy-start(f32[1280]{0:T(1024)} %param.22) | copy-start | bytes 15364
  32.2 3.0 %copy-start.11 = (f32[1,1,256,16]{2,3,1,0:T(8,128)S(1)}, f32[1,1,256,16]{2,3,1,0:T(8,128)}, u32[]{:S(2)}) copy-start(f32[1,1,256,16]{2,3,1,0:T(8,128)} %copy-done.10) | copy-start | bytes 49156
  32.2 33.1 %copy-start.8 = (f32[16,2,128]{2,1,0:T(2,128)S(1)}, f32[16,2,128]{2,1,0:T(2,128)}, u32[]{:S(2)}) copy-start(f32[16,2,128]{2,1,0:T(2,128)} %copy-done.7) | copy-start | bytes 49156
  35.2 30.6 %copy-start.6 = (f32[256,16]{0,1:T(8,128)S(1)}, f32[256,16]{0,1:T(8,128)}, u32[]{:S(2)}) copy-start(f32[256,16]{0,1:T(8,128)} %copy-done.5) | copy-start | bytes 49156
  112.5 35.9 %copy-start.9 = (f32[256,16]{0,1:T(8,128)S(1)}, f32[256,16]{0,1:T(8,128)}, u32[]{:S(2)}) copy-start(f32[256,16]{0,1:T(8,128)} %get-tuple-element.123) | copy-start | bytes 49156
  150.0 1.3 copy-start.3
  151.3 2.4 %copy-start.4 = (bf16[1024,512]{1,0:T(8,128)(2,1)S(1)}, bf16[1024,512]{1,0:T(8,128)(2,1)}, u32[]{:S(2)}) copy-start(bf16[1024,512]{1,0:T(8,128)(2,1)} %param.25) | copy-start | bytes 3145732
  151.3 2.4 %copy-start.18 = (f32[1024]{0:T(1024)S(1)}, f32[1024]{0:T(1024)}, u32[]{:S(2)}) copy-start(f32[1024]{0:T(1024)} %param.24) | copy-start | bytes 12292
Sparse Core Ops, SparseCore 0:
  35.3 77.1 all-gather.3
where the time goes:
time: 163 us; the launch traced here: 162 us
  waiting for transfers between devices  51.4 us (32%)
  other arithmetic  41.5 us (25%)
  blocking collectives  29.8 us (18%)
  between operations  13.8 us (8%)
  matrix products  10.1 us (6%)
  starting transfers between devices  8.23 us (5%)
  local copies, waits for them, and re-layouts  5.74 us (4%)
    all_gather x1, waiting for transfers between devices, entering(): lax.all_gather(a.astype(kind), axis)  44.2 us
    add x31, other arithmetic, combine(): later[0][:, :, None, None] * earlier[1] + later[1]  34.4 us
    all_gather x1, blocking collectives, entering(): lax.all_gather(a.astype(kind), axis)  29.8 us
    all_to_all x1, starting transfers between devices, local(): lax.all_to_all(columns, 'table', split_axis=0, concat_axis=2, tiled=True)  6.89 us
    all_to_all x1, waiting for transfers between devices, local(): lax.all_to_all(columns, 'table', split_axis=0, concat_axis=2, tiled=True)  5.21 us
  transfers between devices with their start and end apart: 3, of which 3 were waited for; matrix products, arithmetic and copies ran while one was open for 4% of the time, Pallas kernels for 0%

commit v1 on v0

--- a/solution.py
+++ b/solution.py
@@ -7,26 +7,6 @@
 
 
 epsilon = 1e-05
-
-
-def entering(shard, axis, join, neutral):
-    place = lax.axis_index(axis)
-    gathered = jax.tree.map(
-        lambda a, kind: lax.all_gather(a.astype(kind), axis), shard, (jnp.bfloat16, jnp.bfloat16)
-    )
-    state = jax.tree.map(lambda a, e: jnp.zeros_like(a) + jnp.asarray(e, a.dtype), shard, neutral)
-
-    def one(step, state):
-        return join(
-            state,
-            jax.tree.map(
-                lambda a, own: lax.dynamic_index_in_dim(a, step, 0, False).astype(own.dtype),
-                gathered,
-                shard,
-            ),
-        )
-
-    return lax.fori_loop(0, place, one, state)
 
 
 def passed_along(block, axis, distance):
@@ -92,14 +72,74 @@
     return jnp.exp(cs)[..., None] * picked
 
 
-def carry_in(total_part, final_part):
-
-    def combine(earlier, later):
-        return (earlier[0] * later[0], later[0][:, :, None, None] * earlier[1] + later[1])
-
-    identity = (jnp.ones_like(total_part), jnp.zeros_like(final_part))
-    prefix = entering((jnp.exp(total_part), final_part), "seq", combine, identity)
-    return prefix[1]
+GROUP = 8
+
+
+def parts_of(values):
+    high = values.astype(jnp.bfloat16)
+    rest = values - high.astype(jnp.float32)
+    middle = rest.astype(jnp.bfloat16)
+    low = (rest - middle.astype(jnp.float32)).astype(jnp.bfloat16)
+    return jnp.stack([high, middle, low])
+
+
+def within_groups(blocks):
+    count = lax.axis_size("seq") // GROUP
+    groups = [[g * GROUP + i for i in range(GROUP)] for g in range(count)]
+    return lax.all_to_all(
+        blocks, "seq", split_axis=0, concat_axis=0, tiled=True, axis_index_groups=groups
+    )
+
+
+def with_decay(state, logs):
+    lead = state.shape[:-3]
+    heads, head_dim, width = state.shape[-3:]
+    rows = jnp.moveaxis(parts_of(logs), 0, -1).reshape(lead + (heads * 3, 1))
+    rows = jnp.broadcast_to(rows, lead + (heads * 3, width))
+    pad = [(0, 0)] * len(lead) + [(0, -(heads * 3) % 8), (0, 0)]
+    flat = state.astype(jnp.bfloat16).reshape(lead + (heads * head_dim, width))
+    return jnp.concatenate([flat, jnp.pad(rows, pad)], axis=-2)
+
+
+def without_decay(block, heads):
+    width = block.shape[-1]
+    lead = block.shape[:-2]
+    block = block.astype(jnp.float32)
+    size = block.shape[-2] - heads * 3 - (-(heads * 3) % 8)
+    state = block[..., :size, :].reshape(lead + (heads, size // heads, width))
+    logs = block[..., size : size + heads * 3, 0].reshape(lead + (heads, 3)).sum(-1)
+    return (state, logs)
+
+
+def carry_in(total, final):
+    heads, head_dim, width = final.shape
+    own = heads // GROUP
+    grouped = with_decay(
+        final.reshape(GROUP, own, head_dim, width), total.reshape(GROUP, own)
+    )
+    states, logs = without_decay(within_groups(grouped), own)
+    prefix = [jnp.zeros_like(states[0])]
+    before = [jnp.zeros_like(logs[0])]
+    for member in range(GROUP):
+        prefix.append(jnp.exp(logs[member])[:, None, None] * prefix[-1] + states[member])
+        before.append(before[-1] + logs[member])
+    block = with_decay(prefix[-1], before[-1])
+    count = lax.axis_size("seq") // GROUP
+    arrived = [
+        without_decay(passed_along(block, "seq", GROUP * step), own) for step in range(1, count)
+    ]
+    enter = arrived[-1][0]
+    for state, log in arrived[-2::-1]:
+        enter = state + jnp.exp(log)[:, None, None] * enter
+    back = jnp.stack(
+        [
+            prefix[member] + jnp.exp(before[member])[:, None, None] * enter
+            for member in range(GROUP)
+        ]
+    ).astype(jnp.bfloat16)
+    return within_groups(back.reshape(GROUP, own * head_dim, width)).reshape(
+        heads, head_dim, width
+    )
 
 
 def local(
@@ -148,7 +188,7 @@
     steps_dt = jax.nn.softplus(step_raw + step_bias)
     decay = -rates * steps_dt * gaps[:, :, None]
     y_in, cs, entries, starts, final, total = jax.vmap(local_pass)(xs, bm, cm, steps_dt, decay)
-    incoming = carry_in(total, final)
+    incoming = carry_in(total[0], final[0])[None].astype(jnp.float32)
     state_terms = jax.vmap(carried_output)(cm, cs, entries, starts, incoming)
     y = (y_in + state_terms).reshape(hists, length, inner)
     gated = y * jax.nn.silu(gate.astype(jnp.float32))

time: 163 us -> 96.2 us (0.59)
  the two profiles are of different devices: /device:TPU:481 before, /device:TPU:1 now
where the time goes in v1:
time: 96.2 us; the launch traced here: 95.5 us
  starting transfers between devices  32.7 us (34%)
  blocking collectives  16.6 us (17%)
  other arithmetic  13.6 us (14%)
  local copies, waits for them, and re-layouts  11.8 us (12%)
  waiting for transfers between devices  11 us (11%)
  matrix products  9.44 us (10%)
    ppermute x4, starting transfers between devices, passed_along(): return lax.ppermute(block, axis, route)  21 us
    all_to_all x1, blocking collectives, within_groups(): lax.all_to_all(blocks, 'seq', split_axis=0, concat_axis=0, tiled=True, ax...  16.6 us
    all_to_all x1, starting transfers between devices, local(): lax.all_to_all(columns, 'table', split_axis=0, concat_axis=2, tiled=True)  7.73 us
    all_to_all x1, waiting for transfers between devices, local(): lax.all_to_all(columns, 'table', split_axis=0, concat_axis=2, tiled=True)  5.79 us
    unnamed x7, other arithmetic  5.08 us
    all_to_all x1, starting transfers between devices, within_groups(): lax.all_to_all(blocks, 'seq', split_axis=0, concat_axis=0, tiled=True, ax...  3.98 us
    dot_general x1, matrix products, block_terms(): jnp.einsum('hts,shp->thp', mix, cx, preferred_element_type=jnp.float32)  3.2 us
    all_to_all x1, waiting for transfers between devices, within_groups(): lax.all_to_all(blocks, 'seq', split_axis=0, concat_axis=0, tiled=True, ax...  2.97 us
  transfers between devices with their start and end apart: 6, of which 3 were waited for; matrix products, arithmetic and copies ran while one was open for 13% of the time, Pallas kernels for 0%

profile of v1, /device:TPU:1, one launch (start us, length us, event | category | flops | bytes accessed | tf_op | source)
XLA Modules:
  0.0 95.5 jit_solution(16573989811518434025)
XLA Ops:
  0.0 7.7 %all-to-all-start = ((bf16[16,256,32]{1,2,0:T(8,128)(2,1)}), bf16[16,256,32]{1,2,0:T(8,128)(2,1)S(1)}, u32[]{:S(2)}, u32[]{:S(2)}) async-start(bf16[16,256,32]{1,2,0:T(8,128)(2,1)} %param.12), calls=%async_computation | async-start | bytes 524288 | tf_op jit(solution)/shard_map/all_to_all | solution.py:165
  7.8 0.7 neg.18
  8.4 0.9 slice_reduce_fusion.6
  9.4 5.8 %all-to-all-done = bf16[16,256,32]{1,2,0:T(8,128)(2,1)S(1)} async-done(((bf16[16,256,32]{1,2,0:T(8,128)(2,1)}), bf16[16,256,32]{1,2,0:T(8,128)(2,1)S(1)}, u32[]{:S(2)}, u32[]{:S(2)}) %all-to-all-start) | async-done | bytes 262176 | tf_op jit(solution)/shard_map/all_to_all | solution.py:165
  15.3 0.8 fusion.22
  16.1 0.2 compare_select_fusion
  16.4 0.6 reduce-window.6
  16.9 0.2 slice_reduce_fusion
  17.3 0.6 exponential_bitcast_fusion
  18.0 0.2 slice_reduce_fusion.1
  18.2 0.5 fusion
  18.8 5.5 %collective-permute-start = (bf16[1,3,1280]{2,1,0:T(4,128)(2,1)S(1)}, bf16[1,3,1280]{2,1,0:T(4,128)(2,1)S(1)}, u32[]{:S(2)}, u32[]{:S(2)}) collective-permute-start(bf16[1,3,1280]{2,1,0:T(4,128)(2,1)S(1)} %slice.182), channel_id=1, source_target_pairs={{0,16},{16,32},{32,48},{48,64},{64,80},{80,96},{96,112},{112,128},... | collective-permute-start | bytes 23048 | tf_op jit(solution)/shard_map/ppermute | solution.py:15
  24.3 0.2 exponential_reduce_fusion
  24.7 1.1 %mul.674 = f32[256,16,64]{0,2,1:T(8,128)} broadcast(f32[256,16]{0,1:T(8,128)S(1)} %fusion.60), dimensions={0,1} | broadcast | bytes 1064960 | tf_op jit(solution)/shard_map/vmap()/while/body/eval_jaxpr/mul | solution.py:33
  25.8 1.6 %copy.82 = f32[1,256,1024]{2,1,0:T(8,128)S(1)} copy(f32[1,256,1024]{1,2,0:T(8,128)} %bitcast.196) | data formatting | bytes 2097152 | tf_op jit(solution)/shard_map/vmap()/while/body/eval_jaxpr/mul | solution.py:33
  27.7 0.4 copy-done.4
  28.0 0.8 multiply_convert_fusion.4
  28.9 0.9 multiply_convert_fusion.6
  29.8 1.2 %copy.83 = bf16[1,256,1024]{1,2,0:T(8,128)(2,1)S(1)} copy(bf16[1,256,1024]{2,1,0:T(8,128)(2,1)} %multiply_convert_fusion.6) | data formatting | bytes 1048576 | tf_op jit(solution)/shard_map/vmap()/while/body/eval_jaxpr/convert_element_type | solution.py:33
  31.1 0.3 fusion.14
  31.5 16.6 %all_to_all.19 = bf16[8,136,128]{2,1,0:T(8,128)(2,1)S(1)} all-to-all(bf16[8,136,128]{2,1,0:T(8,128)(2,1)S(1)} %fusion.25), channel_id=1, replica_groups={{0,16,32,48,64,80,96,112},{128,144,160,176,192,208,224,240},{256,272,28..., dimensions={0} | all-to-all | bytes 557056 | tf_op jit(solution)/shard_map/all_to_all | solution.py:89
  48.4 0.4 exponential_reduce_fusion.1
  50.2 0.2 fusion.29
  50.5 8.8 %collective-permute-start.1 = (bf16[136,128]{1,0:T(8,128)(2,1)S(1)}, bf16[136,128]{1,0:T(8,128)(2,1)S(1)}, u32[]{:S(2)}, u32[]{:S(2)}) collective-permute-start(bf16[136,128]{1,0:T(8,128)(2,1)S(1)} %pad_maximum_fusion), channel_id=1, source_target_pairs={{0,128},{16,144},{32,160},{48,176},{64,192},{80,208},{96,224},{112... | collective-permute-start | bytes 104456 | tf_op jit(solution)/shard_map/ppermute | solution.py:15
  59.3 5.4 %collective-permute-start.2 = (bf16[136,128]{1,0:T(8,128)(2,1)S(1)}, bf16[136,128]{1,0:T(8,128)(2,1)S(1)}, u32[]{:S(2)}, u32[]{:S(2)}) collective-permute-start(bf16[136,128]{1,0:T(8,128)(2,1)S(1)} %pad_maximum_fusion), channel_id=1, source_target_pairs={{0,256},{16,272},{32,288},{48,304},{64,320},{80,336},{96,352},{112... | collective-permute-start | bytes 104456 | tf_op jit(solution)/shard_map/ppermute | solution.py:15
  64.7 1.3 %collective-permute-start.3 = (bf16[136,128]{1,0:T(8,128)(2,1)S(1)}, bf16[136,128]{1,0:T(8,128)(2,1)S(1)}, u32[]{:S(2)}, u32[]{:S(2)}) collective-permute-start(bf16[136,128]{1,0:T(8,128)(2,1)S(1)} %pad_maximum_fusion), channel_id=1, source_target_pairs={{0,384},{16,400},{32,416},{48,432},{64,448},{80,464},{96,480},{112... | collective-permute-start | bytes 104456 | tf_op jit(solution)/shard_map/ppermute | solution.py:15
  68.1 2.2 %collective-permute-done.3 = bf16[136,128]{1,0:T(8,128)(2,1)S(1)} collective-permute-done((bf16[136,128]{1,0:T(8,128)(2,1)S(1)}, bf16[136,128]{1,0:T(8,128)(2,1)S(1)}, u32[]{:S(2)}, u32[]{:S(2)}) %collective-permute-start.3) | collective-permute-done | bytes 34848 | tf_op jit(solution)/shard_map/ppermute | solution.py:15
  70.3 0.7 bitcast_dynamic-update-slice_fusion
  71.0 0.7 fusion.53
  71.7 0.7 fusion.54
  72.5 0.7 fusion.55
  73.2 0.7 fusion.56
  73.9 0.7 fusion.57
  74.7 0.7 fusion.58
  75.4 0.7 fusion.59
  76.1 4.0 %all-to-all-start.2 = ((bf16[8,128,128]{2,1,0:T(8,128)(2,1)}), bf16[8,128,128]{2,1,0:T(8,128)(2,1)S(1)}, u32[]{:S(2)}, u32[]{:S(2)}) async-start(bf16[8,128,128]{2,1,0:T(8,128)(2,1)} %fusion.59), calls=%async_computation.2 | async-start | bytes 524288 | tf_op jit(solution)/shard_map/all_to_all | solution.py:89
  80.1 0.6 iota_compare_fusion.1
  80.9 0.7 mul.667
  81.6 0.6 bitcast_add_fusion.14
  82.2 0.2 copy.77
  82.5 0.2 fusion.46
  82.7 3.2 %fusion.8 = f32[256,16,64]{0,2,1:T(8,128)} fusion(bf16[256,16,64]{0,2,1:T(8,128)(2,1)S(1)} %bitcast.200, f32[16,256]{1,0:T(8,128)S(1)} %bitcast.201, f32[16,256]{1,0:T(8,128)} %bitcast_add_fusion.14, f32[256,256]{1,0:T(8,128)S(1)} %fusion.46, pred[256,256]{1,0:T(8,128)(4,1)} %iota_compare_fusion.1), kind=kOutput, calls=%fused_computation.10 | convolution fusion | flops 139460608 | bytes 1933312 | tf_op jit(solution)/shard_map/vmap()/while/body/eval_jaxpr/hts,shp->thp/dot_general | solution.py:32
  85.9 3.0 %all-to-all-done.2 = bf16[8,128,128]{2,1,0:T(8,128)(2,1)S(1)} async-done(((bf16[8,128,128]{2,1,0:T(8,128)(2,1)}), bf16[8,128,128]{2,1,0:T(8,128)(2,1)S(1)}, u32[]{:S(2)}, u32[]{:S(2)}) %all-to-all-start.2) | async-done | bytes 262176 | tf_op jit(solution)/shard_map/all_to_all | solution.py:89
  88.8 0.2 multiply_convert_fusion.8
  89.0 1.5 %fusion.9 = f32[256,16,64]{0,2,1:T(8,128)S(1)} fusion(f32[256,16,64]{0,2,1:T(8,128)} %fusion.8, bf16[16,64,128]{2,1,0:T(8,128)(2,1)S(1)} %bitcast.198, f32[256,16]{0,1:T(8,128)} %get-tuple-element.68, bf16[1,256,1280]{2,1,0:T(8,128)(2,1)S(1)} %multiply_convert_fusion.4), kind=kOutput, calls=%fused_computation.12 | convolution fusion | flops 67633152 | bytes 2441216 | tf_op jit(solution)/shard_map/vmap(ktn,khpn->kthp)/dot_general | solution.py:71
  90.6 1.3 %copy.89 = f32[256,1024]{1,0:T(8,128)} copy(f32[256,1024]{0,1:T(8,128)S(1)} %bitcast.195) | data formatting | bytes 2097152 | tf_op jit(solution)/shard_map/reshape | solution.py:193
  91.9 2.3 %multiply_reduce_fusion = (f32[256]{0:T(256)S(1)}, f32[256,1024]{1,0:T(8,128)S(1)}) fusion(f32[256,1024]{1,0:T(8,128)} %copy.89, bf16[256,512]{0,1:T(8,128)(2,1)S(1)} %fusion.22, bf16[512,1024]{1,0:T(8,128)(2,1)} %param.15), kind=kOutput, calls=%fused_computation.35 | convolution fusion | flops 270794496 | bytes 3408896 | tf_op jit(solution)/shard_map/brd,de->bre/dot_general | solution.py:170
  94.3 1.2 %fusion.15 = bf16[1,256,512]{2,1,0:T(8,128)(2,1)} fusion(bf16[1024,512]{1,0:T(8,128)(2,1)S(1)} %copy-done.1, f32[256,1024]{1,0:T(8,128)S(1)} %get-tuple-element.88, f32[1024]{0:T(1024)S(1)} %copy-done.5, f32[256]{0:T(256)S(1)} %add_rsqrt_fusion), kind=kOutput, calls=%fused_computation.28 | convolution fusion | flops 269352960 | bytes 2364416 | tf_op jit(solution)/shard_map/bri,id->brd/dot_general | solution.py:196
  (98 shorter events, 5.2 us)
Async XLA Ops:
  0.0 18.2 %copy-start = (bf16[512,1280]{1,0:T(8,128)(2,1)S(1)}, bf16[512,1280]{1,0:T(8,128)(2,1)}, u32[]{:S(2)}) copy-start(bf16[512,1280]{1,0:T(8,128)(2,1)} %param.16) | copy-start | bytes 3932164
  0.0 16.1 %copy-start.3 = (bf16[512,16]{0,1:T(8,128)(2,1)S(1)}, bf16[512,16]{0,1:T(8,128)(2,1)}, u32[]{:S(2)}) copy-start(bf16[512,16]{0,1:T(8,128)(2,1)} %param.17) | copy-start | bytes 49156
  0.0 16.1 %copy-start.7 = (f32[16]{0:T(128)S(1)}, f32[16]{0:T(128)}, u32[]{:S(2)}) copy-start(f32[16]{0:T(128)} %param.18) | copy-start | bytes 196
  0.0 16.3 %copy-start.6 = (f32[1,256]{1,0:T(1,128)S(1)}, f32[1,256]{1,0:T(1,128)}, u32[]{:S(2)}) copy-start(f32[1,256]{1,0:T(1,128)} %param.13) | copy-start | bytes 3076
  0.0 15.1 %all-to-all-start = ((bf16[16,256,32]{1,2,0:T(8,128)(2,1)}), bf16[16,256,32]{1,2,0:T(8,128)(2,1)S(1)}, u32[]{:S(2)}, u32[]{:S(2)}) async-start(bf16[16,256,32]{1,2,0:T(8,128)(2,1)} %param.12), calls=%async_computation | async-start | bytes 524288 | tf_op jit(solution)/shard_map/all_to_all | solution.py:165
  18.8 8.8 %collective-permute-start = (bf16[1,3,1280]{2,1,0:T(4,128)(2,1)S(1)}, bf16[1,3,1280]{2,1,0:T(4,128)(2,1)S(1)}, u32[]{:S(2)}, u32[]{:S(2)}) collective-permute-start(bf16[1,3,1280]{2,1,0:T(4,128)(2,1)S(1)} %slice.182), channel_id=1, source_target_pairs={{0,16},{16,32},{32,48},{48,64},{64,80},{80,96},{96,112},{112,128},... | collective-permute-start | bytes 23048 | tf_op jit(solution)/shard_map/ppermute | solution.py:15
  27.3 0.7 copy-start.4
  50.5 16.6 %collective-permute-start.1 = (bf16[136,128]{1,0:T(8,128)(2,1)S(1)}, bf16[136,128]{1,0:T(8,128)(2,1)S(1)}, u32[]{:S(2)}, u32[]{:S(2)}) collective-permute-start(bf16[136,128]{1,0:T(8,128)(2,1)S(1)} %pad_maximum_fusion), channel_id=1, source_target_pairs={{0,128},{16,144},{32,160},{48,176},{64,192},{80,208},{96,224},{112... | collective-permute-start | bytes 104456 | tf_op jit(solution)/shard_map/ppermute | solution.py:15
  59.3 7.9 %collective-permute-start.2 = (bf16[136,128]{1,0:T(8,128)(2,1)S(1)}, bf16[136,128]{1,0:T(8,128)(2,1)S(1)}, u32[]{:S(2)}, u32[]{:S(2)}) collective-permute-start(bf16[136,128]{1,0:T(8,128)(2,1)S(1)} %pad_maximum_fusion), channel_id=1, source_target_pairs={{0,256},{16,272},{32,288},{48,304},{64,320},{80,336},{96,352},{112... | collective-permute-start | bytes 104456 | tf_op jit(solution)/shard_map/ppermute | solution.py:15
  64.7 5.6 %collective-permute-start.3 = (bf16[136,128]{1,0:T(8,128)(2,1)S(1)}, bf16[136,128]{1,0:T(8,128)(2,1)S(1)}, u32[]{:S(2)}, u32[]{:S(2)}) collective-permute-start(bf16[136,128]{1,0:T(8,128)(2,1)S(1)} %pad_maximum_fusion), channel_id=1, source_target_pairs={{0,384},{16,400},{32,416},{48,432},{64,448},{80,464},{96,480},{112... | collective-permute-start | bytes 104456 | tf_op jit(solution)/shard_map/ppermute | solution.py:15
  76.1 12.7 %all-to-all-start.2 = ((bf16[8,128,128]{2,1,0:T(8,128)(2,1)}), bf16[8,128,128]{2,1,0:T(8,128)(2,1)S(1)}, u32[]{:S(2)}, u32[]{:S(2)}) async-start(bf16[8,128,128]{2,1,0:T(8,128)(2,1)} %fusion.59), calls=%async_computation.2 | async-start | bytes 524288 | tf_op jit(solution)/shard_map/all_to_all | solution.py:89
  82.6 6.2 %copy-start.2 = (f32[8,128]{1,0:T(8,128)S(1)}, f32[8,128]{1,0:T(8,128)}, u32[]{:S(2)}) copy-start(f32[8,128]{1,0:T(8,128)} %mul.667) | copy-start | bytes 12292
  91.9 2.4 %copy-start.1 = (bf16[1024,512]{1,0:T(8,128)(2,1)S(1)}, bf16[1024,512]{1,0:T(8,128)(2,1)}, u32[]{:S(2)}) copy-start(bf16[1024,512]{1,0:T(8,128)(2,1)} %param.23) | copy-start | bytes 3145732
  91.9 2.4 %copy-start.5 = (f32[1024]{0:T(1024)S(1)}, f32[1024]{0:T(1024)}, u32[]{:S(2)}) copy-start(f32[1024]{0:T(1024)} %param.22) | copy-start | bytes 12292

commit v2 on v0

v2 whole, which is shorter than its diff:
```python
import functools

import jax
import jax.numpy as jnp
from jax import lax
from jax.experimental import pallas as pl
from jax.experimental.pallas import tpu as pltpu
from jax.sharding import PartitionSpec as P

GROUP = 8
EDGE = 128
EXTRA = 8
BIAS, GAIN_IN, GAIN_OUT = 4, 5, 6
epsilon = 1e-05
f32 = jnp.float32
bf16 = jnp.bfloat16


def passed_along(block, axis, distance):
    devices = range(lax.axis_size(axis))
    route = [(i - distance, i) for i in devices if i - distance in devices]
    return lax.ppermute(block, axis, route)


def within_groups(blocks):
    count = lax.axis_size("seq") // GROUP
    groups = [[g * GROUP + i for i in range(GROUP)] for g in range(count)]
    return lax.all_to_all(
        blocks, "seq", split_axis=0, concat_axis=0, tiled=True, axis_index_groups=groups
    )


def contract(a, b, dims):
    return lax.dot_general(a, b, (dims, ((), ())), preferred_element_type=f32)


def columns_of(vec_ref, at):
    return vec_ref[:, at : at + EDGE].T


def normed_columns(x_ref, vec_ref, out_ref):
    depth, length = x_ref.shape
    total = jnp.zeros((1, length), f32)
    for at in range(0, depth, 64):
        x = x_ref[at : at + 64, :].astype(f32)
        total = total + jnp.sum(x * x, axis=0, keepdims=True)
    scale = lax.rsqrt(total / depth + epsilon)
    for at in range(0, depth, EDGE):
        gain = columns_of(vec_ref, at)[:, GAIN_IN : GAIN_IN + 1]
        x = x_ref[at : at + EDGE, :].astype(f32)
        out_ref[at : at + EDGE, :] = (x * scale * gain).astype(bf16)


def running_sum(values):
    length = values.shape[1]
    lane = lax.broadcasted_iota(jnp.int32, values.shape, 1)
    reach = 1
    while reach < length:
        values = values + jnp.where(lane >= reach, pltpu.roll(values, reach, axis=1), 0.0)
        reach *= 2
    return values


def main_kernel(x_ref, vec_ref, w_xbc_ref, w_step_ref, head_ref, gaps_ref,
                normed_ref, act_ref, dt_ref, cs_ref, state_ref, logs_ref, first_ref, coef_first_ref,
                coef_ref, rows_ref):
    width = act_ref.shape[0]
    length = x_ref.shape[1]
    heads = dt_ref.shape[0]
    inner, state_width = state_ref.shape
    head_dim = inner // heads
    normed_columns(x_ref, vec_ref, normed_ref)
    first_ref[...] = x_ref[:, 0:EDGE].astype(f32).T[0:EXTRA, :]
    normed = normed_ref[...]
    raw = jnp.dot(w_step_ref[...], normed, preferred_element_type=f32)
    raw = raw + head_ref[:, 0:1]
    dt = jnp.maximum(raw, 0.0) + jnp.log1p(jnp.exp(-jnp.abs(raw)))
    dt_ref[...] = dt
    cs = running_sum(-head_ref[:, 1:2] * dt * gaps_ref[...])
    cs_ref[...] = cs
    coef = jnp.exp(cs[:, length - 1 : length] - cs) * dt
    coef_first = coef[:, 0:EDGE].T[0:EXTRA, :]
    for head in range(heads):
        coef_first_ref[:, head * head_dim : (head + 1) * head_dim] = jnp.broadcast_to(
            coef_first[:, head : head + 1], (EXTRA, head_dim)
        )
    lane = lax.broadcasted_iota(jnp.int32, coef.shape, 1)
    coef_ref[...] = jnp.where(lane >= EXTRA, coef, 0.0)
    total = jnp.broadcast_to(cs[:, length - 1 : length], (heads, state_width))
    pack_logs(total, rows_ref)
    logs_ref[...] = rows_ref[...].astype(bf16)

    def act_of(at, step):
        whole = (
            jnp.dot(w_xbc_ref[at : at + step, :], normed, preferred_element_type=f32)
            .astype(bf16)
            .astype(f32)
        )
        weights = columns_of(vec_ref, at)
        conv = weights[:, BIAS : BIAS + 1]
        for tap in range(BIAS):
            back = BIAS - 1 - tap
            moved = pltpu.roll(whole, back, axis=1) if back else whole
            conv = conv + weights[:, tap : tap + 1] * moved
        act = (conv * jax.nn.sigmoid(conv)).astype(bf16)
        act_ref[at : at + step, :] = act
        return act

    b = act_of(inner, state_width)
    act_of(inner + state_width, state_width)
    step = 2 * head_dim
    for at in range(0, inner, step):
        act = act_of(at, step).astype(f32)
        head = at // head_dim
        coef = jnp.concatenate(
            [jnp.broadcast_to(coef_ref[h : h + 1, :], (head_dim, length)) for h in (head, head + 1)],
            axis=0,
        )
        state_ref[at : at + step, :] = contract((act * coef).astype(bf16), b, ((1,), (1,)))


def edge_kernel(edge_ref, first_ref, vec_ref, w_xbc_ref, coef_ref, state_ref, logs_ref,
                send_ref, act_ref, rows_ref):
    inner, state_width = state_ref.shape
    depth = first_ref.shape[1]
    before = edge_ref[...].astype(f32).T[EDGE - EXTRA :, :]
    x = jnp.concatenate([before, first_ref[...]], axis=0)
    scale = lax.rsqrt(jnp.mean(x * x, axis=1, keepdims=True) + epsilon)
    normed = (x * scale * vec_ref[GAIN_IN : GAIN_IN + 1, :depth]).astype(bf16)
    rows_ref[...] = contract(normed, w_xbc_ref[...], ((1,), (1,))).astype(bf16).astype(f32)
    conv = vec_ref[BIAS : BIAS + 1, :]
    for tap in range(BIAS):
        at = EXTRA - (BIAS - 1 - tap)
        conv = conv + vec_ref[tap : tap + 1, :] * rows_ref[at : at + EXTRA, :]
    act = (conv * jax.nn.sigmoid(conv)).astype(bf16).astype(f32)
    act_ref[...] = act
    weighted = (act[:, :inner] * coef_ref[...]).astype(bf16).astype(f32)
    none = jnp.zeros_like(weighted)
    weighted = jnp.concatenate([weighted, none], axis=0).astype(bf16)
    b = act[:, inner : inner + state_width]
    b = jnp.concatenate([b, jnp.zeros_like(b)], axis=0).astype(bf16)
    size = inner // GROUP
    for part in range(GROUP):
        rows = slice(part * size, (part + 1) * size)
        late = contract(weighted[:, rows], b, ((0,), (0,)))
        send_ref[part, 0:size, :] = (state_ref[rows, :] + late).astype(bf16)
        send_ref[part, size : size + EXTRA, :] = logs_ref[part * EXTRA : (part + 1) * EXTRA, :]


def pack_logs(total, rows_ref):
    heads = total.shape[0]
    own = rows_ref.shape[0] // EXTRA
    own = heads // own
    rows_ref[...] = jnp.zeros_like(rows_ref)
    rest = total
    for piece in range(3):
        part = rest.astype(bf16).astype(f32)
        rest = rest - part
        for head in range(heads):
            at = head // own * EXTRA + head % own * 3 + piece
            rows_ref[at : at + 1, :] = part[head : head + 1, :]


def read_logs(rows, own):
    rows = rows.astype(f32)
    return [
        rows[3 * h : 3 * h + 1, :] + rows[3 * h + 1 : 3 * h + 2, :] + rows[3 * h + 2 : 3 * h + 3, :]
        for h in range(own)
    ]


def prefix_kernel(own, states_ref, send_ref, rows_ref):
    size = send_ref.shape[0] - EXTRA
    head_dim = size // own
    width = send_ref.shape[1]
    logs = [read_logs(states_ref[m, size : size + EXTRA, :], own) for m in range(GROUP)]
    for h in range(own):
        rows = slice(h * head_dim, (h + 1) * head_dim)
        state = jnp.zeros((head_dim, width), f32)
        for m in range(GROUP):
            state = jnp.exp(logs[m][h]) * state + states_ref[m, rows, :].astype(f32)
        send_ref[rows, :] = state.astype(bf16)
    total = [sum(logs[m][h] for m in range(GROUP)) for h in range(own)]
    pack_logs(jnp.concatenate(total, axis=0), rows_ref)
    send_ref[size : size + EXTRA, :] = rows_ref[...].astype(bf16)


def combine_kernel(own, states_ref, *refs):
    arrived, back_ref = refs[:-1], refs[-1]
    size = back_ref.shape[1]
    head_dim = size // own
    width = back_ref.shape[2]
    logs = [read_logs(states_ref[m, size : size + EXTRA, :], own) for m in range(GROUP)]
    jumps = [read_logs(ref[size : size + EXTRA, :], own) for ref in arrived]
    for h in range(own):
        rows = slice(h * head_dim, (h + 1) * head_dim)
        state = jnp.zeros((head_dim, width), f32)
        for ref, jump in zip(arrived[::-1], jumps[::-1]):
            state = jnp.exp(jump[h]) * state + ref[rows, :].astype(f32)
        for m in range(GROUP):
            back_ref[m, rows, :] = state.astype(bf16)
            state = jnp.exp(logs[m][h]) * state + states_ref[m, rows, :].astype(f32)


def inside_kernel(normed_ref, w_gate_ref, main_ref, first_ref, dt_ref, cs_ref,
                  gate_ref, y_ref, query_ref, act_ref, scores_ref, mix_ref, weight_ref, sem):
    fetch = pltpu.make_async_copy(w_gate_ref, weight_ref, sem)
    fetch.start()
    heads, length = dt_ref.shape
    inner = gate_ref.shape[0]
    lane = lax.broadcasted_iota(jnp.int32, (EDGE, EDGE), 1)
    rest = jnp.zeros((EDGE - EXTRA, EDGE), f32)
    for at in range(0, act_ref.shape[0], EDGE):
        rows = slice(at, at + EDGE)
        first = jnp.concatenate([first_ref[:, rows], rest], axis=0).T
        kept = main_ref[rows, 0:EDGE].astype(f32)
        act_ref[rows, 0:EDGE] = jnp.where(lane < EXTRA, first, kept).astype(bf16)
        act_ref[rows, EDGE:] = main_ref[rows, EDGE:]
    head_dim = inner // heads
    state_width = (act_ref.shape[0] - inner) // 2
    query_ref[...] = act_ref[inner + state_width :, :]
    scores_ref[...] = contract(
        act_ref[inner : inner + state_width, :], act_ref[inner + state_width :, :], ((0,), (0,))
    )
    cs_col = cs_ref[...].T
    dt_col = dt_ref[...].T
    half = length // 2
    mix_ref[...] = jnp.zeros_like(mix_ref)
    later = lax.broadcasted_iota(jnp.int32, (half, half), 1)
    early = lax.broadcasted_iota(jnp.int32, (half, half), 0)
    keep = later >= early
    for h in range(heads):
        for s in (0, half):
            cs_s = jnp.broadcast_to(cs_col[s : s + half, h : h + 1], (half, half))
            dt_s = jnp.broadcast_to(dt_col[s : s + half, h : h + 1], (half, half))
            for t in range(s, length, half):
                diff = cs_ref[h : h + 1, t : t + half] - cs_s
                if s == t:
                    diff = jnp.where(keep, diff, -jnp.inf)
                mix_ref[s : s + half, t : t + half] = (
                    scores_ref[s : s + half, t : t + half] * jnp.exp(diff) * dt_s
                ).astype(bf16)
        rows = slice(h * head_dim, (h + 1) * head_dim)
        y_ref[rows, :] = jnp.dot(act_ref[rows, :], mix_ref[...], preferred_element_type=f32)
    fetch.wait()
    normed = normed_ref[...]
    for at in range(0, inner, 256):
        gate = contract(weight_ref[:, at : at + 256], normed, ((0,), (0,)))
        gate = gate.astype(bf16).astype(f32)
        gate_ref[at : at + 256, :] = gate * jax.nn.sigmoid(gate)


def output_kernel(carried_ref, query_ref, cs_ref, y_ref, gate_ref, vec_ref, w_out_ref,
                  out_ref, gated_ref, normed_ref, weight_ref, sem):
    fetch = pltpu.make_async_copy(w_out_ref, weight_ref, sem)
    fetch.start()
    heads, length = cs_ref.shape
    inner = y_ref.shape[0]
    head_dim = inner // heads
    queries = query_ref[...]
    grown = jnp.exp(cs_ref[...])
    total = jnp.zeros((1, length), f32)
    step = 2 * head_dim
    for at in range(0, inner, step):
        picked = jnp.dot(carried_ref[at : at + step, :], queries, preferred_element_type=f32)
        for h in range(at // head_dim, (at + step) // head_dim):
            rows = slice(h * head_dim, (h + 1) * head_dim)
            own = picked[h * head_dim - at : (h + 1) * head_dim - at, :]
            y = y_ref[rows, :] + grown[h : h + 1, :] * own
            gated = y * gate_ref[rows, :]
            gated_ref[rows, :] = gated
            total = total + jnp.sum(gated * gated, axis=0, keepdims=True)
    scale = lax.rsqrt(total / inner + epsilon)
    for at in range(0, inner, EDGE):
        gain = columns_of(vec_ref, at)[:, GAIN_OUT : GAIN_OUT + 1]
        normed_ref[at : at + EDGE, :] = (gated_ref[at : at + EDGE, :] * scale * gain).astype(bf16)
    fetch.wait()
    out_ref[...] = contract(normed_ref[...], weight_ref[...], ((0,), (0,))).astype(bf16)


def call(kernel, outs, scratch, *args, fetched=()):
    vmem = pl.BlockSpec(memory_space=pltpu.VMEM)
    left = pl.BlockSpec(memory_space=pl.ANY)
    single = not isinstance(outs, list)
    return pl.pallas_call(
        kernel,
        out_shape=outs,
        in_specs=[left if at in fetched else vmem for at in range(len(args))],
        out_specs=vmem if single else [vmem] * len(outs),
        scratch_shapes=scratch,
        compiler_params=pltpu.CompilerParams(vmem_limit_bytes=12 << 20),
    )(*args)


def local(
    columns,
    gaps,
    norm_in,
    w_gate,
    w_xbc,
    w_step,
    step_bias,
    conv_weight,
    conv_bias,
    rates,
    norm_out,
    w_out,
):
    length = columns.shape[1]
    depth, inner = w_gate.shape
    heads = w_step.shape[1]
    width = w_xbc.shape[1]
    state_width = (width - inner) // 2
    own = heads // GROUP
    size = inner // GROUP
    shape = jax.ShapeDtypeStruct

    rows = [conv_weight, conv_bias[None], norm_in[None], norm_out[None]]
    vec = jnp.concatenate([jnp.pad(r, ((0, 0), (0, width - r.shape[1]))) for r in rows])
    vec = jnp.pad(vec, ((0, 8 - vec.shape[0]), (0, 0)))
    head = jnp.stack([step_bias, rates], axis=1)

    whole = lax.all_to_all(columns, "table", split_axis=0, concat_axis=2, tiled=True)
    whole, w_xbc_t, vec, head = lax.optimization_barrier((whole, w_xbc.T, vec, head))
    x = whole.reshape(length, depth).T
    edge = passed_along(x[:, length - EDGE :], "seq", 1)
    normed, act, dt, cs, state, logs, first, coef_first = call(
        main_kernel,
        [
            shape((depth, length), bf16),
            shape((width, length), bf16),
            shape((heads, length), f32),
            shape((heads, length), f32),
            shape((inner, state_width), f32),
            shape((GROUP * EXTRA, state_width), bf16),
            shape((EXTRA, depth), f32),
            shape((EXTRA, inner), f32),
        ],
        [pltpu.VMEM((heads, length), f32), pltpu.VMEM((GROUP * EXTRA, state_width), f32)],
        x, vec, w_xbc_t, w_step.T, head, gaps,
    )
    send, act_first = call(
        edge_kernel,
        [shape((GROUP, size + EXTRA, state_width), bf16), shape((EXTRA, width), f32)],
        [pltpu.VMEM((2 * EXTRA, width), f32)],
        edge, first, vec, w_xbc_t, coef_first, state, logs,
    )
    states = within_groups(send)
    total = call(
        functools.partial(prefix_kernel, own),
        shape((size + EXTRA, state_width), bf16),
        [pltpu.VMEM((EXTRA, state_width), f32)],
        states,
    )
    count = lax.axis_size("seq") // GROUP
    arrived = [passed_along(total, "seq", GROUP * step) for step in range(1, count)]
    gate, y, query = call(
        inside_kernel,
        [
            shape((inner, length), f32),
            shape((inner, length), f32),
            shape((state_width, length), bf16),
        ],
        [
            pltpu.VMEM((width, length), bf16),
            pltpu.VMEM((length, length), f32),
            pltpu.VMEM((length, length), bf16),
            pltpu.VMEM((depth, inner), bf16),
            pltpu.SemaphoreType.DMA,
        ],
        normed, w_gate, act, act_first, dt, cs,
        fetched=(1,),
    )
    gate, y, *arrived = lax.optimization_barrier((gate, y, *arrived))
    back = call(
        functools.partial(combine_kernel, own),
        shape((GROUP, size, state_width), bf16),
        [],
        states, *arrived,
    )
    carried = within_groups(back).reshape(inner, state_width)
    out = call(
        output_kernel,
        shape((length, w_out.shape[1]), bf16),
        [
            pltpu.VMEM((inner, length), f32),
            pltpu.VMEM((inner, length), bf16),
            pltpu.VMEM(w_out.shape, bf16),
            pltpu.SemaphoreType.DMA,
        ],
        carried, query, cs, y, gate, vec, w_out,
        fetched=(6,),
    )
    return out[None]


def solution(mesh):
    in_specs = (
        P(None, "seq", "table"),
        P("table", "seq"),
        P(),
        P(),
        P(),
        P(),
        P(),
        P(),
        P(),
        P(),
        P(),
        P(),
    )
    out_specs = P("table", "seq", None)
    return jax.shard_map(local, mesh=mesh, in_specs=in_specs, out_specs=out_specs, check_vma=False)
```

time: 163 us -> 76.7 us (0.47)
  the two profiles are of different devices: /device:TPU:481 before, /device:TPU:1 now
where the time goes in v2:
time: 76.7 us; the launch traced here: 76.3 us
  starting transfers between devices  29 us (38%)
  blocking collectives  28.4 us (37%)
  Pallas kernels  9.56 us (12%)
  waiting for transfers between devices  7.2 us (9%)
  local copies, waits for them, and re-layouts  1.8 us (2%)
    all_to_all x2, blocking collectives, within_groups(): lax.all_to_all(blocks, 'seq', split_axis=0, concat_axis=0, tiled=True, ax...  28.4 us
    ppermute x4, starting transfers between devices, passed_along(): return lax.ppermute(block, axis, route)  21.5 us
    pallas_call x6, Pallas kernels, call(): pl.pallas_call(kernel, out_shape=outs, in_specs=[left if at in fetched el...  9.56 us
    all_to_all x1, starting transfers between devices, local(): lax.all_to_all(columns, 'table', split_axis=0, concat_axis=2, tiled=True)  7.58 us
    all_to_all x1, waiting for transfers between devices, local(): lax.all_to_all(columns, 'table', split_axis=0, concat_axis=2, tiled=True)  5.53 us
    unnamed x21, local copies, waits for them, and re-layouts  1.7 us
    ppermute x4, waiting for transfers between devices, passed_along(): return lax.ppermute(block, axis, route)  1.68 us
  transfers between devices with their start and end apart: 5, of which 2 were waited for; matrix products, arithmetic and copies ran while one was open for 2% of the time, Pallas kernels for 9%

profile of v2, /device:TPU:1, one launch (start us, length us, event | category | flops | bytes accessed | tf_op | source)
XLA Modules:
  0.0 76.3 jit_solution(4519829655609222984)
XLA Ops:
  0.0 7.6 %all-to-all-start = ((bf16[16,256,32]{1,2,0:T(8,128)(2,1)}), bf16[16,256,32]{1,2,0:T(8,128)(2,1)S(1)}, u32[]{:S(2)}, u32[]{:S(2)}) async-start(bf16[16,256,32]{1,2,0:T(8,128)(2,1)} %param.12), calls=%async_computation | async-start | bytes 524288 | tf_op jit(solution)/shard_map/all_to_all | solution.py:323
  7.6 0.0 copy-start.5
  7.6 0.0 copy-start.4
  7.6 0.0 copy-start.6
  7.6 0.0 copy-start.7
  7.6 0.0 copy-start.8
  7.7 0.0 copy-start.9
  7.7 0.0 copy-start.2
  7.7 0.0 copy-start.3
  7.7 1.6 %copy.16 = bf16[512,1280]{0,1:T(8,128)(2,1)S(1)} copy(bf16[512,1280]{1,0:T(8,128)(2,1)} %param.16) | data formatting | bytes 2621440 | tf_op args[4]
  9.3 0.0 copy-done.5
  9.4 0.0 copy-done.4
  9.4 0.0 copy-done.6
  9.4 0.0 copy-done.7
  9.4 0.0 copy-done.8
  9.4 0.0 copy-done.9
  9.5 5.5 %all-to-all-done = bf16[16,256,32]{1,2,0:T(8,128)(2,1)S(1)} async-done(((bf16[16,256,32]{1,2,0:T(8,128)(2,1)}), bf16[16,256,32]{1,2,0:T(8,128)(2,1)S(1)}, u32[]{:S(2)}, u32[]{:S(2)}) %all-to-all-start) | async-done | bytes 262176 | tf_op jit(solution)/shard_map/all_to_all | solution.py:323
  15.0 5.5 %collective-permute-start = (bf16[512,128]{1,0:T(8,128)(2,1)S(1)}, bf16[512,128]{1,0:T(8,128)(2,1)S(1)}, u32[]{:S(2)}, u32[]{:S(2)}) collective-permute-start(bf16[512,128]{1,0:T(8,128)(2,1)S(1)} %slice.4), channel_id=1, source_target_pairs={{0,16},{16,32},{32,48},{48,64},{64,80},{80,96},{96,112},{112,128},... | collective-permute-start | bytes 393224 | tf_op jit(solution)/shard_map/ppermute | solution.py:22
  20.5 0.1 copy.17.head_ref
  20.6 0.0 copy-done.2
  20.6 0.0 copy-done.3
  20.6 4.1 %shard_map.118 = (bf16[512,256]{1,0:T(8,128)(2,1)S(1)}, bf16[1280,256]{1,0:T(8,128)(2,1)S(1)}, f32[16,256]{1,0:T(8,128)S(1)}, f32[16,256]{1,0:T(8,128)S(1)}, f32...) custom-call(bf16[512,256]{1,0:T(8,128)(2,1)S(1)} %bitcast.19, ...), custom_call_target="tpu_custom_call" | custom-call | tf_op jit(solution)/shard_map/pallas_call | solution.py:285
  24.7 0.0 collective-permute-done.edge_ref
  24.7 0.0 copy-start
  24.7 0.9 %shard_map.119 = (bf16[8,136,128]{2,1,0:T(8,128)(2,1)S(1)}, f32[8,1280]{1,0:T(8,128)S(1)}) custom-call(bf16[512,128]{1,0:T(8,128)(2,1)S(1)} %collective-permute-done.edge_ref, f32[8,512]{1,0:T(8,128)S(1)} %get-tuple-element.31.first_ref, f32[8,1280]{1,0:T(8,128)S(1)} %pad.14.vec_ref, bf16[1280,512]{1,0:T(8,128)(2,1)S(1)} %bitcast.17, ...), custom_call_target="tpu_custom_call" | custom-call | tf_op jit(solution)/shard_map/pallas_call | solution.py:285
  25.7 16.6 %all_to_all.28.states_ref = bf16[8,136,128]{2,1,0:T(8,128)(2,1)S(1)} all-to-all(bf16[8,136,128]{2,1,0:T(8,128)(2,1)S(1)} %get-tuple-element.35), channel_id=1, replica_groups={{0,16,32,48,64,80,96,112},{128,144,160,176,192,208,224,240},{256,272,28..., dimensions={0} | all-to-all | bytes 557056 | tf_op jit(solution)/shard_map/all_to_all | solution.py:28
  42.3 0.1 shard_map.121
  42.4 8.8 %collective-permute-start.1 = (bf16[136,128]{1,0:T(8,128)(2,1)S(1)}, bf16[136,128]{1,0:T(8,128)(2,1)S(1)}, u32[]{:S(2)}, u32[]{:S(2)}) collective-permute-start(bf16[136,128]{1,0:T(8,128)(2,1)S(1)} %shard_map.121), channel_id=1, source_target_pairs={{0,128},{16,144},{32,160},{48,176},{64,192},{80,208},{96,224},{112... | collective-permute-start | bytes 104456 | tf_op jit(solution)/shard_map/ppermute | solution.py:22
  51.2 5.9 %collective-permute-start.2 = (bf16[136,128]{1,0:T(8,128)(2,1)S(1)}, bf16[136,128]{1,0:T(8,128)(2,1)S(1)}, u32[]{:S(2)}, u32[]{:S(2)}) collective-permute-start(bf16[136,128]{1,0:T(8,128)(2,1)S(1)} %shard_map.121), channel_id=1, source_target_pairs={{0,256},{16,272},{32,288},{48,304},{64,320},{80,336},{96,352},{112... | collective-permute-start | bytes 104456 | tf_op jit(solution)/shard_map/ppermute | solution.py:22
  57.1 1.3 %collective-permute-start.3 = (bf16[136,128]{1,0:T(8,128)(2,1)S(1)}, bf16[136,128]{1,0:T(8,128)(2,1)S(1)}, u32[]{:S(2)}, u32[]{:S(2)}) collective-permute-start(bf16[136,128]{1,0:T(8,128)(2,1)S(1)} %shard_map.121), channel_id=1, source_target_pairs={{0,384},{16,400},{32,416},{48,432},{64,448},{80,464},{96,480},{112... | collective-permute-start | bytes 104456 | tf_op jit(solution)/shard_map/ppermute | solution.py:22
  58.4 0.0 copy-done
  58.4 0.0 copy-start.1
  58.4 2.6 %shard_map.120 = (f32[1024,256]{1,0:T(8,128)S(1)}, f32[1024,256]{1,0:T(8,128)S(1)}, bf16[128,256]{1,0:T(8,128)(2,1)S(1)}) custom-call(bf16[512,256]{1,0:T(8,128)(2,1)S(1)} %get-tuple-element.36.normed_ref, bf16[512,1024]{1,0:T(8,128)(2,1)S(1)} %copy-done, bf16[1280,256]{1,0:T(8,128)(2,1)S(1)} %get-tuple-element.37.main_ref, ...), custom_call_target="tpu_custom_call" | custom-call | tf_op jit(solution)/shard_map/pallas_call | solution.py:285
  61.0 0.0 collective-permute-done.1.refs_0_
  61.0 0.0 collective-permute-done.2.refs_1_
  61.0 1.7 %collective-permute-done.3.refs_2_ = bf16[136,128]{1,0:T(8,128)(2,1)S(1)} collective-permute-done((bf16[136,128]{1,0:T(8,128)(2,1)S(1)}, bf16[136,128]{1,0:T(8,128)(2,1)S(1)}, u32[]{:S(2)}, u32[]{:S(2)}) %collective-permute-start.3) | collective-permute-done | bytes 34848 | tf_op jit(solution)/shard_map/ppermute | solution.py:22
  62.6 0.1 shard_map.122
  62.7 11.8 %all_to_all.29 = bf16[8,128,128]{2,1,0:T(8,128)(2,1)S(1)} all-to-all(bf16[8,128,128]{2,1,0:T(8,128)(2,1)S(1)} %shard_map.122), channel_id=1, replica_groups={{0,16,32,48,64,80,96,112},{128,144,160,176,192,208,224,240},{256,272,28..., dimensions={0} | all-to-all | bytes 524288 | tf_op jit(solution)/shard_map/all_to_all | solution.py:28
  74.5 0.0 copy-done.1
  74.5 1.8 %shard_map.123 = bf16[256,512]{1,0:T(8,128)(2,1)} custom-call(bf16[1024,128]{1,0:T(8,128)(2,1)S(1)} %bitcast.20, bf16[128,256]{1,0:T(8,128)(2,1)S(1)} %get-tuple-element.46.query_ref, f32[16,256]{1,0:T(8,128)S(1)} %get-tuple-element.40.cs_ref, f32[1024,256]{1,0:T(8,128)S(1)} %get-tuple-element.47.y_ref, f32[1024,256]{1,0:T(8,128)S(1)} %get-tuple-element.48.gate_ref, ...), custom_call_target="tpu_custom_call" | custom-call | tf_op jit(solution)/shard_map/pallas_call | solution.py:285
  (5 shorter events, 0.1 us)
Async XLA Ops:
  0.0 15.0 %all-to-all-start = ((bf16[16,256,32]{1,2,0:T(8,128)(2,1)}), bf16[16,256,32]{1,2,0:T(8,128)(2,1)S(1)}, u32[]{:S(2)}, u32[]{:S(2)}) async-start(bf16[16,256,32]{1,2,0:T(8,128)(2,1)} %param.12), calls=%async_computation | async-start | bytes 524288 | tf_op jit(solution)/shard_map/all_to_all | solution.py:323
  7.6 1.7 %copy-start.5 = (f32[1280]{0:T(1024)S(1)}, f32[1280]{0:T(1024)}, u32[]{:S(2)}) copy-start(f32[1280]{0:T(1024)} %param.20) | copy-start | bytes 15364
  7.6 1.8 %copy-start.4 = (f32[4,1280]{1,0:T(4,128)S(1)}, f32[4,1280]{1,0:T(4,128)}, u32[]{:S(2)}) copy-start(f32[4,1280]{1,0:T(4,128)} %param.19) | copy-start | bytes 61444
  7.6 1.8 %copy-start.6 = (f32[1024]{0:T(1024)S(1)}, f32[1024]{0:T(1024)}, u32[]{:S(2)}) copy-start(f32[1024]{0:T(1024)} %param.22) | copy-start | bytes 12292
  7.6 1.7 %copy-start.7 = (f32[512]{0:T(512)S(1)}, f32[512]{0:T(512)}, u32[]{:S(2)}) copy-start(f32[512]{0:T(512)} %param.14) | copy-start | bytes 6148
  7.6 1.8 %copy-start.8 = (f32[16]{0:T(128)S(1)}, f32[16]{0:T(128)}, u32[]{:S(2)}) copy-start(f32[16]{0:T(128)} %param.21) | copy-start | bytes 196
  7.7 1.8 %copy-start.9 = (f32[16]{0:T(128)S(1)}, f32[16]{0:T(128)}, u32[]{:S(2)}) copy-start(f32[16]{0:T(128)} %param.18) | copy-start | bytes 196
  7.7 12.9 %copy-start.2 = (bf16[512,16]{0,1:T(8,128)(2,1)S(1)}, bf16[512,16]{0,1:T(8,128)(2,1)}, u32[]{:S(2)}) copy-start(bf16[512,16]{0,1:T(8,128)(2,1)} %param.17) | copy-start | bytes 49156
  7.7 12.9 %copy-start.3 = (f32[1,256]{1,0:T(1,128)S(1)}, f32[1,256]{1,0:T(1,128)}, u32[]{:S(2)}) copy-start(f32[1,256]{1,0:T(1,128)} %gaps_ref.1) | copy-start | bytes 3076
  15.0 9.7 %collective-permute-start = (bf16[512,128]{1,0:T(8,128)(2,1)S(1)}, bf16[512,128]{1,0:T(8,128)(2,1)S(1)}, u32[]{:S(2)}, u32[]{:S(2)}) collective-permute-start(bf16[512,128]{1,0:T(8,128)(2,1)S(1)} %slice.4), channel_id=1, source_target_pairs={{0,16},{16,32},{32,48},{48,64},{64,80},{80,96},{96,112},{112,128},... | collective-permute-start | bytes 393224 | tf_op jit(solution)/shard_map/ppermute | solution.py:22
  24.7 33.7 %copy-start = (bf16[512,1024]{1,0:T(8,128)(2,1)S(1)}, bf16[512,1024]{1,0:T(8,128)(2,1)}, u32[]{:S(2)}) copy-start(bf16[512,1024]{1,0:T(8,128)(2,1)} %w_gate_ref.1) | copy-start | bytes 3145732
  42.4 18.6 %collective-permute-start.1 = (bf16[136,128]{1,0:T(8,128)(2,1)S(1)}, bf16[136,128]{1,0:T(8,128)(2,1)S(1)}, u32[]{:S(2)}, u32[]{:S(2)}) collective-permute-start(bf16[136,128]{1,0:T(8,128)(2,1)S(1)} %shard_map.121), channel_id=1, source_target_pairs={{0,128},{16,144},{32,160},{48,176},{64,192},{80,208},{96,224},{112... | collective-permute-start | bytes 104456 | tf_op jit(solution)/shard_map/ppermute | solution.py:22
  51.2 9.8 %collective-permute-start.2 = (bf16[136,128]{1,0:T(8,128)(2,1)S(1)}, bf16[136,128]{1,0:T(8,128)(2,1)S(1)}, u32[]{:S(2)}, u32[]{:S(2)}) collective-permute-start(bf16[136,128]{1,0:T(8,128)(2,1)S(1)} %shard_map.121), channel_id=1, source_target_pairs={{0,256},{16,272},{32,288},{48,304},{64,320},{80,336},{96,352},{112... | collective-permute-start | bytes 104456 | tf_op jit(solution)/shard_map/ppermute | solution.py:22
  57.1 5.6 %collective-permute-start.3 = (bf16[136,128]{1,0:T(8,128)(2,1)S(1)}, bf16[136,128]{1,0:T(8,128)(2,1)S(1)}, u32[]{:S(2)}, u32[]{:S(2)}) collective-permute-start(bf16[136,128]{1,0:T(8,128)(2,1)S(1)} %shard_map.121), channel_id=1, source_target_pairs={{0,384},{16,400},{32,416},{48,432},{64,448},{80,464},{96,480},{112... | collective-permute-start | bytes 104456 | tf_op jit(solution)/shard_map/ppermute | solution.py:22
  58.4 16.1 %copy-start.1 = (bf16[1024,512]{1,0:T(8,128)(2,1)S(1)}, bf16[1024,512]{1,0:T(8,128)(2,1)}, u32[]{:S(2)}) copy-start(bf16[1024,512]{1,0:T(8,128)(2,1)} %w_out_ref.1) | copy-start | bytes 3145732

commit v3 on v2

--- a/solution.py
+++ b/solution.py
@@ -63,9 +63,8 @@
 
 def main_kernel(x_ref, vec_ref, w_xbc_ref, w_step_ref, head_ref, gaps_ref,
                 normed_ref, act_ref, dt_ref, cs_ref, state_ref, logs_ref, first_ref, coef_first_ref,
-                coef_ref, rows_ref):
-    width = act_ref.shape[0]
-    length = x_ref.shape[1]
+                coef_ref, rows_ref, upright_ref, shift_ref):
+    depth, length = x_ref.shape
     heads = dt_ref.shape[0]
     inner, state_width = state_ref.shape
     head_dim = inner // heads
@@ -90,19 +89,20 @@
     pack_logs(total, rows_ref)
     logs_ref[...] = rows_ref[...].astype(bf16)
 
+    for at in range(0, depth, EDGE):
+        upright_ref[:, at : at + EDGE] = normed_ref[at : at + EDGE, :].astype(f32).T.astype(bf16)
+    shift_ref[0:EXTRA, :] = jnp.zeros((EXTRA, shift_ref.shape[1]), f32)
+    upright = upright_ref[...]
+
     def act_of(at, step):
-        whole = (
-            jnp.dot(w_xbc_ref[at : at + step, :], normed, preferred_element_type=f32)
-            .astype(bf16)
-            .astype(f32)
-        )
-        weights = columns_of(vec_ref, at)
-        conv = weights[:, BIAS : BIAS + 1]
+        cols = slice(at, at + step)
+        whole = jnp.dot(upright, w_xbc_ref[:, cols], preferred_element_type=f32)
+        shift_ref[EXTRA:, cols] = whole.astype(bf16).astype(f32)
+        conv = vec_ref[BIAS : BIAS + 1, cols]
         for tap in range(BIAS):
-            back = BIAS - 1 - tap
-            moved = pltpu.roll(whole, back, axis=1) if back else whole
-            conv = conv + weights[:, tap : tap + 1] * moved
-        act = (conv * jax.nn.sigmoid(conv)).astype(bf16)
+            first = EXTRA - (BIAS - 1 - tap)
+            conv = conv + vec_ref[tap : tap + 1, cols] * shift_ref[first : first + length, cols]
+        act = (conv * jax.nn.sigmoid(conv)).T.astype(bf16)
         act_ref[at : at + step, :] = act
         return act
 
@@ -127,7 +127,8 @@
     x = jnp.concatenate([before, first_ref[...]], axis=0)
     scale = lax.rsqrt(jnp.mean(x * x, axis=1, keepdims=True) + epsilon)
     normed = (x * scale * vec_ref[GAIN_IN : GAIN_IN + 1, :depth]).astype(bf16)
-    rows_ref[...] = contract(normed, w_xbc_ref[...], ((1,), (1,))).astype(bf16).astype(f32)
+    whole = jnp.dot(normed, w_xbc_ref[...], preferred_element_type=f32)
+    rows_ref[...] = whole.astype(bf16).astype(f32)
     conv = vec_ref[BIAS : BIAS + 1, :]
     for tap in range(BIAS):
         at = EXTRA - (BIAS - 1 - tap)
@@ -195,7 +196,7 @@
     for h in range(own):
         rows = slice(h * head_dim, (h + 1) * head_dim)
         state = jnp.zeros((head_dim, width), f32)
-        for ref, jump in zip(arrived[::-1], jumps[::-1]):
+        for ref, jump in zip(arrived, jumps):
             state = jnp.exp(jump[h]) * state + ref[rows, :].astype(f32)
         for m in range(GROUP):
             back_ref[m, rows, :] = state.astype(bf16)
@@ -321,7 +322,7 @@
     head = jnp.stack([step_bias, rates], axis=1)
 
     whole = lax.all_to_all(columns, "table", split_axis=0, concat_axis=2, tiled=True)
-    whole, w_xbc_t, vec, head = lax.optimization_barrier((whole, w_xbc.T, vec, head))
+    whole, w_xbc, vec, head = lax.optimization_barrier((whole, w_xbc, vec, head))
     x = whole.reshape(length, depth).T
     edge = passed_along(x[:, length - EDGE :], "seq", 1)
     normed, act, dt, cs, state, logs, first, coef_first = call(
@@ -336,14 +337,19 @@
             shape((EXTRA, depth), f32),
             shape((EXTRA, inner), f32),
         ],
-        [pltpu.VMEM((heads, length), f32), pltpu.VMEM((GROUP * EXTRA, state_width), f32)],
-        x, vec, w_xbc_t, w_step.T, head, gaps,
+        [
+            pltpu.VMEM((heads, length), f32),
+            pltpu.VMEM((GROUP * EXTRA, state_width), f32),
+            pltpu.VMEM((length, depth), bf16),
+            pltpu.VMEM((EXTRA + length, width), f32),
+        ],
+        x, vec, w_xbc, w_step.T, head, gaps,
     )
     send, act_first = call(
         edge_kernel,
         [shape((GROUP, size + EXTRA, state_width), bf16), shape((EXTRA, width), f32)],
         [pltpu.VMEM((2 * EXTRA, width), f32)],
-        edge, first, vec, w_xbc_t, coef_first, state, logs,
+        edge, first, vec, w_xbc, coef_first, state, logs,
     )
     states = within_groups(send)
     total = call(
@@ -353,7 +359,7 @@
         states,
     )
     count = lax.axis_size("seq") // GROUP
-    arrived = [passed_along(total, "seq", GROUP * step) for step in range(1, count)]
+    arrived = [passed_along(total, "seq", GROUP * step) for step in range(count - 1, 0, -1)]
     gate, y, query = call(
         inside_kernel,
         [

time: 76.7 us -> 77.1 us (level)
  waiting for transfers between devices: 7.2 us -> 5.22 us
  local copies, waits for them, and re-layouts: 1.8 us -> 3.53 us
  other arithmetic: 0.04 us -> 1.46 us
    ppermute x4, waiting for transfers between devices: 1.68 us -> 0.01 us  [passed_along(): return lax.ppermute(block, axis, route)]
    unnamed x21 -> x12, local copies, waits for them, and re-layouts: 1.7 us -> 2.73 us
  transfers between devices with their start and end apart: 5 -> 5, of which waited for: 2 -> 1; matrix products, arithmetic and copies ran while one was open for 2% -> 3% of each run, Pallas kernels for 9% -> 8%
where the time goes in v3:
time: 77.1 us; the launch traced here: 76.5 us
  blocking collectives  28.8 us (37%)
  starting transfers between devices  28.6 us (37%)
  Pallas kernels  8.8 us (11%)
  waiting for transfers between devices  5.22 us (7%)
  local copies, waits for them, and re-layouts  3.53 us (5%)
  other arithmetic  1.46 us (2%)
    all_to_all x2, blocking collectives, within_groups(): lax.all_to_all(blocks, 'seq', split_axis=0, concat_axis=0, tiled=True, ax...  28.8 us
    ppermute x4, starting transfers between devices, passed_along(): return lax.ppermute(block, axis, route)  21 us
    pallas_call x6, Pallas kernels, call(): pl.pallas_call(kernel, out_shape=outs, in_specs=[left if at in fetched el...  8.8 us
    all_to_all x1, starting transfers between devices, local(): lax.all_to_all(columns, 'table', split_axis=0, concat_axis=2, tiled=True)  7.58 us
    all_to_all x1, waiting for transfers between devices, local(): lax.all_to_all(columns, 'table', split_axis=0, concat_axis=2, tiled=True)  5.21 us
    unnamed x12, local copies, waits for them, and re-layouts  2.73 us
  transfers between devices with their start and end apart: 5, of which 1 were waited for; matrix products, arithmetic and copies ran while one was open for 3% of the time, Pallas kernels for 8%

profile of v3, /device:TPU:1, one launch (start us, length us, event | category | flops | bytes accessed | tf_op | source)
XLA Modules:
  0.0 76.5 jit_solution(10595213051982894802)
XLA Ops:
  0.0 7.6 %all-to-all-start = ((bf16[16,256,32]{1,2,0:T(8,128)(2,1)}), bf16[16,256,32]{1,2,0:T(8,128)(2,1)S(1)}, u32[]{:S(2)}, u32[]{:S(2)}) async-start(bf16[16,256,32]{1,2,0:T(8,128)(2,1)} %param.12), calls=%async_computation | async-start | bytes 524288 | tf_op jit(solution)/shard_map/all_to_all | solution.py:324
  7.6 0.7 broadcast_in_dim.12
  8.3 0.8 %select_maximum_fusion = f32[7,1280]{1,0:T(8,128)S(1)} fusion(f32[1,1024]{1,0:T(1,128)} %bitcast.19, f32[1,512]{1,0:T(1,128)} %bitcast.20, f32[1,1280]{1,0:T(1,128)S(1)} %broadcast_in_dim.12, f32[4,1280]{1,0:T(4,128)} %param.19), kind=kLoop, calls=%fused_computation.2 | loop fusion | flops 80640 | bytes 67584 | tf_op jit(solution)/shard_map/concatenate | solution.py:320
  9.1 0.7 pad_maximum_fusion
  9.8 5.2 %all-to-all-done = bf16[16,256,32]{1,2,0:T(8,128)(2,1)S(1)} async-done(((bf16[16,256,32]{1,2,0:T(8,128)(2,1)}), bf16[16,256,32]{1,2,0:T(8,128)(2,1)S(1)}, u32[]{:S(2)}, u32[]{:S(2)}) %all-to-all-start) | async-done | bytes 262176 | tf_op jit(solution)/shard_map/all_to_all | solution.py:324
  15.0 5.5 %collective-permute-start = (bf16[512,128]{1,0:T(8,128)(2,1)S(1)}, bf16[512,128]{1,0:T(8,128)(2,1)S(1)}, u32[]{:S(2)}, u32[]{:S(2)}) collective-permute-start(bf16[512,128]{1,0:T(8,128)(2,1)S(1)} %slice.4), channel_id=1, source_target_pairs={{0,16},{16,32},{32,48},{48,64},{64,80},{80,96},{96,112},{112,128},... | collective-permute-start | bytes 393224 | tf_op jit(solution)/shard_map/ppermute | solution.py:22
  20.5 0.1 copy.15.head_ref
  20.6 0.0 copy-start
  20.6 1.3 %copy-done = bf16[512,1280]{1,0:T(8,128)(2,1)S(1)} copy-done((bf16[512,1280]{1,0:T(8,128)(2,1)S(1)}, bf16[512,1280]{1,0:T(8,128)(2,1)}, u32[]{:S(2)}) %copy-start) | copy-done | bytes 1310744
  21.9 0.0 copy-start.4
  21.9 0.7 copy-done.4
  22.6 0.0 copy-start.5
  22.6 0.7 copy-done.5
  23.3 0.0 copy-start.1
  23.3 3.5 %shard_map.118 = (bf16[512,256]{1,0:T(8,128)(2,1)S(1)}, bf16[1280,256]{1,0:T(8,128)(2,1)S(1)}, f32[16,256]{1,0:T(8,128)S(1)}, f32[16,256]{1,0:T(8,128)S(1)}, f32...) custom-call(bf16[512,256]{1,0:T(8,128)(2,1)S(1)} %bitcast.16, ...), custom_call_target="tpu_custom_call" | custom-call | tf_op jit(solution)/shard_map/pallas_call | solution.py:286
  26.9 0.0 collective-permute-done.edge_ref
  26.9 0.0 copy-done.1
  26.9 0.0 copy-start.2
  26.9 0.7 shard_map.119
  27.6 16.6 %all_to_all.28.states_ref = bf16[8,136,128]{2,1,0:T(8,128)(2,1)S(1)} all-to-all(bf16[8,136,128]{2,1,0:T(8,128)(2,1)S(1)} %get-tuple-element.35), channel_id=1, replica_groups={{0,16,32,48,64,80,96,112},{128,144,160,176,192,208,224,240},{256,272,28..., dimensions={0} | all-to-all | bytes 557056 | tf_op jit(solution)/shard_map/all_to_all | solution.py:28
  44.3 0.1 shard_map.121
  44.4 7.2 %collective-permute-start.1 = (bf16[136,128]{1,0:T(8,128)(2,1)S(1)}, bf16[136,128]{1,0:T(8,128)(2,1)S(1)}, u32[]{:S(2)}, u32[]{:S(2)}) collective-permute-start(bf16[136,128]{1,0:T(8,128)(2,1)S(1)} %shard_map.121), channel_id=1, source_target_pairs={{0,384},{16,400},{32,416},{48,432},{64,448},{80,464},{96,480},{112... | collective-permute-start | bytes 104456 | tf_op jit(solution)/shard_map/ppermute | solution.py:22
  51.5 4.1 %collective-permute-start.2 = (bf16[136,128]{1,0:T(8,128)(2,1)S(1)}, bf16[136,128]{1,0:T(8,128)(2,1)S(1)}, u32[]{:S(2)}, u32[]{:S(2)}) collective-permute-start(bf16[136,128]{1,0:T(8,128)(2,1)S(1)} %shard_map.121), channel_id=1, source_target_pairs={{0,256},{16,272},{32,288},{48,304},{64,320},{80,336},{96,352},{112... | collective-permute-start | bytes 104456 | tf_op jit(solution)/shard_map/ppermute | solution.py:22
  55.7 4.2 %collective-permute-start.3 = (bf16[136,128]{1,0:T(8,128)(2,1)S(1)}, bf16[136,128]{1,0:T(8,128)(2,1)S(1)}, u32[]{:S(2)}, u32[]{:S(2)}) collective-permute-start(bf16[136,128]{1,0:T(8,128)(2,1)S(1)} %shard_map.121), channel_id=1, source_target_pairs={{0,128},{16,144},{32,160},{48,176},{64,192},{80,208},{96,224},{112... | collective-permute-start | bytes 104456 | tf_op jit(solution)/shard_map/ppermute | solution.py:22
  59.9 0.0 copy-done.2
  59.9 0.0 copy-start.3
  59.9 2.5 %shard_map.120 = (f32[1024,256]{1,0:T(8,128)S(1)}, f32[1024,256]{1,0:T(8,128)S(1)}, bf16[128,256]{1,0:T(8,128)(2,1)S(1)}) custom-call(bf16[512,256]{1,0:T(8,128)(2,1)S(1)} %get-tuple-element.36.normed_ref, bf16[512,1024]{1,0:T(8,128)(2,1)S(1)} %copy-done.2, bf16[1280,256]{1,0:T(8,128)(2,1)S(1)} %get-tuple-element.37.main_ref, ...), custom_call_target="tpu_custom_call" | custom-call | tf_op jit(solution)/shard_map/pallas_call | solution.py:286
  62.4 0.0 collective-permute-done.1.refs_0_
  62.4 0.0 collective-permute-done.2.refs_1_
  62.4 0.0 collective-permute-done.3.refs_2_
  62.4 0.1 shard_map.122
  62.5 12.2 %all_to_all.29 = bf16[8,128,128]{2,1,0:T(8,128)(2,1)S(1)} all-to-all(bf16[8,128,128]{2,1,0:T(8,128)(2,1)S(1)} %shard_map.122), channel_id=1, replica_groups={{0,16,32,48,64,80,96,112},{128,144,160,176,192,208,224,240},{256,272,28..., dimensions={0} | all-to-all | bytes 524288 | tf_op jit(solution)/shard_map/all_to_all | solution.py:28
  74.7 0.0 copy-done.3
  74.7 1.8 %shard_map.123 = bf16[256,512]{1,0:T(8,128)(2,1)} custom-call(bf16[1024,128]{1,0:T(8,128)(2,1)S(1)} %bitcast.17, bf16[128,256]{1,0:T(8,128)(2,1)S(1)} %get-tuple-element.46.query_ref, f32[16,256]{1,0:T(8,128)S(1)} %get-tuple-element.40.cs_ref, f32[1024,256]{1,0:T(8,128)S(1)} %get-tuple-element.47.y_ref, f32[1024,256]{1,0:T(8,128)S(1)} %get-tuple-element.48.gate_ref, ...), custom_call_target="tpu_custom_call" | custom-call | tf_op jit(solution)/shard_map/pallas_call | solution.py:286
  (2 shorter events, 0.0 us)
Async XLA Ops:
  0.0 15.0 %all-to-all-start = ((bf16[16,256,32]{1,2,0:T(8,128)(2,1)}), bf16[16,256,32]{1,2,0:T(8,128)(2,1)S(1)}, u32[]{:S(2)}, u32[]{:S(2)}) async-start(bf16[16,256,32]{1,2,0:T(8,128)(2,1)} %param.12), calls=%async_computation | async-start | bytes 524288 | tf_op jit(solution)/shard_map/all_to_all | solution.py:324
  15.0 11.9 %collective-permute-start = (bf16[512,128]{1,0:T(8,128)(2,1)S(1)}, bf16[512,128]{1,0:T(8,128)(2,1)S(1)}, u32[]{:S(2)}, u32[]{:S(2)}) collective-permute-start(bf16[512,128]{1,0:T(8,128)(2,1)S(1)} %slice.4), channel_id=1, source_target_pairs={{0,16},{16,32},{32,48},{48,64},{64,80},{80,96},{96,112},{112,128},... | collective-permute-start | bytes 393224 | tf_op jit(solution)/shard_map/ppermute | solution.py:22
  20.6 1.3 %copy-start = (bf16[512,1280]{1,0:T(8,128)(2,1)S(1)}, bf16[512,1280]{1,0:T(8,128)(2,1)}, u32[]{:S(2)}) copy-start(bf16[512,1280]{1,0:T(8,128)(2,1)} %w_xbc_ref.1) | copy-start | bytes 3932164
  21.9 0.7 copy-start.4
  22.6 0.7 copy-start.5
  23.3 3.6 %copy-start.1 = (bf16[512,1280]{1,0:T(8,128)(2,1)S(1)}, bf16[512,1280]{1,0:T(8,128)(2,1)}, u32[]{:S(2)}) copy-start(bf16[512,1280]{1,0:T(8,128)(2,1)} %w_xbc_ref.1) | copy-start | bytes 3932164
  26.9 33.0 %copy-start.2 = (bf16[512,1024]{1,0:T(8,128)(2,1)S(1)}, bf16[512,1024]{1,0:T(8,128)(2,1)}, u32[]{:S(2)}) copy-start(bf16[512,1024]{1,0:T(8,128)(2,1)} %w_gate_ref.1) | copy-start | bytes 3145732
  44.4 18.1 %collective-permute-start.1 = (bf16[136,128]{1,0:T(8,128)(2,1)S(1)}, bf16[136,128]{1,0:T(8,128)(2,1)S(1)}, u32[]{:S(2)}, u32[]{:S(2)}) collective-permute-start(bf16[136,128]{1,0:T(8,128)(2,1)S(1)} %shard_map.121), channel_id=1, source_target_pairs={{0,384},{16,400},{32,416},{48,432},{64,448},{80,464},{96,480},{112... | collective-permute-start | bytes 104456 | tf_op jit(solution)/shard_map/ppermute | solution.py:22
  51.5 10.9 %collective-permute-start.2 = (bf16[136,128]{1,0:T(8,128)(2,1)S(1)}, bf16[136,128]{1,0:T(8,128)(2,1)S(1)}, u32[]{:S(2)}, u32[]{:S(2)}) collective-permute-start(bf16[136,128]{1,0:T(8,128)(2,1)S(1)} %shard_map.121), channel_id=1, source_target_pairs={{0,256},{16,272},{32,288},{48,304},{64,320},{80,336},{96,352},{112... | collective-permute-start | bytes 104456 | tf_op jit(solution)/shard_map/ppermute | solution.py:22
  55.7 6.8 %collective-permute-start.3 = (bf16[136,128]{1,0:T(8,128)(2,1)S(1)}, bf16[136,128]{1,0:T(8,128)(2,1)S(1)}, u32[]{:S(2)}, u32[]{:S(2)}) collective-permute-start(bf16[136,128]{1,0:T(8,128)(2,1)S(1)} %shard_map.121), channel_id=1, source_target_pairs={{0,128},{16,144},{32,160},{48,176},{64,192},{80,208},{96,224},{112... | collective-permute-start | bytes 104456 | tf_op jit(solution)/shard_map/ppermute | solution.py:22
  59.9 14.8 %copy-start.3 = (bf16[1024,512]{1,0:T(8,128)(2,1)S(1)}, bf16[1024,512]{1,0:T(8,128)(2,1)}, u32[]{:S(2)}) copy-start(bf16[1024,512]{1,0:T(8,128)(2,1)} %w_out_ref.1) | copy-start | bytes 3145732

commit v4 on v3

--- a/solution.py
+++ b/solution.py
@@ -16,10 +16,14 @@
 bf16 = jnp.bfloat16
 
 
-def passed_along(block, axis, distance):
+def passed_along(block, axis, distance, senders=None):
     devices = range(lax.axis_size(axis))
-    route = [(i - distance, i) for i in devices if i - distance in devices]
+    route = [(i, i + distance) for i in senders or devices if i + distance in devices]
     return lax.ppermute(block, axis, route)
+
+
+def members(*groups):
+    return [g * GROUP + i for g in groups for i in range(GROUP)]
 
 
 def within_groups(blocks):
@@ -59,6 +63,18 @@
         values = values + jnp.where(lane >= reach, pltpu.roll(values, reach, axis=1), 0.0)
         reach *= 2
     return values
+
+
+def stage_kernel(*refs):
+    count = len(refs) // 2
+    sems = refs[-1]
+    copies = [
+        pltpu.make_async_copy(refs[at], refs[count + at], sems.at[at]) for at in range(count)
+    ]
+    for copy in copies:
+        copy.start()
+    for copy in copies:
+        copy.wait()
 
 
 def main_kernel(x_ref, vec_ref, w_xbc_ref, w_step_ref, head_ref, gaps_ref,
@@ -186,18 +202,25 @@
     send_ref[size : size + EXTRA, :] = rows_ref[...].astype(bf16)
 
 
-def combine_kernel(own, states_ref, *refs):
-    arrived, back_ref = refs[:-1], refs[-1]
+def join_kernel(own, total_ref, earlier_ref, send_ref):
+    size = send_ref.shape[0]
+    head_dim = size // own
+    jumps = read_logs(total_ref[size : size + EXTRA, :], own)
+    for h in range(own):
+        rows = slice(h * head_dim, (h + 1) * head_dim)
+        state = jnp.exp(jumps[h]) * earlier_ref[rows, :].astype(f32)
+        send_ref[rows, :] = (total_ref[rows, :].astype(f32) + state).astype(bf16)
+
+
+def combine_kernel(own, states_ref, near_ref, far_a_ref, far_b_ref, back_ref):
     size = back_ref.shape[1]
     head_dim = size // own
-    width = back_ref.shape[2]
     logs = [read_logs(states_ref[m, size : size + EXTRA, :], own) for m in range(GROUP)]
-    jumps = [read_logs(ref[size : size + EXTRA, :], own) for ref in arrived]
+    jumps = read_logs(near_ref[size : size + EXTRA, :], own)
     for h in range(own):
         rows = slice(h * head_dim, (h + 1) * head_dim)
-        state = jnp.zeros((head_dim, width), f32)
-        for ref, jump in zip(arrived, jumps):
-            state = jnp.exp(jump[h]) * state + ref[rows, :].astype(f32)
+        far = far_a_ref[rows, :].astype(f32) + far_b_ref[rows, :].astype(f32)
+        state = near_ref[rows, :].astype(f32) + jnp.exp(jumps[h]) * far
         for m in range(GROUP):
             back_ref[m, rows, :] = state.astype(bf16)
             state = jnp.exp(logs[m][h]) * state + states_ref[m, rows, :].astype(f32)
@@ -281,7 +304,7 @@
 
 def call(kernel, outs, scratch, *args, fetched=()):
     vmem = pl.BlockSpec(memory_space=pltpu.VMEM)
-    left = pl.BlockSpec(memory_space=pl.ANY)
+    left = pl.BlockSpec(memory_space=pltpu.HBM)
     single = not isinstance(outs, list)
     return pl.pallas_call(
         kernel,
@@ -322,7 +345,16 @@
     head = jnp.stack([step_bias, rates], axis=1)
 
     whole = lax.all_to_all(columns, "table", split_axis=0, concat_axis=2, tiled=True)
-    whole, w_xbc, vec, head = lax.optimization_barrier((whole, w_xbc, vec, head))
+    staged = [w_xbc, w_step.T, gaps]
+    staged = call(
+        stage_kernel,
+        [shape(a.shape, a.dtype) for a in staged],
+        [pltpu.SemaphoreType.DMA((len(staged),))],
+        *staged,
+        fetched=range(len(staged)),
+    )
+    whole, vec, head, *staged = lax.optimization_barrier((whole, vec, head, *staged))
+    w_xbc, w_step_t, gaps = staged
     x = whole.reshape(length, depth).T
     edge = passed_along(x[:, length - EDGE :], "seq", 1)
     normed, act, dt, cs, state, logs, first, coef_first = call(
@@ -343,7 +375,7 @@
             pltpu.VMEM((length, depth), bf16),
             pltpu.VMEM((EXTRA + length, width), f32),
         ],
-        x, vec, w_xbc, w_step.T, head, gaps,
+        x, vec, w_xbc, w_step_t, head, gaps,
     )
     send, act_first = call(
         edge_kernel,
@@ -358,8 +390,16 @@
         [pltpu.VMEM((EXTRA, state_width), f32)],
         states,
     )
-    count = lax.axis_size("seq") // GROUP
-    arrived = [passed_along(total, "seq", GROUP * step) for step in range(count - 1, 0, -1)]
+    assert lax.axis_size("seq") == 4 * GROUP
+    near = passed_along(total, "seq", GROUP, members(0, 2))
+    joined = call(
+        functools.partial(join_kernel, own),
+        shape((size, state_width), bf16),
+        [],
+        total, near,
+    )
+    far_b = passed_along(joined, "seq", 2 * GROUP, members(1))
+    far_a = passed_along(joined, "seq", GROUP, members(1))
     gate, y, query = call(
         inside_kernel,
         [
@@ -377,12 +417,12 @@
         normed, w_gate, act, act_first, dt, cs,
         fetched=(1,),
     )
-    gate, y, *arrived = lax.optimization_barrier((gate, y, *arrived))
+    gate, y, far_b, far_a = lax.optimization_barrier((gate, y, far_b, far_a))
     back = call(
         functools.partial(combine_kernel, own),
         shape((GROUP, size, state_width), bf16),
         [],
-        states, *arrived,
+        states, near, far_a, far_b,
     )
     carried = within_groups(back).reshape(inner, state_width)
     out = call(

time: 77.1 us -> 76.3 us (0.990)
  the two profiles are of different devices: /device:TPU:1 before, /device:TPU:128 now
where the time goes in v4:
time: 76.3 us; the launch traced here: 75.7 us
  blocking collectives  29.4 us (39%)
  starting transfers between devices  18.4 us (24%)
  waiting for transfers between devices  14.5 us (19%)
  Pallas kernels  8.97 us (12%)
  local copies, waits for them, and re-layouts  3.53 us (5%)
  other arithmetic  0.79 us (1%)
    all_to_all x2, blocking collectives, within_groups(): lax.all_to_all(blocks, 'seq', split_axis=0, concat_axis=0, tiled=True, ax...  29.4 us
    ppermute x4, starting transfers between devices, passed_along(): return lax.ppermute(block, axis, route)  11.2 us
    ppermute x4, waiting for transfers between devices, passed_along(): return lax.ppermute(block, axis, route)  10.4 us
    pallas_call x8, Pallas kernels, call(): pl.pallas_call(kernel, out_shape=outs, in_specs=[left if at in fetched el...  8.97 us
    all_to_all x1, starting transfers between devices, local(): lax.all_to_all(columns, 'table', split_axis=0, concat_axis=2, tiled=True)  7.17 us
    all_to_all x1, waiting for transfers between devices, local(): lax.all_to_all(columns, 'table', split_axis=0, concat_axis=2, tiled=True)  4.11 us
    unnamed x14, local copies, waits for them, and re-layouts  2.72 us
  transfers between devices with their start and end apart: 5, of which 3 were waited for; matrix products, arithmetic and copies ran while one was open for 2% of the time, Pallas kernels for 8%

profile of v4, /device:TPU:128, one launch (start us, length us, event | category | flops | bytes accessed | tf_op | source)
XLA Modules:
  0.0 75.7 jit_solution(1484402219739603589)
XLA Ops:
  0.0 0.0 copy-start.5
  0.0 0.0 copy-start.6
  0.0 7.2 %all-to-all-start = ((bf16[16,256,32]{1,2,0:T(8,128)(2,1)}), bf16[16,256,32]{1,2,0:T(8,128)(2,1)S(1)}, u32[]{:S(2)}, u32[]{:S(2)}) async-start(bf16[16,256,32]{1,2,0:T(8,128)(2,1)} %param.12), calls=%async_computation | async-start | bytes 524288 | tf_op jit(solution)/shard_map/all_to_all | solution.py:347
  7.2 0.7 broadcast_in_dim.12
  7.9 0.8 %select_maximum_fusion = f32[7,1280]{1,0:T(8,128)S(1)} fusion(f32[1,1024]{1,0:T(1,128)} %bitcast.19, f32[1,512]{1,0:T(1,128)} %bitcast.20, f32[1,1280]{1,0:T(1,128)S(1)} %broadcast_in_dim.12, f32[4,1280]{1,0:T(4,128)} %param.19), kind=kLoop, calls=%fused_computation.2 | loop fusion | flops 80640 | bytes 67584 | tf_op jit(solution)/shard_map/concatenate | solution.py:343
  8.7 0.0 copy-start
  8.7 1.3 %copy-done = bf16[512,1280]{1,0:T(8,128)(2,1)S(1)} copy-done((bf16[512,1280]{1,0:T(8,128)(2,1)S(1)}, bf16[512,1280]{1,0:T(8,128)(2,1)}, u32[]{:S(2)}) %copy-start) | copy-done | bytes 1310744
  10.0 0.0 copy-start.3
  10.0 0.7 copy-done.3
  10.7 0.0 copy-start.4
  10.7 0.7 copy-done.4
  11.4 0.1 shard_map.118
  11.5 0.0 copy-done.5
  11.6 0.0 copy-done.6
  11.6 4.1 %all-to-all-done = bf16[16,256,32]{1,2,0:T(8,128)(2,1)S(1)} async-done(((bf16[16,256,32]{1,2,0:T(8,128)(2,1)}), bf16[16,256,32]{1,2,0:T(8,128)(2,1)S(1)}, u32[]{:S(2)}, u32[]{:S(2)}) %all-to-all-start) | async-done | bytes 262176 | tf_op jit(solution)/shard_map/all_to_all | solution.py:347
  15.7 1.9 %collective-permute-start = (bf16[512,128]{1,0:T(8,128)(2,1)S(1)}, bf16[512,128]{1,0:T(8,128)(2,1)S(1)}, u32[]{:S(2)}, u32[]{:S(2)}) collective-permute-start(bf16[512,128]{1,0:T(8,128)(2,1)S(1)} %slice.4), channel_id=1, source_target_pairs={{0,16},{16,32},{32,48},{48,64},{64,80},{80,96},{96,112},{112,128},... | collective-permute-start | bytes 393224 | tf_op jit(solution)/shard_map/ppermute | solution.py:22
  17.6 0.1 copy.15.head_ref
  17.7 3.5 %shard_map.119 = (bf16[512,256]{1,0:T(8,128)(2,1)S(1)}, bf16[1280,256]{1,0:T(8,128)(2,1)S(1)}, f32[16,256]{1,0:T(8,128)S(1)}, f32[16,256]{1,0:T(8,128)S(1)}, f32...) custom-call(bf16[512,256]{1,0:T(8,128)(2,1)S(1)} %bitcast.16, ...), custom_call_target="tpu_custom_call" | custom-call | tf_op jit(solution)/shard_map/pallas_call | solution.py:309
  21.3 1.9 %collective-permute-done.edge_ref = bf16[512,128]{1,0:T(8,128)(2,1)S(1)} collective-permute-done((bf16[512,128]{1,0:T(8,128)(2,1)S(1)}, bf16[512,128]{1,0:T(8,128)(2,1)S(1)}, u32[]{:S(2)}, u32[]{:S(2)}) %collective-permute-start) | collective-permute-done | bytes 131104 | tf_op jit(solution)/shard_map/ppermute | solution.py:22
  23.2 0.0 copy-start.1
  23.2 0.7 shard_map.120
  23.9 16.7 %all_to_all.28.states_ref = bf16[8,136,128]{2,1,0:T(8,128)(2,1)S(1)} all-to-all(bf16[8,136,128]{2,1,0:T(8,128)(2,1)S(1)} %get-tuple-element.44), channel_id=1, replica_groups={{0,16,32,48,64,80,96,112},{128,144,160,176,192,208,224,240},{256,272,28..., dimensions={0} | all-to-all | bytes 557056 | tf_op jit(solution)/shard_map/all_to_all | solution.py:32
  40.7 0.1 shard_map.121.total_ref
  40.8 1.3 %collective-permute-start.1 = (bf16[136,128]{1,0:T(8,128)(2,1)S(1)}, bf16[136,128]{1,0:T(8,128)(2,1)S(1)}, u32[]{:S(2)}, u32[]{:S(2)}) collective-permute-start(bf16[136,128]{1,0:T(8,128)(2,1)S(1)} %shard_map.121.total_ref), channel_id=1, source_target_pairs={{0,128},{16,144},{32,160},{48,176},{64,192},{80,208},{96,224},{112... | collective-permute-start | bytes 104456 | tf_op jit(solution)/shard_map/ppermute | solution.py:22
  42.0 8.4 %collective-permute-done.1.earlier_ref.near_ref = bf16[136,128]{1,0:T(8,128)(2,1)S(1)} collective-permute-done((bf16[136,128]{1,0:T(8,128)(2,1)S(1)}, bf16[136,128]{1,0:T(8,128)(2,1)S(1)}, u32[]{:S(2)}, u32[]{:S(2)}) %collective-permute-start.1) | collective-permute-done | bytes 34848 | tf_op jit(solution)/shard_map/ppermute | solution.py:22
  50.5 6.7 %collective-permute-start.2 = (bf16[128,128]{1,0:T(8,128)(2,1)S(1)}, bf16[128,128]{1,0:T(8,128)(2,1)S(1)}, u32[]{:S(2)}, u32[]{:S(2)}) collective-permute-start(bf16[128,128]{1,0:T(8,128)(2,1)S(1)} %shard_map.123), channel_id=1, source_target_pairs={{128,384},{144,400},{160,416},{176,432},{192,448},{208,464},{224,4... | collective-permute-start | bytes 98312 | tf_op jit(solution)/shard_map/ppermute | solution.py:22
  57.2 1.3 %collective-permute-start.3 = (bf16[128,128]{1,0:T(8,128)(2,1)S(1)}, bf16[128,128]{1,0:T(8,128)(2,1)S(1)}, u32[]{:S(2)}, u32[]{:S(2)}) collective-permute-start(bf16[128,128]{1,0:T(8,128)(2,1)S(1)} %shard_map.123), channel_id=1, source_target_pairs={{128,256},{144,272},{160,288},{176,304},{192,320},{208,336},{224,3... | collective-permute-start | bytes 98312 | tf_op jit(solution)/shard_map/ppermute | solution.py:22
  58.5 0.0 copy-done.1
  58.5 0.0 copy-start.2
  58.5 2.6 %shard_map.122 = (f32[1024,256]{1,0:T(8,128)S(1)}, f32[1024,256]{1,0:T(8,128)S(1)}, bf16[128,256]{1,0:T(8,128)(2,1)S(1)}) custom-call(bf16[512,256]{1,0:T(8,128)(2,1)S(1)} %get-tuple-element.45.normed_ref, bf16[512,1024]{1,0:T(8,128)(2,1)S(1)} %copy-done.1, bf16[1280,256]{1,0:T(8,128)(2,1)S(1)} %get-tuple-element.46.main_ref, ...), custom_call_target="tpu_custom_call" | custom-call | tf_op jit(solution)/shard_map/pallas_call | solution.py:309
  61.1 0.0 collective-permute-done.2.far_b_ref
  61.1 0.0 collective-permute-done.3.far_a_ref
  61.1 0.1 shard_map.124
  61.2 12.7 %all_to_all.29 = bf16[8,128,128]{2,1,0:T(8,128)(2,1)S(1)} all-to-all(bf16[8,128,128]{2,1,0:T(8,128)(2,1)S(1)} %shard_map.124), channel_id=1, replica_groups={{0,16,32,48,64,80,96,112},{128,144,160,176,192,208,224,240},{256,272,28..., dimensions={0} | all-to-all | bytes 524288 | tf_op jit(solution)/shard_map/all_to_all | solution.py:32
  73.9 0.0 copy-done.2
  73.9 1.8 %shard_map.125 = bf16[256,512]{1,0:T(8,128)(2,1)} custom-call(bf16[1024,128]{1,0:T(8,128)(2,1)S(1)} %bitcast.17, bf16[128,256]{1,0:T(8,128)(2,1)S(1)} %get-tuple-element.54.query_ref, f32[16,256]{1,0:T(8,128)S(1)} %get-tuple-element.49.cs_ref, f32[1024,256]{1,0:T(8,128)S(1)} %get-tuple-element.55.y_ref, f32[1024,256]{1,0:T(8,128)S(1)} %get-tuple-element.56.gate_ref, ...), custom_call_target="tpu_custom_call" | custom-call | tf_op jit(solution)/shard_map/pallas_call | solution.py:309
  (4 shorter events, 0.0 us)
Async XLA Ops:
  0.0 11.5 %copy-start.5 = (f32[16]{0:T(128)S(1)}, f32[16]{0:T(128)}, u32[]{:S(2)}) copy-start(f32[16]{0:T(128)} %param.21) | copy-start | bytes 196
  0.0 11.6 %copy-start.6 = (f32[16]{0:T(128)S(1)}, f32[16]{0:T(128)}, u32[]{:S(2)}) copy-start(f32[16]{0:T(128)} %param.18) | copy-start | bytes 196
  0.0 15.7 %all-to-all-start = ((bf16[16,256,32]{1,2,0:T(8,128)(2,1)}), bf16[16,256,32]{1,2,0:T(8,128)(2,1)S(1)}, u32[]{:S(2)}, u32[]{:S(2)}) async-start(bf16[16,256,32]{1,2,0:T(8,128)(2,1)} %param.12), calls=%async_computation | async-start | bytes 524288 | tf_op jit(solution)/shard_map/all_to_all | solution.py:347
  8.7 1.3 %copy-start = (bf16[512,1280]{1,0:T(8,128)(2,1)S(1)}, bf16[512,1280]{1,0:T(8,128)(2,1)}, u32[]{:S(2)}) copy-start(bf16[512,1280]{1,0:T(8,128)(2,1)} %refs_0_.1) | copy-start | bytes 3932164
  10.0 0.7 copy-start.3
  10.7 0.7 copy-start.4
  15.7 7.5 %collective-permute-start = (bf16[512,128]{1,0:T(8,128)(2,1)S(1)}, bf16[512,128]{1,0:T(8,128)(2,1)S(1)}, u32[]{:S(2)}, u32[]{:S(2)}) collective-permute-start(bf16[512,128]{1,0:T(8,128)(2,1)S(1)} %slice.4), channel_id=1, source_target_pairs={{0,16},{16,32},{32,48},{48,64},{64,80},{80,96},{96,112},{112,128},... | collective-permute-start | bytes 393224 | tf_op jit(solution)/shard_map/ppermute | solution.py:22
  23.2 35.3 %copy-start.1 = (bf16[512,1024]{1,0:T(8,128)(2,1)S(1)}, bf16[512,1024]{1,0:T(8,128)(2,1)}, u32[]{:S(2)}) copy-start(bf16[512,1024]{1,0:T(8,128)(2,1)} %w_gate_ref.1) | copy-start | bytes 3145732
  40.8 9.7 %collective-permute-start.1 = (bf16[136,128]{1,0:T(8,128)(2,1)S(1)}, bf16[136,128]{1,0:T(8,128)(2,1)S(1)}, u32[]{:S(2)}, u32[]{:S(2)}) collective-permute-start(bf16[136,128]{1,0:T(8,128)(2,1)S(1)} %shard_map.121.total_ref), channel_id=1, source_target_pairs={{0,128},{16,144},{32,160},{48,176},{64,192},{80,208},{96,224},{112... | collective-permute-start | bytes 104456 | tf_op jit(solution)/shard_map/ppermute | solution.py:22
  50.5 10.6 %collective-permute-start.2 = (bf16[128,128]{1,0:T(8,128)(2,1)S(1)}, bf16[128,128]{1,0:T(8,128)(2,1)S(1)}, u32[]{:S(2)}, u32[]{:S(2)}) collective-permute-start(bf16[128,128]{1,0:T(8,128)(2,1)S(1)} %shard_map.123), channel_id=1, source_target_pairs={{128,384},{144,400},{160,416},{176,432},{192,448},{208,464},{224,4... | collective-permute-start | bytes 98312 | tf_op jit(solution)/shard_map/ppermute | solution.py:22
  57.2 3.9 %collective-permute-start.3 = (bf16[128,128]{1,0:T(8,128)(2,1)S(1)}, bf16[128,128]{1,0:T(8,128)(2,1)S(1)}, u32[]{:S(2)}, u32[]{:S(2)}) collective-permute-start(bf16[128,128]{1,0:T(8,128)(2,1)S(1)} %shard_map.123), channel_id=1, source_target_pairs={{128,256},{144,272},{160,288},{176,304},{192,320},{208,336},{224,3... | collective-permute-start | bytes 98312 | tf_op jit(solution)/shard_map/ppermute | solution.py:22
  58.5 15.4 %copy-start.2 = (bf16[1024,512]{1,0:T(8,128)(2,1)S(1)}, bf16[1024,512]{1,0:T(8,128)(2,1)}, u32[]{:S(2)}) copy-start(bf16[1024,512]{1,0:T(8,128)(2,1)} %w_out_ref.1) | copy-start | bytes 3145732

commit v5 on v4

--- a/solution.py
+++ b/solution.py
@@ -212,15 +212,14 @@
         send_ref[rows, :] = (total_ref[rows, :].astype(f32) + state).astype(bf16)
 
 
-def combine_kernel(own, states_ref, near_ref, far_a_ref, far_b_ref, back_ref):
+def combine_kernel(own, states_ref, *refs):
+    arrived, back_ref = refs[:-1], refs[-1]
     size = back_ref.shape[1]
     head_dim = size // own
     logs = [read_logs(states_ref[m, size : size + EXTRA, :], own) for m in range(GROUP)]
-    jumps = read_logs(near_ref[size : size + EXTRA, :], own)
     for h in range(own):
         rows = slice(h * head_dim, (h + 1) * head_dim)
-        far = far_a_ref[rows, :].astype(f32) + far_b_ref[rows, :].astype(f32)
-        state = near_ref[rows, :].astype(f32) + jnp.exp(jumps[h]) * far
+        state = sum(ref[rows, :].astype(f32) for ref in arrived)
         for m in range(GROUP):
             back_ref[m, rows, :] = state.astype(bf16)
             state = jnp.exp(logs[m][h]) * state + states_ref[m, rows, :].astype(f32)
@@ -270,8 +269,7 @@
     normed = normed_ref[...]
     for at in range(0, inner, 256):
         gate = contract(weight_ref[:, at : at + 256], normed, ((0,), (0,)))
-        gate = gate.astype(bf16).astype(f32)
-        gate_ref[at : at + 256, :] = gate * jax.nn.sigmoid(gate)
+        gate_ref[at : at + 256, :] = gate.astype(bf16)
 
 
 def output_kernel(carried_ref, query_ref, cs_ref, y_ref, gate_ref, vec_ref, w_out_ref,
@@ -291,7 +289,8 @@
             rows = slice(h * head_dim, (h + 1) * head_dim)
             own = picked[h * head_dim - at : (h + 1) * head_dim - at, :]
             y = y_ref[rows, :] + grown[h : h + 1, :] * own
-            gated = y * gate_ref[rows, :]
+            gate = gate_ref[rows, :].astype(f32)
+            gated = y * (gate * jax.nn.sigmoid(gate))
             gated_ref[rows, :] = gated
             total = total + jnp.sum(gated * gated, axis=0, keepdims=True)
     scale = lax.rsqrt(total / inner + epsilon)
@@ -384,26 +383,10 @@
         edge, first, vec, w_xbc, coef_first, state, logs,
     )
     states = within_groups(send)
-    total = call(
-        functools.partial(prefix_kernel, own),
-        shape((size + EXTRA, state_width), bf16),
-        [pltpu.VMEM((EXTRA, state_width), f32)],
-        states,
-    )
-    assert lax.axis_size("seq") == 4 * GROUP
-    near = passed_along(total, "seq", GROUP, members(0, 2))
-    joined = call(
-        functools.partial(join_kernel, own),
-        shape((size, state_width), bf16),
-        [],
-        total, near,
-    )
-    far_b = passed_along(joined, "seq", 2 * GROUP, members(1))
-    far_a = passed_along(joined, "seq", GROUP, members(1))
     gate, y, query = call(
         inside_kernel,
         [
-            shape((inner, length), f32),
+            shape((inner, length), bf16),
             shape((inner, length), f32),
             shape((state_width, length), bf16),
         ],
@@ -417,12 +400,30 @@
         normed, w_gate, act, act_first, dt, cs,
         fetched=(1,),
     )
-    gate, y, far_b, far_a = lax.optimization_barrier((gate, y, far_b, far_a))
+    total = call(
+        functools.partial(prefix_kernel, own),
+        shape((size + EXTRA, state_width), bf16),
+        [pltpu.VMEM((EXTRA, state_width), f32)],
+        states,
+    )
+    send = total[:size]
+    arrived = []
+    for group in range(lax.axis_size("seq") // GROUP - 1):
+        if group:
+            send = call(
+                functools.partial(join_kernel, own),
+                shape((size, state_width), bf16),
+                [],
+                total, arrived[-1],
+            )
+        arrived.append(passed_along(send, "seq", GROUP, members(group)))
+        if not group:
+            arrived[0], gate, y, query = lax.optimization_barrier((arrived[0], gate, y, query))
     back = call(
         functools.partial(combine_kernel, own),
         shape((GROUP, size, state_width), bf16),
         [],
-        states, near, far_a, far_b,
+        states, *arrived,
     )
     carried = within_groups(back).reshape(inner, state_width)
     out = call(

time: 76.3 us -> 74.7 us (0.979)
  the two profiles are of different devices: /device:TPU:128 before, /device:TPU:384 now
where the time goes in v5:
time: 74.7 us; the launch traced here: 74.2 us
  blocking collectives  25.5 us (34%)
  waiting for transfers between devices  23.4 us (31%)
  starting transfers between devices  11.7 us (16%)
  Pallas kernels  9.09 us (12%)
  local copies, waits for them, and re-layouts  3.53 us (5%)
  other arithmetic  0.79 us (1%)
    all_to_all x2, blocking collectives, within_groups(): lax.all_to_all(blocks, 'seq', split_axis=0, concat_axis=0, tiled=True, ax...  25.5 us
    ppermute x4, waiting for transfers between devices, passed_along(): return lax.ppermute(block, axis, route)  19.3 us
    pallas_call x9, Pallas kernels, call(): pl.pallas_call(kernel, out_shape=outs, in_specs=[left if at in fetched el...  9.09 us
    all_to_all x1, starting transfers between devices, local(): lax.all_to_all(columns, 'table', split_axis=0, concat_axis=2, tiled=True)  7.17 us
    ppermute x4, starting transfers between devices, passed_along(): return lax.ppermute(block, axis, route)  4.54 us
    all_to_all x1, waiting for transfers between devices, local(): lax.all_to_all(columns, 'table', split_axis=0, concat_axis=2, tiled=True)  4.11 us
    unnamed x14, local copies, waits for them, and re-layouts  2.72 us
  transfers between devices with their start and end apart: 5, of which 3 were waited for; matrix products, arithmetic and copies ran while one was open for 2% of the time, Pallas kernels for 8%

profile of v5, /device:TPU:384, one launch (start us, length us, event | category | flops | bytes accessed | tf_op | source)
XLA Modules:
  0.0 74.2 jit_solution(15710351548561790099)
XLA Ops:
  0.0 0.0 copy-start.5
  0.0 0.0 copy-start.6
  0.0 7.2 %all-to-all-start = ((bf16[16,256,32]{1,2,0:T(8,128)(2,1)}), bf16[16,256,32]{1,2,0:T(8,128)(2,1)S(1)}, u32[]{:S(2)}, u32[]{:S(2)}) async-start(bf16[16,256,32]{1,2,0:T(8,128)(2,1)} %param.12), calls=%async_computation | async-start | bytes 524288 | tf_op jit(solution)/shard_map/all_to_all | solution.py:346
  7.2 0.7 broadcast_in_dim.12
  7.9 0.8 %select_maximum_fusion = f32[7,1280]{1,0:T(8,128)S(1)} fusion(f32[1,1024]{1,0:T(1,128)} %bitcast.19, f32[1,512]{1,0:T(1,128)} %bitcast.20, f32[1,1280]{1,0:T(1,128)S(1)} %broadcast_in_dim.12, f32[4,1280]{1,0:T(4,128)} %param.19), kind=kLoop, calls=%fused_computation.2 | loop fusion | flops 80640 | bytes 67584 | tf_op jit(solution)/shard_map/concatenate | solution.py:342
  8.7 0.0 copy-start
  8.7 1.3 %copy-done = bf16[512,1280]{1,0:T(8,128)(2,1)S(1)} copy-done((bf16[512,1280]{1,0:T(8,128)(2,1)S(1)}, bf16[512,1280]{1,0:T(8,128)(2,1)}, u32[]{:S(2)}) %copy-start) | copy-done | bytes 1310744
  10.0 0.0 copy-start.3
  10.0 0.7 copy-done.3
  10.7 0.0 copy-start.4
  10.7 0.7 copy-done.4
  11.4 0.1 shard_map.118
  11.5 0.0 copy-done.5
  11.6 0.0 copy-done.6
  11.6 4.1 %all-to-all-done = bf16[16,256,32]{1,2,0:T(8,128)(2,1)S(1)} async-done(((bf16[16,256,32]{1,2,0:T(8,128)(2,1)}), bf16[16,256,32]{1,2,0:T(8,128)(2,1)S(1)}, u32[]{:S(2)}, u32[]{:S(2)}) %all-to-all-start) | async-done | bytes 262176 | tf_op jit(solution)/shard_map/all_to_all | solution.py:346
  15.7 1.9 %collective-permute-start = (bf16[512,128]{1,0:T(8,128)(2,1)S(1)}, bf16[512,128]{1,0:T(8,128)(2,1)S(1)}, u32[]{:S(2)}, u32[]{:S(2)}) collective-permute-start(bf16[512,128]{1,0:T(8,128)(2,1)S(1)} %slice.8), channel_id=1, source_target_pairs={{0,16},{16,32},{32,48},{48,64},{64,80},{80,96},{96,112},{112,128},... | collective-permute-start | bytes 393224 | tf_op jit(solution)/shard_map/ppermute | solution.py:22
  17.6 0.1 copy.15.head_ref
  17.7 3.5 %shard_map.119 = (bf16[512,256]{1,0:T(8,128)(2,1)S(1)}, bf16[1280,256]{1,0:T(8,128)(2,1)S(1)}, f32[16,256]{1,0:T(8,128)S(1)}, f32[16,256]{1,0:T(8,128)S(1)}, f32...) custom-call(bf16[512,256]{1,0:T(8,128)(2,1)S(1)} %bitcast.16, ...), custom_call_target="tpu_custom_call" | custom-call | tf_op jit(solution)/shard_map/pallas_call | solution.py:308
  21.3 1.9 %collective-permute-done.edge_ref = bf16[512,128]{1,0:T(8,128)(2,1)S(1)} collective-permute-done((bf16[512,128]{1,0:T(8,128)(2,1)S(1)}, bf16[512,128]{1,0:T(8,128)(2,1)S(1)}, u32[]{:S(2)}, u32[]{:S(2)}) %collective-permute-start) | collective-permute-done | bytes 131104 | tf_op jit(solution)/shard_map/ppermute | solution.py:22
  23.2 0.0 copy-start.2
  23.2 0.7 shard_map.120
  23.9 12.5 %all_to_all.28.states_ref = bf16[8,136,128]{2,1,0:T(8,128)(2,1)S(1)} all-to-all(bf16[8,136,128]{2,1,0:T(8,128)(2,1)S(1)} %get-tuple-element.44), channel_id=1, replica_groups={{0,16,32,48,64,80,96,112},{128,144,160,176,192,208,224,240},{256,272,28..., dimensions={0} | all-to-all | bytes 557056 | tf_op jit(solution)/shard_map/all_to_all | solution.py:32
  36.5 0.1 shard_map.121.total_ref
  36.5 0.7 collective-permute-start.1
  37.2 0.0 copy-done.2
  37.2 0.0 copy-start.1
  37.2 2.5 %shard_map.122 = (bf16[1024,256]{1,0:T(8,128)(2,1)S(1)}, f32[1024,256]{1,0:T(8,128)S(1)}, bf16[128,256]{1,0:T(8,128)(2,1)S(1)}) custom-call(bf16[512,256]{1,0:T(8,128)(2,1)S(1)} %get-tuple-element.45.normed_ref, bf16[512,1024]{1,0:T(8,128)(2,1)S(1)} %copy-done.2, bf16[1280,256]{1,0:T(8,128)(2,1)S(1)} %get-tuple-element.46.main_ref, ...), custom_call_target="tpu_custom_call" | custom-call | tf_op jit(solution)/shard_map/pallas_call | solution.py:308
  39.8 0.0 collective-permute-done.1.earlier_ref.refs_0_
  39.8 0.7 collective-permute-start.2
  40.5 0.0 collective-permute-done.2.earlier_ref.refs_1_
  40.5 1.3 %collective-permute-start.3 = (bf16[128,128]{1,0:T(8,128)(2,1)S(1)}, bf16[128,128]{1,0:T(8,128)(2,1)S(1)}, u32[]{:S(2)}, u32[]{:S(2)}) collective-permute-start(bf16[128,128]{1,0:T(8,128)(2,1)S(1)} %shard_map.124), channel_id=1, source_target_pairs={{256,384},{272,400},{288,416},{304,432},{320,448},{336,464},{352,4... | collective-permute-start | bytes 98312 | tf_op jit(solution)/shard_map/ppermute | solution.py:22
  41.8 17.3 %collective-permute-done.3.refs_2_ = bf16[128,128]{1,0:T(8,128)(2,1)S(1)} collective-permute-done((bf16[128,128]{1,0:T(8,128)(2,1)S(1)}, bf16[128,128]{1,0:T(8,128)(2,1)S(1)}, u32[]{:S(2)}, u32[]{:S(2)}) %collective-permute-start.3) | collective-permute-done | bytes 32800 | tf_op jit(solution)/shard_map/ppermute | solution.py:22
  59.1 0.1 shard_map.125
  59.2 13.0 %all_to_all.29 = bf16[8,128,128]{2,1,0:T(8,128)(2,1)S(1)} all-to-all(bf16[8,128,128]{2,1,0:T(8,128)(2,1)S(1)} %shard_map.125), channel_id=1, replica_groups={{0,16,32,48,64,80,96,112},{128,144,160,176,192,208,224,240},{256,272,28..., dimensions={0} | all-to-all | bytes 524288 | tf_op jit(solution)/shard_map/all_to_all | solution.py:32
  72.2 0.0 copy-done.1
  72.2 1.9 %shard_map.126 = bf16[256,512]{1,0:T(8,128)(2,1)} custom-call(bf16[1024,128]{1,0:T(8,128)(2,1)S(1)} %bitcast.17, bf16[128,256]{1,0:T(8,128)(2,1)S(1)} %get-tuple-element.54.query_ref, f32[16,256]{1,0:T(8,128)S(1)} %get-tuple-element.49.cs_ref, f32[1024,256]{1,0:T(8,128)S(1)} %get-tuple-element.55.y_ref, bf16[1024,256]{1,0:T(8,128)(2,1)S(1)} %get-tuple-element.56.gate_ref, ...), custom_call_target="tpu_custom_call" | custom-call | tf_op jit(solution)/shard_map/pallas_call | solution.py:308
  (6 shorter events, 0.1 us)
Async XLA Ops:
  0.0 11.5 %copy-start.5 = (f32[16]{0:T(128)S(1)}, f32[16]{0:T(128)}, u32[]{:S(2)}) copy-start(f32[16]{0:T(128)} %param.21) | copy-start | bytes 196
  0.0 11.6 %copy-start.6 = (f32[16]{0:T(128)S(1)}, f32[16]{0:T(128)}, u32[]{:S(2)}) copy-start(f32[16]{0:T(128)} %param.18) | copy-start | bytes 196
  0.0 15.7 %all-to-all-start = ((bf16[16,256,32]{1,2,0:T(8,128)(2,1)}), bf16[16,256,32]{1,2,0:T(8,128)(2,1)S(1)}, u32[]{:S(2)}, u32[]{:S(2)}) async-start(bf16[16,256,32]{1,2,0:T(8,128)(2,1)} %param.12), calls=%async_computation | async-start | bytes 524288 | tf_op jit(solution)/shard_map/all_to_all | solution.py:346
  8.7 1.3 %copy-start = (bf16[512,1280]{1,0:T(8,128)(2,1)S(1)}, bf16[512,1280]{1,0:T(8,128)(2,1)}, u32[]{:S(2)}) copy-start(bf16[512,1280]{1,0:T(8,128)(2,1)} %refs_0_.1) | copy-start | bytes 3932164
  10.0 0.7 copy-start.3
  10.7 0.7 copy-start.4
  15.7 7.5 %collective-permute-start = (bf16[512,128]{1,0:T(8,128)(2,1)S(1)}, bf16[512,128]{1,0:T(8,128)(2,1)S(1)}, u32[]{:S(2)}, u32[]{:S(2)}) collective-permute-start(bf16[512,128]{1,0:T(8,128)(2,1)S(1)} %slice.8), channel_id=1, source_target_pairs={{0,16},{16,32},{32,48},{48,64},{64,80},{80,96},{96,112},{112,128},... | collective-permute-start | bytes 393224 | tf_op jit(solution)/shard_map/ppermute | solution.py:22
  23.2 14.0 %copy-start.2 = (bf16[512,1024]{1,0:T(8,128)(2,1)S(1)}, bf16[512,1024]{1,0:T(8,128)(2,1)}, u32[]{:S(2)}) copy-start(bf16[512,1024]{1,0:T(8,128)(2,1)} %w_gate_ref.1) | copy-start | bytes 3145732
  36.5 3.2 %collective-permute-start.1 = (bf16[128,128]{1,0:T(8,128)(2,1)S(1)}, bf16[128,128]{1,0:T(8,128)(2,1)S(1)}, u32[]{:S(2)}, u32[]{:S(2)}) collective-permute-start(bf16[128,128]{1,0:T(8,128)(2,1)S(1)} %slice.9), channel_id=1, source_target_pairs={{0,128},{16,144},{32,160},{48,176},{64,192},{80,208},{96,224},{112... | collective-permute-start | bytes 98312 | tf_op jit(solution)/shard_map/ppermute | solution.py:22
  37.2 35.0 %copy-start.1 = (bf16[1024,512]{1,0:T(8,128)(2,1)S(1)}, bf16[1024,512]{1,0:T(8,128)(2,1)}, u32[]{:S(2)}) copy-start(bf16[1024,512]{1,0:T(8,128)(2,1)} %w_out_ref.1) | copy-start | bytes 3145732
  39.8 0.7 collective-permute-start.2
  40.5 18.6 %collective-permute-start.3 = (bf16[128,128]{1,0:T(8,128)(2,1)S(1)}, bf16[128,128]{1,0:T(8,128)(2,1)S(1)}, u32[]{:S(2)}, u32[]{:S(2)}) collective-permute-start(bf16[128,128]{1,0:T(8,128)(2,1)S(1)} %shard_map.124), channel_id=1, source_target_pairs={{256,384},{272,400},{288,416},{304,432},{320,448},{336,464},{352,4... | collective-permute-start | bytes 98312 | tf_op jit(solution)/shard_map/ppermute | solution.py:22

commit v6 on v4

--- a/solution.py
+++ b/solution.py
@@ -203,8 +203,9 @@
 
 
 def join_kernel(own, total_ref, earlier_ref, send_ref):
-    size = send_ref.shape[0]
+    size = send_ref.shape[0] - EXTRA
     head_dim = size // own
+    send_ref[size:, :] = jnp.zeros((EXTRA, send_ref.shape[1]), bf16)
     jumps = read_logs(total_ref[size : size + EXTRA, :], own)
     for h in range(own):
         rows = slice(h * head_dim, (h + 1) * head_dim)
@@ -212,7 +213,7 @@
         send_ref[rows, :] = (total_ref[rows, :].astype(f32) + state).astype(bf16)
 
 
-def combine_kernel(own, states_ref, near_ref, far_a_ref, far_b_ref, back_ref):
+def combine_kernel(own, states_ref, near_ref, far_b_ref, far_a_ref, first_ref, back_ref):
     size = back_ref.shape[1]
     head_dim = size // own
     logs = [read_logs(states_ref[m, size : size + EXTRA, :], own) for m in range(GROUP)]
@@ -220,7 +221,8 @@
     for h in range(own):
         rows = slice(h * head_dim, (h + 1) * head_dim)
         far = far_a_ref[rows, :].astype(f32) + far_b_ref[rows, :].astype(f32)
-        state = near_ref[rows, :].astype(f32) + jnp.exp(jumps[h]) * far
+        close = first_ref[rows, :].astype(f32) + near_ref[rows, :].astype(f32)
+        state = close + jnp.exp(jumps[h]) * far
         for m in range(GROUP):
             back_ref[m, rows, :] = state.astype(bf16)
             state = jnp.exp(logs[m][h]) * state + states_ref[m, rows, :].astype(f32)
@@ -270,8 +272,7 @@
     normed = normed_ref[...]
     for at in range(0, inner, 256):
         gate = contract(weight_ref[:, at : at + 256], normed, ((0,), (0,)))
-        gate = gate.astype(bf16).astype(f32)
-        gate_ref[at : at + 256, :] = gate * jax.nn.sigmoid(gate)
+        gate_ref[at : at + 256, :] = gate.astype(bf16)
 
 
 def output_kernel(carried_ref, query_ref, cs_ref, y_ref, gate_ref, vec_ref, w_out_ref,
@@ -291,7 +292,8 @@
             rows = slice(h * head_dim, (h + 1) * head_dim)
             own = picked[h * head_dim - at : (h + 1) * head_dim - at, :]
             y = y_ref[rows, :] + grown[h : h + 1, :] * own
-            gated = y * gate_ref[rows, :]
+            gate = gate_ref[rows, :].astype(f32)
+            gated = y * (gate * jax.nn.sigmoid(gate))
             gated_ref[rows, :] = gated
             total = total + jnp.sum(gated * gated, axis=0, keepdims=True)
     scale = lax.rsqrt(total / inner + epsilon)
@@ -391,19 +393,20 @@
         states,
     )
     assert lax.axis_size("seq") == 4 * GROUP
-    near = passed_along(total, "seq", GROUP, members(0, 2))
+    first = passed_along(total, "seq", GROUP, members(0))
     joined = call(
         functools.partial(join_kernel, own),
-        shape((size, state_width), bf16),
+        shape((size + EXTRA, state_width), bf16),
         [],
-        total, near,
-    )
+        total, first,
+    )
+    joined, act = lax.optimization_barrier((joined, act))
+    far_a = passed_along(joined, "seq", GROUP, members(1))
     far_b = passed_along(joined, "seq", 2 * GROUP, members(1))
-    far_a = passed_along(joined, "seq", GROUP, members(1))
     gate, y, query = call(
         inside_kernel,
         [
-            shape((inner, length), f32),
+            shape((inner, length), bf16),
             shape((inner, length), f32),
             shape((state_width, length), bf16),
         ],
@@ -417,12 +420,13 @@
         normed, w_gate, act, act_first, dt, cs,
         fetched=(1,),
     )
-    gate, y, far_b, far_a = lax.optimization_barrier((gate, y, far_b, far_a))
+    total, gate, y = lax.optimization_barrier((total, gate, y))
+    near = passed_along(total, "seq", GROUP, members(2))
     back = call(
         functools.partial(combine_kernel, own),
         shape((GROUP, size, state_width), bf16),
         [],
-        states, near, far_a, far_b,
+        states, near, far_b, far_a, first,
     )
     carried = within_groups(back).reshape(inner, state_width)
     out = call(

time: 76.3 us -> 72.6 us (0.952)
  the two profiles are of different devices: /device:TPU:128 before, /device:TPU:1 now
where the time goes in v6:
time: 72.6 us; the launch traced here: 72 us
  blocking collectives  30.4 us (42%)
  starting transfers between devices  24 us (33%)
  Pallas kernels  9.09 us (13%)
  waiting for transfers between devices  4.03 us (6%)
  local copies, waits for them, and re-layouts  3.53 us (5%)
  other arithmetic  0.79 us (1%)
    all_to_all x2, blocking collectives, within_groups(): lax.all_to_all(blocks, 'seq', split_axis=0, concat_axis=0, tiled=True, ax...  30.4 us
    ppermute x5, starting transfers between devices, passed_along(): return lax.ppermute(block, axis, route)  16.3 us
    pallas_call x8, Pallas kernels, call(): pl.pallas_call(kernel, out_shape=outs, in_specs=[left if at in fetched el...  9.09 us
    all_to_all x1, starting transfers between devices, local(): lax.all_to_all(columns, 'table', split_axis=0, concat_axis=2, tiled=True)  7.72 us
    all_to_all x1, waiting for transfers between devices, local(): lax.all_to_all(columns, 'table', split_axis=0, concat_axis=2, tiled=True)  3 us
    unnamed x14, local copies, waits for them, and re-layouts  2.73 us
  transfers between devices with their start and end apart: 6, of which 2 were waited for; matrix products, arithmetic and copies ran while one was open for 2% of the time, Pallas kernels for 9%

profile of v6, /device:TPU:1, one launch (start us, length us, event | category | flops | bytes accessed | tf_op | source)
XLA Modules:
  0.0 72.0 jit_solution(10670953452342178008)
XLA Ops:
  0.0 0.0 copy-start.5
  0.0 0.0 copy-start.6
  0.0 7.7 %all-to-all-start = ((bf16[16,256,32]{1,2,0:T(8,128)(2,1)}), bf16[16,256,32]{1,2,0:T(8,128)(2,1)S(1)}, u32[]{:S(2)}, u32[]{:S(2)}) async-start(bf16[16,256,32]{1,2,0:T(8,128)(2,1)} %param.12), calls=%async_computation | async-start | bytes 524288 | tf_op jit(solution)/shard_map/all_to_all | solution.py:349
  7.7 0.7 broadcast_in_dim.12
  8.4 0.8 %select_maximum_fusion = f32[7,1280]{1,0:T(8,128)S(1)} fusion(f32[1,1024]{1,0:T(1,128)} %bitcast.19, f32[1,512]{1,0:T(1,128)} %bitcast.20, f32[1,1280]{1,0:T(1,128)S(1)} %broadcast_in_dim.12, f32[4,1280]{1,0:T(4,128)} %param.19), kind=kLoop, calls=%fused_computation.2 | loop fusion | flops 80640 | bytes 67584 | tf_op jit(solution)/shard_map/concatenate | solution.py:345
  9.2 0.0 copy-start
  9.2 1.3 %copy-done = bf16[512,1280]{1,0:T(8,128)(2,1)S(1)} copy-done((bf16[512,1280]{1,0:T(8,128)(2,1)S(1)}, bf16[512,1280]{1,0:T(8,128)(2,1)}, u32[]{:S(2)}) %copy-start) | copy-done | bytes 1310744
  10.6 0.0 copy-start.3
  10.6 0.7 copy-done.3
  11.3 0.0 copy-start.4
  11.3 0.7 copy-done.4
  11.9 0.1 shard_map.118
  12.1 0.0 copy-done.5
  12.1 0.0 copy-done.6
  12.1 3.0 %all-to-all-done = bf16[16,256,32]{1,2,0:T(8,128)(2,1)S(1)} async-done(((bf16[16,256,32]{1,2,0:T(8,128)(2,1)}), bf16[16,256,32]{1,2,0:T(8,128)(2,1)S(1)}, u32[]{:S(2)}, u32[]{:S(2)}) %all-to-all-start) | async-done | bytes 262176 | tf_op jit(solution)/shard_map/all_to_all | solution.py:349
  15.1 5.5 %collective-permute-start = (bf16[512,128]{1,0:T(8,128)(2,1)S(1)}, bf16[512,128]{1,0:T(8,128)(2,1)S(1)}, u32[]{:S(2)}, u32[]{:S(2)}) collective-permute-start(bf16[512,128]{1,0:T(8,128)(2,1)S(1)} %slice.4), channel_id=1, source_target_pairs={{0,16},{16,32},{32,48},{48,64},{64,80},{80,96},{96,112},{112,128},... | collective-permute-start | bytes 393224 | tf_op jit(solution)/shard_map/ppermute | solution.py:22
  20.6 0.1 copy.15.head_ref
  20.7 3.5 %shard_map.119 = (bf16[512,256]{1,0:T(8,128)(2,1)S(1)}, bf16[1280,256]{1,0:T(8,128)(2,1)S(1)}, f32[16,256]{1,0:T(8,128)S(1)}, f32[16,256]{1,0:T(8,128)S(1)}, f32...) custom-call(bf16[512,256]{1,0:T(8,128)(2,1)S(1)} %bitcast.16, ...), custom_call_target="tpu_custom_call" | custom-call | tf_op jit(solution)/shard_map/pallas_call | solution.py:311
  24.3 0.0 collective-permute-done.edge_ref
  24.3 0.0 copy-start.2
  24.3 0.7 %shard_map.120 = (bf16[8,136,128]{2,1,0:T(8,128)(2,1)S(1)}, f32[8,1280]{1,0:T(8,128)S(1)}) custom-call(bf16[512,128]{1,0:T(8,128)(2,1)S(1)} %collective-permute-done.edge_ref, f32[8,512]{1,0:T(8,128)S(1)} %get-tuple-element.41.first_ref, f32[8,1280]{1,0:T(8,128)S(1)} %pad.14.vec_ref, bf16[512,1280]{1,0:T(8,128)(2,1)S(1)} %get-tuple-element.37.w_xbc_ref, ...), custom_call_target="tpu_custom_call" | custom-call | tf_op jit(solution)/shard_map/pallas_call | solution.py:311
  25.1 16.6 %all_to_all.28.states_ref = bf16[8,136,128]{2,1,0:T(8,128)(2,1)S(1)} all-to-all(bf16[8,136,128]{2,1,0:T(8,128)(2,1)S(1)} %get-tuple-element.45), channel_id=1, replica_groups={{0,16,32,48,64,80,96,112},{128,144,160,176,192,208,224,240},{256,272,28..., dimensions={0} | all-to-all | bytes 557056 | tf_op jit(solution)/shard_map/all_to_all | solution.py:32
  41.7 0.1 shard_map.121.total_ref
  41.8 8.8 %collective-permute-start.1 = (bf16[136,128]{1,0:T(8,128)(2,1)S(1)}, bf16[136,128]{1,0:T(8,128)(2,1)S(1)}, u32[]{:S(2)}, u32[]{:S(2)}) collective-permute-start(bf16[136,128]{1,0:T(8,128)(2,1)S(1)} %shard_map.121.total_ref), channel_id=1, source_target_pairs={{0,128},{16,144},{32,160},{48,176},{64,192},{80,208},{96,224},{112... | collective-permute-start | bytes 104456 | tf_op jit(solution)/shard_map/ppermute | solution.py:22
  50.6 1.0 %collective-permute-done.1.earlier_ref.first_ref = bf16[136,128]{1,0:T(8,128)(2,1)S(1)} collective-permute-done((bf16[136,128]{1,0:T(8,128)(2,1)S(1)}, bf16[136,128]{1,0:T(8,128)(2,1)S(1)}, u32[]{:S(2)}, u32[]{:S(2)}) %collective-permute-start.1) | collective-permute-done | bytes 34848 | tf_op jit(solution)/shard_map/ppermute | solution.py:22
  51.6 0.7 collective-permute-start.4
  52.3 0.7 collective-permute-start.3
  53.0 0.0 copy-done.2
  53.0 0.0 copy-start.1
  53.0 2.5 %shard_map.123 = (bf16[1024,256]{1,0:T(8,128)(2,1)S(1)}, f32[1024,256]{1,0:T(8,128)S(1)}, bf16[128,256]{1,0:T(8,128)(2,1)S(1)}) custom-call(bf16[512,256]{1,0:T(8,128)(2,1)S(1)} %get-tuple-element.46.normed_ref, bf16[512,1024]{1,0:T(8,128)(2,1)S(1)} %copy-done.2, bf16[1280,256]{1,0:T(8,128)(2,1)S(1)} %get-tuple-element.48.main_ref, ...), custom_call_target="tpu_custom_call" | custom-call | tf_op jit(solution)/shard_map/pallas_call | solution.py:311
  55.5 0.7 collective-permute-start.2
  56.2 0.0 collective-permute-done.4.far_a_ref
  56.2 0.0 collective-permute-done.3.far_b_ref
  56.2 0.0 collective-permute-done.2.near_ref
  56.2 0.1 shard_map.124
  56.3 13.7 %all_to_all.29 = bf16[8,128,128]{2,1,0:T(8,128)(2,1)S(1)} all-to-all(bf16[8,128,128]{2,1,0:T(8,128)(2,1)S(1)} %shard_map.124), channel_id=1, replica_groups={{0,16,32,48,64,80,96,112},{128,144,160,176,192,208,224,240},{256,272,28..., dimensions={0} | all-to-all | bytes 524288 | tf_op jit(solution)/shard_map/all_to_all | solution.py:32
  70.1 0.0 copy-done.1
  70.1 1.9 %shard_map.125 = bf16[256,512]{1,0:T(8,128)(2,1)} custom-call(bf16[1024,128]{1,0:T(8,128)(2,1)S(1)} %bitcast.17, bf16[128,256]{1,0:T(8,128)(2,1)S(1)} %get-tuple-element.56.query_ref, f32[16,256]{1,0:T(8,128)S(1)} %get-tuple-element.51.cs_ref, f32[1024,256]{1,0:T(8,128)S(1)} %get-tuple-element.57.y_ref, bf16[1024,256]{1,0:T(8,128)(2,1)S(1)} %get-tuple-element.58.gate_ref, ...), custom_call_target="tpu_custom_call" | custom-call | tf_op jit(solution)/shard_map/pallas_call | solution.py:311
  (4 shorter events, 0.0 us)
Async XLA Ops:
  0.0 12.1 %copy-start.5 = (f32[16]{0:T(128)S(1)}, f32[16]{0:T(128)}, u32[]{:S(2)}) copy-start(f32[16]{0:T(128)} %param.21) | copy-start | bytes 196
  0.0 12.1 %copy-start.6 = (f32[16]{0:T(128)S(1)}, f32[16]{0:T(128)}, u32[]{:S(2)}) copy-start(f32[16]{0:T(128)} %param.18) | copy-start | bytes 196
  0.0 15.1 %all-to-all-start = ((bf16[16,256,32]{1,2,0:T(8,128)(2,1)}), bf16[16,256,32]{1,2,0:T(8,128)(2,1)S(1)}, u32[]{:S(2)}, u32[]{:S(2)}) async-start(bf16[16,256,32]{1,2,0:T(8,128)(2,1)} %param.12), calls=%async_computation | async-start | bytes 524288 | tf_op jit(solution)/shard_map/all_to_all | solution.py:349
  9.2 1.3 %copy-start = (bf16[512,1280]{1,0:T(8,128)(2,1)S(1)}, bf16[512,1280]{1,0:T(8,128)(2,1)}, u32[]{:S(2)}) copy-start(bf16[512,1280]{1,0:T(8,128)(2,1)} %refs_0_.1) | copy-start | bytes 3932164
  10.6 0.7 copy-start.3
  11.3 0.7 copy-start.4
  15.1 9.1 %collective-permute-start = (bf16[512,128]{1,0:T(8,128)(2,1)S(1)}, bf16[512,128]{1,0:T(8,128)(2,1)S(1)}, u32[]{:S(2)}, u32[]{:S(2)}) collective-permute-start(bf16[512,128]{1,0:T(8,128)(2,1)S(1)} %slice.4), channel_id=1, source_target_pairs={{0,16},{16,32},{32,48},{48,64},{64,80},{80,96},{96,112},{112,128},... | collective-permute-start | bytes 393224 | tf_op jit(solution)/shard_map/ppermute | solution.py:22
  24.3 28.7 %copy-start.2 = (bf16[512,1024]{1,0:T(8,128)(2,1)S(1)}, bf16[512,1024]{1,0:T(8,128)(2,1)}, u32[]{:S(2)}) copy-start(bf16[512,1024]{1,0:T(8,128)(2,1)} %w_gate_ref.1) | copy-start | bytes 3145732
  41.8 9.8 %collective-permute-start.1 = (bf16[136,128]{1,0:T(8,128)(2,1)S(1)}, bf16[136,128]{1,0:T(8,128)(2,1)S(1)}, u32[]{:S(2)}, u32[]{:S(2)}) collective-permute-start(bf16[136,128]{1,0:T(8,128)(2,1)S(1)} %shard_map.121.total_ref), channel_id=1, source_target_pairs={{0,128},{16,144},{32,160},{48,176},{64,192},{80,208},{96,224},{112... | collective-permute-start | bytes 104456 | tf_op jit(solution)/shard_map/ppermute | solution.py:22
  51.6 4.6 %collective-permute-start.4 = (bf16[136,128]{1,0:T(8,128)(2,1)S(1)}, bf16[136,128]{1,0:T(8,128)(2,1)S(1)}, u32[]{:S(2)}, u32[]{:S(2)}) collective-permute-start(bf16[136,128]{1,0:T(8,128)(2,1)S(1)} %shard_map.122), channel_id=1, source_target_pairs={{128,256},{144,272},{160,288},{176,304},{192,320},{208,336},{224,3... | collective-permute-start | bytes 104456 | tf_op jit(solution)/shard_map/ppermute | solution.py:22
  52.3 3.9 %collective-permute-start.3 = (bf16[136,128]{1,0:T(8,128)(2,1)S(1)}, bf16[136,128]{1,0:T(8,128)(2,1)S(1)}, u32[]{:S(2)}, u32[]{:S(2)}) collective-permute-start(bf16[136,128]{1,0:T(8,128)(2,1)S(1)} %shard_map.122), channel_id=1, source_target_pairs={{128,384},{144,400},{160,416},{176,432},{192,448},{208,464},{224,4... | collective-permute-start | bytes 104456 | tf_op jit(solution)/shard_map/ppermute | solution.py:22
  53.0 17.1 %copy-start.1 = (bf16[1024,512]{1,0:T(8,128)(2,1)S(1)}, bf16[1024,512]{1,0:T(8,128)(2,1)}, u32[]{:S(2)}) copy-start(bf16[1024,512]{1,0:T(8,128)(2,1)} %w_out_ref.1) | copy-start | bytes 3145732
  55.5 0.7 collective-permute-start.2

commit v7 on v6

--- a/solution.py
+++ b/solution.py
@@ -202,27 +202,32 @@
     send_ref[size : size + EXTRA, :] = rows_ref[...].astype(bf16)
 
 
-def join_kernel(own, total_ref, earlier_ref, send_ref):
+def join_kernel(own, total_ref, earlier_ref, send_ref, same_ref):
     size = send_ref.shape[0] - EXTRA
     head_dim = size // own
-    send_ref[size:, :] = jnp.zeros((EXTRA, send_ref.shape[1]), bf16)
-    jumps = read_logs(total_ref[size : size + EXTRA, :], own)
+    jumps = read_logs(total_ref[size:, :], own)
     for h in range(own):
         rows = slice(h * head_dim, (h + 1) * head_dim)
         state = jnp.exp(jumps[h]) * earlier_ref[rows, :].astype(f32)
         send_ref[rows, :] = (total_ref[rows, :].astype(f32) + state).astype(bf16)
-
-
-def combine_kernel(own, states_ref, near_ref, far_b_ref, far_a_ref, first_ref, back_ref):
+    send_ref[size:, :] = jnp.zeros((EXTRA, send_ref.shape[1]), bf16)
+    same_ref[...] = total_ref[...]
+
+
+def combine_kernel(own, states_ref, *refs):
+    *whole, near_ref, middle_ref, far_ref, back_ref = refs
     size = back_ref.shape[1]
     head_dim = size // own
     logs = [read_logs(states_ref[m, size : size + EXTRA, :], own) for m in range(GROUP)]
-    jumps = read_logs(near_ref[size : size + EXTRA, :], own)
+    near_jumps = read_logs(near_ref[size:, :], own)
+    middle_jumps = read_logs(middle_ref[size:, :], own)
     for h in range(own):
         rows = slice(h * head_dim, (h + 1) * head_dim)
-        far = far_a_ref[rows, :].astype(f32) + far_b_ref[rows, :].astype(f32)
-        close = first_ref[rows, :].astype(f32) + near_ref[rows, :].astype(f32)
-        state = close + jnp.exp(jumps[h]) * far
+        state = middle_ref[rows, :].astype(f32)
+        state = state + jnp.exp(middle_jumps[h]) * far_ref[rows, :].astype(f32)
+        state = near_ref[rows, :].astype(f32) + jnp.exp(near_jumps[h]) * state
+        for ref in whole:
+            state = state + ref[rows, :].astype(f32)
         for m in range(GROUP):
             back_ref[m, rows, :] = state.astype(bf16)
             state = jnp.exp(logs[m][h]) * state + states_ref[m, rows, :].astype(f32)
@@ -308,6 +313,10 @@
     vmem = pl.BlockSpec(memory_space=pltpu.VMEM)
     left = pl.BlockSpec(memory_space=pltpu.HBM)
     single = not isinstance(outs, list)
+    args = [
+        pltpu.with_memory_space_constraint(a, pltpu.HBM) if at in fetched else a
+        for at, a in enumerate(args)
+    ]
     return pl.pallas_call(
         kernel,
         out_shape=outs,
@@ -394,15 +403,24 @@
     )
     assert lax.axis_size("seq") == 4 * GROUP
     first = passed_along(total, "seq", GROUP, members(0))
-    joined = call(
+    middle = passed_along(total, "seq", 2 * GROUP, members(1))
+    far = passed_along(total, "seq", 3 * GROUP, members(0))
+    joined, same = call(
         functools.partial(join_kernel, own),
-        shape((size + EXTRA, state_width), bf16),
+        [shape((size + EXTRA, state_width), bf16)] * 2,
         [],
         total, first,
     )
-    joined, act = lax.optimization_barrier((joined, act))
-    far_a = passed_along(joined, "seq", GROUP, members(1))
-    far_b = passed_along(joined, "seq", 2 * GROUP, members(1))
+    after = passed_along(joined, "seq", GROUP, members(1))
+    near = passed_along(same, "seq", GROUP, members(2))
+    back = call(
+        functools.partial(combine_kernel, own),
+        shape((GROUP, size, state_width), bf16),
+        [],
+        states, first, after, near, middle, far,
+    )
+    back, act = lax.optimization_barrier((back, act))
+    carried = within_groups(back).reshape(inner, state_width)
     gate, y, query = call(
         inside_kernel,
         [
@@ -420,15 +438,6 @@
         normed, w_gate, act, act_first, dt, cs,
         fetched=(1,),
     )
-    total, gate, y = lax.optimization_barrier((total, gate, y))
-    near = passed_along(total, "seq", GROUP, members(2))
-    back = call(
-        functools.partial(combine_kernel, own),
-        shape((GROUP, size, state_width), bf16),
-        [],
-        states, near, far_b, far_a, first,
-    )
-    carried = within_groups(back).reshape(inner, state_width)
     out = call(
         output_kernel,
         shape((length, w_out.shape[1]), bf16),

time: 72.6 us -> 71.9 us (level)
  blocking collectives: 30.4 us -> 16.6 us
  starting transfers between devices: 24 us -> 30.2 us
  waiting for transfers between devices: 4.03 us -> 9.76 us
  Pallas kernels: 9.09 us -> 13 us
  local copies, waits for them, and re-layouts: 3.53 us -> 0.81 us
    all_to_all x2 -> x1, blocking collectives: 30.4 us -> 16.6 us  [within_groups(): lax.all_to_all(blocks, 'seq', split_axis=0, concat_axis=0, tiled=True, ax...]
    all_to_all x0 -> x1, waiting for transfers between devices: none -> 5.24 us  [within_groups(): lax.all_to_all(blocks, 'seq', split_axis=0, concat_axis=0, tiled=True, ax...]
    all_to_all x0 -> x1, starting transfers between devices: none -> 4.86 us  [within_groups(): lax.all_to_all(blocks, 'seq', split_axis=0, concat_axis=0, tiled=True, ax...]
    pallas_call x8, Pallas kernels: 9.09 us -> 13 us  [call(): pl.pallas_call(kernel, out_shape=outs, in_specs=[left if at in fetched el...]
    unnamed x14 -> x4, local copies, waits for them, and re-layouts: 2.73 us -> 0.01 us
    all_to_all x1, waiting for transfers between devices: 3 us -> 4.5 us  [local(): lax.all_to_all(columns, 'table', split_axis=0, concat_axis=2, tiled=True)]
    ppermute x5 -> x6, starting transfers between devices: 16.3 us -> 17.6 us  [passed_along(): return lax.ppermute(block, axis, route)]
    ppermute x5 -> x6, waiting for transfers between devices: 1.03 us -> 0.02 us  [passed_along(): return lax.ppermute(block, axis, route)]
  transfers between devices with their start and end apart: 6 -> 8, of which waited for: 2 -> 2; matrix products, arithmetic and copies ran while one was open for 2% -> 2% of each run, Pallas kernels for 9% -> 12%
where the time goes in v7:
time: 71.9 us; the launch traced here: 71.3 us
  starting transfers between devices  30.2 us (42%)
  blocking collectives  16.6 us (23%)
  Pallas kernels  13 us (18%)
  waiting for transfers between devices  9.76 us (14%)
  local copies, waits for them, and re-layouts  0.81 us (1%)
  other arithmetic  0.79 us (1%)
    ppermute x6, starting transfers between devices, passed_along(): return lax.ppermute(block, axis, route)  17.6 us
    all_to_all x1, blocking collectives, within_groups(): lax.all_to_all(blocks, 'seq', split_axis=0, concat_axis=0, tiled=True, ax...  16.6 us
    pallas_call x8, Pallas kernels, call(): pl.pallas_call(kernel, out_shape=outs, in_specs=[left if at in fetched el...  13 us
    all_to_all x1, starting transfers between devices, local(): lax.all_to_all(columns, 'table', split_axis=0, concat_axis=2, tiled=True)  7.72 us
    all_to_all x1, waiting for transfers between devices, within_groups(): lax.all_to_all(blocks, 'seq', split_axis=0, concat_axis=0, tiled=True, ax...  5.24 us
    all_to_all x1, starting transfers between devices, within_groups(): lax.all_to_all(blocks, 'seq', split_axis=0, concat_axis=0, tiled=True, ax...  4.86 us
    all_to_all x1, waiting for transfers between devices, local(): lax.all_to_all(columns, 'table', split_axis=0, concat_axis=2, tiled=True)  4.5 us
  transfers between devices with their start and end apart: 8, of which 2 were waited for; matrix products, arithmetic and copies ran while one was open for 2% of the time, Pallas kernels for 12%

profile of v7, /device:TPU:1, one launch (start us, length us, event | category | flops | bytes accessed | tf_op | source)
XLA Modules:
  0.0 71.3 jit_solution(10282568734542874605)
XLA Ops:
  0.0 0.0 copy-start
  0.0 0.0 copy-start.1
  0.0 7.7 %all-to-all-start = ((bf16[16,256,32]{1,2,0:T(8,128)(2,1)}), bf16[16,256,32]{1,2,0:T(8,128)(2,1)S(1)}, u32[]{:S(2)}, u32[]{:S(2)}) async-start(bf16[16,256,32]{1,2,0:T(8,128)(2,1)} %param.12), calls=%async_computation | async-start | bytes 524288 | tf_op jit(solution)/shard_map/all_to_all | solution.py:358
  7.7 0.7 broadcast_in_dim.12
  8.4 0.8 %select_maximum_fusion = f32[7,1280]{1,0:T(8,128)S(1)} fusion(f32[1,1024]{1,0:T(1,128)} %bitcast.19, f32[1,512]{1,0:T(1,128)} %bitcast.20, f32[1,1280]{1,0:T(1,128)S(1)} %broadcast_in_dim.12, f32[4,1280]{1,0:T(4,128)} %param.19), kind=kLoop, calls=%fused_computation.2 | loop fusion | flops 80640 | bytes 67584 | tf_op jit(solution)/shard_map/concatenate | solution.py:354
  9.2 1.4 %shard_map.118 = (bf16[512,1280]{1,0:T(8,128)(2,1)S(1)}, bf16[16,512]{1,0:T(8,128)(2,1)S(1)}, f32[1,256]{1,0:T(1,128)S(1)}) custom-call(bf16[512,1280]{1,0:T(8,128)(2,1)} %refs_0_.1, bf16[16,512]{1,0:T(8,128)(2,1)} %bitcast.18, f32[1,256]{1,0:T(1,128)} %refs_2_.1), custom_call_target="tpu_custom_call" | custom-call | tf_op jit(solution)/shard_map/pallas_call | solution.py:320
  10.6 0.0 copy-done
  10.6 0.0 copy-done.1
  10.6 4.5 %all-to-all-done = bf16[16,256,32]{1,2,0:T(8,128)(2,1)S(1)} async-done(((bf16[16,256,32]{1,2,0:T(8,128)(2,1)}), bf16[16,256,32]{1,2,0:T(8,128)(2,1)S(1)}, u32[]{:S(2)}, u32[]{:S(2)}) %all-to-all-start) | async-done | bytes 262176 | tf_op jit(solution)/shard_map/all_to_all | solution.py:358
  15.1 5.5 %collective-permute-start = (bf16[512,128]{1,0:T(8,128)(2,1)S(1)}, bf16[512,128]{1,0:T(8,128)(2,1)S(1)}, u32[]{:S(2)}, u32[]{:S(2)}) collective-permute-start(bf16[512,128]{1,0:T(8,128)(2,1)S(1)} %slice.4), channel_id=1, source_target_pairs={{0,16},{16,32},{32,48},{48,64},{64,80},{80,96},{96,112},{112,128},... | collective-permute-start | bytes 393224 | tf_op jit(solution)/shard_map/ppermute | solution.py:22
  20.6 0.1 copy.15.head_ref
  20.7 3.5 %shard_map.119 = (bf16[512,256]{1,0:T(8,128)(2,1)S(1)}, bf16[1280,256]{1,0:T(8,128)(2,1)S(1)}, f32[16,256]{1,0:T(8,128)S(1)}, f32[16,256]{1,0:T(8,128)S(1)}, f32...) custom-call(bf16[512,256]{1,0:T(8,128)(2,1)S(1)} %bitcast.16, ...), custom_call_target="tpu_custom_call" | custom-call | tf_op jit(solution)/shard_map/pallas_call | solution.py:320
  24.3 0.0 collective-permute-done.edge_ref
  24.3 0.7 %shard_map.120 = (bf16[8,136,128]{2,1,0:T(8,128)(2,1)S(1)}, f32[8,1280]{1,0:T(8,128)S(1)}) custom-call(bf16[512,128]{1,0:T(8,128)(2,1)S(1)} %collective-permute-done.edge_ref, f32[8,512]{1,0:T(8,128)S(1)} %get-tuple-element.40.first_ref, f32[8,1280]{1,0:T(8,128)S(1)} %pad.14.vec_ref, bf16[512,1280]{1,0:T(8,128)(2,1)S(1)} %get-tuple-element.36.w_xbc_ref, ...), custom_call_target="tpu_custom_call" | custom-call | tf_op jit(solution)/shard_map/pallas_call | solution.py:320
  25.0 16.6 %all_to_all.28.states_ref = bf16[8,136,128]{2,1,0:T(8,128)(2,1)S(1)} all-to-all(bf16[8,136,128]{2,1,0:T(8,128)(2,1)S(1)} %get-tuple-element.44), channel_id=1, replica_groups={{0,16,32,48,64,80,96,112},{128,144,160,176,192,208,224,240},{256,272,28..., dimensions={0} | all-to-all | bytes 557056 | tf_op jit(solution)/shard_map/all_to_all | solution.py:32
  41.7 0.1 shard_map.121.total_ref
  41.8 8.8 %collective-permute-start.1 = (bf16[136,128]{1,0:T(8,128)(2,1)S(1)}, bf16[136,128]{1,0:T(8,128)(2,1)S(1)}, u32[]{:S(2)}, u32[]{:S(2)}) collective-permute-start(bf16[136,128]{1,0:T(8,128)(2,1)S(1)} %shard_map.121.total_ref), channel_id=1, source_target_pairs={{0,128},{16,144},{32,160},{48,176},{64,192},{80,208},{96,224},{112... | collective-permute-start | bytes 104456 | tf_op jit(solution)/shard_map/ppermute | solution.py:22
  50.6 1.3 %collective-permute-start.5 = (bf16[136,128]{1,0:T(8,128)(2,1)S(1)}, bf16[136,128]{1,0:T(8,128)(2,1)S(1)}, u32[]{:S(2)}, u32[]{:S(2)}) collective-permute-start(bf16[136,128]{1,0:T(8,128)(2,1)S(1)} %shard_map.121.total_ref), channel_id=1, source_target_pairs={{0,384},{16,400},{32,416},{48,432},{64,448},{80,464},{96,480},{112... | collective-permute-start | bytes 104456 | tf_op jit(solution)/shard_map/ppermute | solution.py:22
  51.9 0.7 collective-permute-start.4
  52.6 0.0 collective-permute-done.1.earlier_ref.refs_0_
  52.6 0.7 collective-permute-start.2
  53.3 0.7 collective-permute-start.3
  53.9 0.0 collective-permute-done.5.refs_4_
  53.9 0.0 collective-permute-done.4.refs_3_
  54.0 0.0 collective-permute-done.2.refs_1_
  54.0 0.0 collective-permute-done.3.refs_2_
  54.0 0.8 %shard_map.123 = bf16[8,128,128]{2,1,0:T(8,128)(2,1)} custom-call(bf16[8,136,128]{2,1,0:T(8,128)(2,1)S(1)} %all_to_all.28.states_ref, bf16[136,128]{1,0:T(8,128)(2,1)S(1)} %collective-permute-done.1.earlier_ref.refs_0_, bf16[136,128]{1,0:T(8,128)(2,1)S(1)} %collective-permute-done.2.refs_1_, bf16[136,128]{1,0:T(8,128)(2,1)S(1)} %collective-permute-done.3.refs_2_, ...), custom_call_target="tpu_custom_call" | custom-call | tf_op jit(solution)/shard_map/pallas_call | solution.py:320
  54.8 4.9 %all-to-all-start.2 = ((bf16[8,128,128]{2,1,0:T(8,128)(2,1)}), bf16[8,128,128]{2,1,0:T(8,128)(2,1)S(1)}, u32[]{:S(2)}, u32[]{:S(2)}) async-start(bf16[8,128,128]{2,1,0:T(8,128)(2,1)} %shard_map.123), calls=%async_computation.2 | async-start | bytes 524288 | tf_op jit(solution)/shard_map/all_to_all | solution.py:32
  59.6 3.5 %shard_map.124 = (bf16[1024,256]{1,0:T(8,128)(2,1)S(1)}, f32[1024,256]{1,0:T(8,128)S(1)}, bf16[128,256]{1,0:T(8,128)(2,1)S(1)}) custom-call(bf16[512,256]{1,0:T(8,128)(2,1)S(1)} %get-tuple-element.49.normed_ref, bf16[512,1024]{1,0:T(8,128)(2,1)} %w_gate_ref.1, bf16[1280,256]{1,0:T(8,128)(2,1)S(1)} %get-tuple-element.50.main_ref, ...), custom_call_target="tpu_custom_call" | custom-call | tf_op jit(solution)/shard_map/pallas_call | solution.py:320
  63.1 5.2 %all-to-all-done.2 = bf16[8,128,128]{2,1,0:T(8,128)(2,1)S(1)} async-done(((bf16[8,128,128]{2,1,0:T(8,128)(2,1)}), bf16[8,128,128]{2,1,0:T(8,128)(2,1)S(1)}, u32[]{:S(2)}, u32[]{:S(2)}) %all-to-all-start.2) | async-done | bytes 262176 | tf_op jit(solution)/shard_map/all_to_all | solution.py:32
  68.4 3.0 %shard_map.125 = bf16[256,512]{1,0:T(8,128)(2,1)} custom-call(bf16[1024,128]{1,0:T(8,128)(2,1)S(1)} %bitcast.17, bf16[128,256]{1,0:T(8,128)(2,1)S(1)} %get-tuple-element.54.query_ref, f32[16,256]{1,0:T(8,128)S(1)} %get-tuple-element.53.cs_ref, f32[1024,256]{1,0:T(8,128)S(1)} %get-tuple-element.55.y_ref, bf16[1024,256]{1,0:T(8,128)(2,1)S(1)} %get-tuple-element.56.gate_ref, ...), custom_call_target="tpu_custom_call" | custom-call | tf_op jit(solution)/shard_map/pallas_call | solution.py:320
  (4 shorter events, 0.0 us)
Async XLA Ops:
  0.0 10.6 %copy-start = (f32[16]{0:T(128)S(1)}, f32[16]{0:T(128)}, u32[]{:S(2)}) copy-start(f32[16]{0:T(128)} %param.21) | copy-start | bytes 196
  0.0 10.6 %copy-start.1 = (f32[16]{0:T(128)S(1)}, f32[16]{0:T(128)}, u32[]{:S(2)}) copy-start(f32[16]{0:T(128)} %param.18) | copy-start | bytes 196
  0.0 15.1 %all-to-all-start = ((bf16[16,256,32]{1,2,0:T(8,128)(2,1)}), bf16[16,256,32]{1,2,0:T(8,128)(2,1)S(1)}, u32[]{:S(2)}, u32[]{:S(2)}) async-start(bf16[16,256,32]{1,2,0:T(8,128)(2,1)} %param.12), calls=%async_computation | async-start | bytes 524288 | tf_op jit(solution)/shard_map/all_to_all | solution.py:358
  15.1 9.1 %collective-permute-start = (bf16[512,128]{1,0:T(8,128)(2,1)S(1)}, bf16[512,128]{1,0:T(8,128)(2,1)S(1)}, u32[]{:S(2)}, u32[]{:S(2)}) collective-permute-start(bf16[512,128]{1,0:T(8,128)(2,1)S(1)} %slice.4), channel_id=1, source_target_pairs={{0,16},{16,32},{32,48},{48,64},{64,80},{80,96},{96,112},{112,128},... | collective-permute-start | bytes 393224 | tf_op jit(solution)/shard_map/ppermute | solution.py:22
  41.8 10.8 %collective-permute-start.1 = (bf16[136,128]{1,0:T(8,128)(2,1)S(1)}, bf16[136,128]{1,0:T(8,128)(2,1)S(1)}, u32[]{:S(2)}, u32[]{:S(2)}) collective-permute-start(bf16[136,128]{1,0:T(8,128)(2,1)S(1)} %shard_map.121.total_ref), channel_id=1, source_target_pairs={{0,128},{16,144},{32,160},{48,176},{64,192},{80,208},{96,224},{112... | collective-permute-start | bytes 104456 | tf_op jit(solution)/shard_map/ppermute | solution.py:22
  50.6 3.4 %collective-permute-start.5 = (bf16[136,128]{1,0:T(8,128)(2,1)S(1)}, bf16[136,128]{1,0:T(8,128)(2,1)S(1)}, u32[]{:S(2)}, u32[]{:S(2)}) collective-permute-start(bf16[136,128]{1,0:T(8,128)(2,1)S(1)} %shard_map.121.total_ref), channel_id=1, source_target_pairs={{0,384},{16,400},{32,416},{48,432},{64,448},{80,464},{96,480},{112... | collective-permute-start | bytes 104456 | tf_op jit(solution)/shard_map/ppermute | solution.py:22
  51.9 2.1 %collective-permute-start.4 = (bf16[136,128]{1,0:T(8,128)(2,1)S(1)}, bf16[136,128]{1,0:T(8,128)(2,1)S(1)}, u32[]{:S(2)}, u32[]{:S(2)}) collective-permute-start(bf16[136,128]{1,0:T(8,128)(2,1)S(1)} %shard_map.121.total_ref), channel_id=1, source_target_pairs={{128,384},{144,400},{160,416},{176,432},{192,448},{208,464},{224,4... | collective-permute-start | bytes 104456 | tf_op jit(solution)/shard_map/ppermute | solution.py:22
  52.6 1.4 %collective-permute-start.2 = (bf16[136,128]{1,0:T(8,128)(2,1)S(1)}, bf16[136,128]{1,0:T(8,128)(2,1)S(1)}, u32[]{:S(2)}, u32[]{:S(2)}) collective-permute-start(bf16[136,128]{1,0:T(8,128)(2,1)S(1)} %get-tuple-element.45), channel_id=1, source_target_pairs={{128,256},{144,272},{160,288},{176,304},{192,320},{208,336},{224,3... | collective-permute-start | bytes 104456 | tf_op jit(solution)/shard_map/ppermute | solution.py:22
  53.3 0.7 collective-permute-start.3
  54.8 13.6 %all-to-all-start.2 = ((bf16[8,128,128]{2,1,0:T(8,128)(2,1)}), bf16[8,128,128]{2,1,0:T(8,128)(2,1)S(1)}, u32[]{:S(2)}, u32[]{:S(2)}) async-start(bf16[8,128,128]{2,1,0:T(8,128)(2,1)} %shard_map.123), calls=%async_computation.2 | async-start | bytes 524288 | tf_op jit(solution)/shard_map/all_to_all | solution.py:32

commit v8 on v7

--- a/solution.py
+++ b/solution.py
@@ -10,6 +10,7 @@
 GROUP = 8
 EDGE = 128
 EXTRA = 8
+PARTS = 4
 BIAS, GAIN_IN, GAIN_OUT = 4, 5, 6
 epsilon = 1e-05
 f32 = jnp.float32
@@ -32,6 +33,20 @@
     return lax.all_to_all(
         blocks, "seq", split_axis=0, concat_axis=0, tiled=True, axis_index_groups=groups
     )
+
+
+def fetch_rows(source, target, sems):
+    count = sems.shape[0]
+    step = source.shape[0] // count
+    copies = [
+        pltpu.make_async_copy(
+            source.at[at * step : (at + 1) * step], target.at[at * step : (at + 1) * step], sems.at[at]
+        )
+        for at in range(count)
+    ]
+    for copy in copies:
+        copy.start()
+    return copies
 
 
 def contract(a, b, dims):
@@ -85,7 +100,6 @@
     inner, state_width = state_ref.shape
     head_dim = inner // heads
     normed_columns(x_ref, vec_ref, normed_ref)
-    first_ref[...] = x_ref[:, 0:EDGE].astype(f32).T[0:EXTRA, :]
     normed = normed_ref[...]
     raw = jnp.dot(w_step_ref[...], normed, preferred_element_type=f32)
     raw = raw + head_ref[:, 0:1]
@@ -133,18 +147,19 @@
             axis=0,
         )
         state_ref[at : at + step, :] = contract((act * coef).astype(bf16), b, ((1,), (1,)))
+    first_ref[...] = shift_ref[EXTRA : 2 * EXTRA, :]
 
 
 def edge_kernel(edge_ref, first_ref, vec_ref, w_xbc_ref, coef_ref, state_ref, logs_ref,
                 send_ref, act_ref, rows_ref):
     inner, state_width = state_ref.shape
-    depth = first_ref.shape[1]
-    before = edge_ref[...].astype(f32).T[EDGE - EXTRA :, :]
-    x = jnp.concatenate([before, first_ref[...]], axis=0)
+    depth = edge_ref.shape[0]
+    x = edge_ref[...].astype(f32).T[EDGE - EXTRA :, :]
     scale = lax.rsqrt(jnp.mean(x * x, axis=1, keepdims=True) + epsilon)
     normed = (x * scale * vec_ref[GAIN_IN : GAIN_IN + 1, :depth]).astype(bf16)
-    whole = jnp.dot(normed, w_xbc_ref[...], preferred_element_type=f32)
-    rows_ref[...] = whole.astype(bf16).astype(f32)
+    before = jnp.dot(normed, w_xbc_ref[...], preferred_element_type=f32)
+    rows_ref[0:EXTRA, :] = before.astype(bf16).astype(f32)
+    rows_ref[EXTRA:, :] = first_ref[...]
     conv = vec_ref[BIAS : BIAS + 1, :]
     for tap in range(BIAS):
         at = EXTRA - (BIAS - 1 - tap)
@@ -234,11 +249,10 @@
 
 
 def inside_kernel(normed_ref, w_gate_ref, main_ref, first_ref, dt_ref, cs_ref,
-                  gate_ref, y_ref, query_ref, act_ref, scores_ref, mix_ref, weight_ref, sem):
-    fetch = pltpu.make_async_copy(w_gate_ref, weight_ref, sem)
-    fetch.start()
+                  grown_ref, y_ref, query_ref, act_ref, scores_ref, mix_ref, weight_ref, sem):
+    fetches = fetch_rows(w_gate_ref, weight_ref, sem)
     heads, length = dt_ref.shape
-    inner = gate_ref.shape[0]
+    inner = y_ref.shape[0]
     lane = lax.broadcasted_iota(jnp.int32, (EDGE, EDGE), 1)
     rest = jnp.zeros((EDGE - EXTRA, EDGE), f32)
     for at in range(0, act_ref.shape[0], EDGE):
@@ -273,39 +287,39 @@
                 ).astype(bf16)
         rows = slice(h * head_dim, (h + 1) * head_dim)
         y_ref[rows, :] = jnp.dot(act_ref[rows, :], mix_ref[...], preferred_element_type=f32)
-    fetch.wait()
+    for fetch in fetches:
+        fetch.wait()
     normed = normed_ref[...]
-    for at in range(0, inner, 256):
-        gate = contract(weight_ref[:, at : at + 256], normed, ((0,), (0,)))
-        gate_ref[at : at + 256, :] = gate.astype(bf16)
-
-
-def output_kernel(carried_ref, query_ref, cs_ref, y_ref, gate_ref, vec_ref, w_out_ref,
-                  out_ref, gated_ref, normed_ref, weight_ref, sem):
-    fetch = pltpu.make_async_copy(w_out_ref, weight_ref, sem)
-    fetch.start()
-    heads, length = cs_ref.shape
-    inner = y_ref.shape[0]
-    head_dim = inner // heads
-    queries = query_ref[...]
-    grown = jnp.exp(cs_ref[...])
-    total = jnp.zeros((1, length), f32)
-    step = 2 * head_dim
+    step = 4 * head_dim
     for at in range(0, inner, step):
-        picked = jnp.dot(carried_ref[at : at + step, :], queries, preferred_element_type=f32)
+        gate = contract(weight_ref[:, at : at + step], normed, ((0,), (0,)))
+        gate = gate.astype(bf16).astype(f32)
+        gate = gate * jax.nn.sigmoid(gate)
         for h in range(at // head_dim, (at + step) // head_dim):
             rows = slice(h * head_dim, (h + 1) * head_dim)
-            own = picked[h * head_dim - at : (h + 1) * head_dim - at, :]
-            y = y_ref[rows, :] + grown[h : h + 1, :] * own
-            gate = gate_ref[rows, :].astype(f32)
-            gated = y * (gate * jax.nn.sigmoid(gate))
-            gated_ref[rows, :] = gated
-            total = total + jnp.sum(gated * gated, axis=0, keepdims=True)
+            own = gate[h * head_dim - at : (h + 1) * head_dim - at, :]
+            grown_ref[rows, :] = jnp.exp(cs_ref[h : h + 1, :]) * own
+            y_ref[rows, :] = y_ref[rows, :] * own
+
+
+def output_kernel(carried_ref, query_ref, grown_ref, y_ref, vec_ref, w_out_ref,
+                  out_ref, gated_ref, normed_ref, weight_ref, sem):
+    fetches = fetch_rows(w_out_ref, weight_ref, sem)
+    inner, length = y_ref.shape
+    queries = query_ref[...]
+    total = jnp.zeros((1, length), f32)
+    for at in range(0, inner, EDGE):
+        rows = slice(at, at + EDGE)
+        picked = jnp.dot(carried_ref[rows, :], queries, preferred_element_type=f32)
+        gated = y_ref[rows, :] + grown_ref[rows, :] * picked
+        gated_ref[rows, :] = gated
+        total = total + jnp.sum(gated * gated, axis=0, keepdims=True)
     scale = lax.rsqrt(total / inner + epsilon)
     for at in range(0, inner, EDGE):
         gain = columns_of(vec_ref, at)[:, GAIN_OUT : GAIN_OUT + 1]
         normed_ref[at : at + EDGE, :] = (gated_ref[at : at + EDGE, :] * scale * gain).astype(bf16)
-    fetch.wait()
+    for fetch in fetches:
+        fetch.wait()
     out_ref[...] = contract(normed_ref[...], weight_ref[...], ((0,), (0,))).astype(bf16)
 
 
@@ -377,7 +391,7 @@
             shape((heads, length), f32),
             shape((inner, state_width), f32),
             shape((GROUP * EXTRA, state_width), bf16),
-            shape((EXTRA, depth), f32),
+            shape((EXTRA, width), f32),
             shape((EXTRA, inner), f32),
         ],
         [
@@ -421,10 +435,10 @@
     )
     back, act = lax.optimization_barrier((back, act))
     carried = within_groups(back).reshape(inner, state_width)
-    gate, y, query = call(
+    grown, y, query = call(
         inside_kernel,
         [
-            shape((inner, length), bf16),
+            shape((inner, length), f32),
             shape((inner, length), f32),
             shape((state_width, length), bf16),
         ],
@@ -433,7 +447,7 @@
             pltpu.VMEM((length, length), f32),
             pltpu.VMEM((length, length), bf16),
             pltpu.VMEM((depth, inner), bf16),
-            pltpu.SemaphoreType.DMA,
+            pltpu.SemaphoreType.DMA((PARTS,)),
         ],
         normed, w_gate, act, act_first, dt, cs,
         fetched=(1,),
@@ -445,10 +459,10 @@
             pltpu.VMEM((inner, length), f32),
             pltpu.VMEM((inner, length), bf16),
             pltpu.VMEM(w_out.shape, bf16),
-            pltpu.SemaphoreType.DMA,
+            pltpu.SemaphoreType.DMA((PARTS,)),
         ],
-        carried, query, cs, y, gate, vec, w_out,
-        fetched=(6,),
+        carried, query, grown, y, vec, w_out,
+        fetched=(5,),
     )
     return out[None]
 

time: 71.9 us -> 71.4 us (level)
  Pallas kernels: 13 us -> 11.6 us
  waiting for transfers between devices: 9.76 us -> 10.7 us
    pallas_call x8, Pallas kernels: 13 us -> 11.6 us  [call(): pl.pallas_call(kernel, out_shape=outs, in_specs=[left if at in fetched el...]
    all_to_all x1, waiting for transfers between devices: 5.24 us -> 6.17 us  [within_groups(): lax.all_to_all(blocks, 'seq', split_axis=0, concat_axis=0, tiled=True, ax...]
  transfers between devices with their start and end apart: 8 -> 8, of which waited for: 2 -> 2; matrix products, arithmetic and copies ran while one was open for 2% -> 2% of each run, Pallas kernels for 12% -> 11%
where the time goes in v8:
time: 71.4 us; the launch traced here: 70.9 us
  starting transfers between devices  30.2 us (42%)
  blocking collectives  16.6 us (23%)
  Pallas kernels  11.6 us (16%)
  waiting for transfers between devices  10.7 us (15%)
  local copies, waits for them, and re-layouts  0.81 us (1%)
  other arithmetic  0.79 us (1%)
    ppermute x6, starting transfers between devices, passed_along(): return lax.ppermute(block, axis, route)  17.6 us
    all_to_all x1, blocking collectives, within_groups(): lax.all_to_all(blocks, 'seq', split_axis=0, concat_axis=0, tiled=True, ax...  16.6 us
    pallas_call x8, Pallas kernels, call(): pl.pallas_call(kernel, out_shape=outs, in_specs=[left if at in fetched el...  11.6 us
    all_to_all x1, starting transfers between devices, local(): lax.all_to_all(columns, 'table', split_axis=0, concat_axis=2, tiled=True)  7.72 us
    all_to_all x1, waiting for transfers between devices, within_groups(): lax.all_to_all(blocks, 'seq', split_axis=0, concat_axis=0, tiled=True, ax...  6.17 us
    all_to_all x1, starting transfers between devices, within_groups(): lax.all_to_all(blocks, 'seq', split_axis=0, concat_axis=0, tiled=True, ax...  4.86 us
    all_to_all x1, waiting for transfers between devices, local(): lax.all_to_all(columns, 'table', split_axis=0, concat_axis=2, tiled=True)  4.5 us
  transfers between devices with their start and end apart: 8, of which 2 were waited for; matrix products, arithmetic and copies ran while one was open for 2% of the time, Pallas kernels for 11%

profile of v8, /device:TPU:1, one launch (start us, length us, event | category | flops | bytes accessed | tf_op | source)
XLA Modules:
  0.0 70.9 jit_solution(2992907679817323122)
XLA Ops:
  0.0 0.0 copy-start
  0.0 0.0 copy-start.1
  0.0 7.7 %all-to-all-start = ((bf16[16,256,32]{1,2,0:T(8,128)(2,1)}), bf16[16,256,32]{1,2,0:T(8,128)(2,1)S(1)}, u32[]{:S(2)}, u32[]{:S(2)}) async-start(bf16[16,256,32]{1,2,0:T(8,128)(2,1)} %param.12), calls=%async_computation | async-start | bytes 524288 | tf_op jit(solution)/shard_map/all_to_all | solution.py:372
  7.7 0.7 broadcast_in_dim.12
  8.4 0.8 %select_maximum_fusion = f32[7,1280]{1,0:T(8,128)S(1)} fusion(f32[1,1024]{1,0:T(1,128)} %bitcast.19, f32[1,512]{1,0:T(1,128)} %bitcast.20, f32[1,1280]{1,0:T(1,128)S(1)} %broadcast_in_dim.12, f32[4,1280]{1,0:T(4,128)} %param.19), kind=kLoop, calls=%fused_computation.2 | loop fusion | flops 80640 | bytes 67584 | tf_op jit(solution)/shard_map/concatenate | solution.py:368
  9.2 1.4 %shard_map.118 = (bf16[512,1280]{1,0:T(8,128)(2,1)S(1)}, bf16[16,512]{1,0:T(8,128)(2,1)S(1)}, f32[1,256]{1,0:T(1,128)S(1)}) custom-call(bf16[512,1280]{1,0:T(8,128)(2,1)} %refs_0_.1, bf16[16,512]{1,0:T(8,128)(2,1)} %bitcast.18, f32[1,256]{1,0:T(1,128)} %refs_2_.1), custom_call_target="tpu_custom_call" | custom-call | tf_op jit(solution)/shard_map/pallas_call | solution.py:334
  10.6 0.0 copy-done
  10.6 0.0 copy-done.1
  10.6 4.5 %all-to-all-done = bf16[16,256,32]{1,2,0:T(8,128)(2,1)S(1)} async-done(((bf16[16,256,32]{1,2,0:T(8,128)(2,1)}), bf16[16,256,32]{1,2,0:T(8,128)(2,1)S(1)}, u32[]{:S(2)}, u32[]{:S(2)}) %all-to-all-start) | async-done | bytes 262176 | tf_op jit(solution)/shard_map/all_to_all | solution.py:372
  15.1 5.5 %collective-permute-start = (bf16[512,128]{1,0:T(8,128)(2,1)S(1)}, bf16[512,128]{1,0:T(8,128)(2,1)S(1)}, u32[]{:S(2)}, u32[]{:S(2)}) collective-permute-start(bf16[512,128]{1,0:T(8,128)(2,1)S(1)} %slice.4), channel_id=1, source_target_pairs={{0,16},{16,32},{32,48},{48,64},{64,80},{80,96},{96,112},{112,128},... | collective-permute-start | bytes 393224 | tf_op jit(solution)/shard_map/ppermute | solution.py:23
  20.6 0.1 copy.15.head_ref
  20.7 3.5 %shard_map.119 = (bf16[512,256]{1,0:T(8,128)(2,1)S(1)}, bf16[1280,256]{1,0:T(8,128)(2,1)S(1)}, f32[16,256]{1,0:T(8,128)S(1)}, f32[16,256]{1,0:T(8,128)S(1)}, f32...) custom-call(bf16[512,256]{1,0:T(8,128)(2,1)S(1)} %bitcast.16, ...), custom_call_target="tpu_custom_call" | custom-call | tf_op jit(solution)/shard_map/pallas_call | solution.py:334
  24.3 0.0 collective-permute-done.edge_ref
  24.3 0.7 %shard_map.120 = (bf16[8,136,128]{2,1,0:T(8,128)(2,1)S(1)}, f32[8,1280]{1,0:T(8,128)S(1)}) custom-call(bf16[512,128]{1,0:T(8,128)(2,1)S(1)} %collective-permute-done.edge_ref, f32[8,1280]{1,0:T(8,128)S(1)} %get-tuple-element.40.first_ref, f32[8,1280]{1,0:T(8,128)S(1)} %pad.14.vec_ref, bf16[512,1280]{1,0:T(8,128)(2,1)S(1)} %get-tuple-element.36.w_xbc_ref, ...), custom_call_target="tpu_custom_call" | custom-call | tf_op jit(solution)/shard_map/pallas_call | solution.py:334
  25.0 16.6 %all_to_all.28.states_ref = bf16[8,136,128]{2,1,0:T(8,128)(2,1)S(1)} all-to-all(bf16[8,136,128]{2,1,0:T(8,128)(2,1)S(1)} %get-tuple-element.44), channel_id=1, replica_groups={{0,16,32,48,64,80,96,112},{128,144,160,176,192,208,224,240},{256,272,28..., dimensions={0} | all-to-all | bytes 557056 | tf_op jit(solution)/shard_map/all_to_all | solution.py:33
  41.7 0.1 shard_map.121.total_ref
  41.8 8.8 %collective-permute-start.1 = (bf16[136,128]{1,0:T(8,128)(2,1)S(1)}, bf16[136,128]{1,0:T(8,128)(2,1)S(1)}, u32[]{:S(2)}, u32[]{:S(2)}) collective-permute-start(bf16[136,128]{1,0:T(8,128)(2,1)S(1)} %shard_map.121.total_ref), channel_id=1, source_target_pairs={{0,128},{16,144},{32,160},{48,176},{64,192},{80,208},{96,224},{112... | collective-permute-start | bytes 104456 | tf_op jit(solution)/shard_map/ppermute | solution.py:23
  50.6 1.3 %collective-permute-start.5 = (bf16[136,128]{1,0:T(8,128)(2,1)S(1)}, bf16[136,128]{1,0:T(8,128)(2,1)S(1)}, u32[]{:S(2)}, u32[]{:S(2)}) collective-permute-start(bf16[136,128]{1,0:T(8,128)(2,1)S(1)} %shard_map.121.total_ref), channel_id=1, source_target_pairs={{0,384},{16,400},{32,416},{48,432},{64,448},{80,464},{96,480},{112... | collective-permute-start | bytes 104456 | tf_op jit(solution)/shard_map/ppermute | solution.py:23
  51.9 0.7 collective-permute-start.4
  52.5 0.0 collective-permute-done.1.earlier_ref.refs_0_
  52.6 0.7 collective-permute-start.2
  53.2 0.7 collective-permute-start.3
  53.9 0.0 collective-permute-done.5.refs_4_
  53.9 0.0 collective-permute-done.4.refs_3_
  53.9 0.0 collective-permute-done.2.refs_1_
  53.9 0.0 collective-permute-done.3.refs_2_
  54.0 0.8 %shard_map.123 = bf16[8,128,128]{2,1,0:T(8,128)(2,1)} custom-call(bf16[8,136,128]{2,1,0:T(8,128)(2,1)S(1)} %all_to_all.28.states_ref, bf16[136,128]{1,0:T(8,128)(2,1)S(1)} %collective-permute-done.1.earlier_ref.refs_0_, bf16[136,128]{1,0:T(8,128)(2,1)S(1)} %collective-permute-done.2.refs_1_, bf16[136,128]{1,0:T(8,128)(2,1)S(1)} %collective-permute-done.3.refs_2_, ...), custom_call_target="tpu_custom_call" | custom-call | tf_op jit(solution)/shard_map/pallas_call | solution.py:334
  54.8 4.9 %all-to-all-start.2 = ((bf16[8,128,128]{2,1,0:T(8,128)(2,1)}), bf16[8,128,128]{2,1,0:T(8,128)(2,1)S(1)}, u32[]{:S(2)}, u32[]{:S(2)}) async-start(bf16[8,128,128]{2,1,0:T(8,128)(2,1)} %shard_map.123), calls=%async_computation.2 | async-start | bytes 524288 | tf_op jit(solution)/shard_map/all_to_all | solution.py:33
  59.6 2.6 %shard_map.124 = (f32[1024,256]{1,0:T(8,128)S(1)}, f32[1024,256]{1,0:T(8,128)S(1)}, bf16[128,256]{1,0:T(8,128)(2,1)S(1)}) custom-call(bf16[512,256]{1,0:T(8,128)(2,1)S(1)} %get-tuple-element.49.normed_ref, bf16[512,1024]{1,0:T(8,128)(2,1)} %w_gate_ref.1, bf16[1280,256]{1,0:T(8,128)(2,1)S(1)} %get-tuple-element.50.main_ref, ...), custom_call_target="tpu_custom_call" | custom-call | tf_op jit(solution)/shard_map/pallas_call | solution.py:334
  62.2 6.2 %all-to-all-done.2 = bf16[8,128,128]{2,1,0:T(8,128)(2,1)S(1)} async-done(((bf16[8,128,128]{2,1,0:T(8,128)(2,1)}), bf16[8,128,128]{2,1,0:T(8,128)(2,1)S(1)}, u32[]{:S(2)}, u32[]{:S(2)}) %all-to-all-start.2) | async-done | bytes 262176 | tf_op jit(solution)/shard_map/all_to_all | solution.py:33
  68.4 2.5 %shard_map.125 = bf16[256,512]{1,0:T(8,128)(2,1)} custom-call(bf16[1024,128]{1,0:T(8,128)(2,1)S(1)} %bitcast.17, bf16[128,256]{1,0:T(8,128)(2,1)S(1)} %get-tuple-element.54.query_ref, f32[1024,256]{1,0:T(8,128)S(1)} %get-tuple-element.55.grown_ref, f32[1024,256]{1,0:T(8,128)S(1)} %get-tuple-element.56.y_ref, f32[8,1280]{1,0:T(8,128)S(1)} %pad.14.vec_ref, ...), custom_call_target="tpu_custom_call" | custom-call | tf_op jit(solution)/shard_map/pallas_call | solution.py:334
  (4 shorter events, 0.0 us)
Async XLA Ops:
  0.0 10.6 %copy-start = (f32[16]{0:T(128)S(1)}, f32[16]{0:T(128)}, u32[]{:S(2)}) copy-start(f32[16]{0:T(128)} %param.21) | copy-start | bytes 196
  0.0 10.6 %copy-start.1 = (f32[16]{0:T(128)S(1)}, f32[16]{0:T(128)}, u32[]{:S(2)}) copy-start(f32[16]{0:T(128)} %param.18) | copy-start | bytes 196
  0.0 15.1 %all-to-all-start = ((bf16[16,256,32]{1,2,0:T(8,128)(2,1)}), bf16[16,256,32]{1,2,0:T(8,128)(2,1)S(1)}, u32[]{:S(2)}, u32[]{:S(2)}) async-start(bf16[16,256,32]{1,2,0:T(8,128)(2,1)} %param.12), calls=%async_computation | async-start | bytes 524288 | tf_op jit(solution)/shard_map/all_to_all | solution.py:372
  15.1 9.1 %collective-permute-start = (bf16[512,128]{1,0:T(8,128)(2,1)S(1)}, bf16[512,128]{1,0:T(8,128)(2,1)S(1)}, u32[]{:S(2)}, u32[]{:S(2)}) collective-permute-start(bf16[512,128]{1,0:T(8,128)(2,1)S(1)} %slice.4), channel_id=1, source_target_pairs={{0,16},{16,32},{32,48},{48,64},{64,80},{80,96},{96,112},{112,128},... | collective-permute-start | bytes 393224 | tf_op jit(solution)/shard_map/ppermute | solution.py:23
  41.8 10.8 %collective-permute-start.1 = (bf16[136,128]{1,0:T(8,128)(2,1)S(1)}, bf16[136,128]{1,0:T(8,128)(2,1)S(1)}, u32[]{:S(2)}, u32[]{:S(2)}) collective-permute-start(bf16[136,128]{1,0:T(8,128)(2,1)S(1)} %shard_map.121.total_ref), channel_id=1, source_target_pairs={{0,128},{16,144},{32,160},{48,176},{64,192},{80,208},{96,224},{112... | collective-permute-start | bytes 104456 | tf_op jit(solution)/shard_map/ppermute | solution.py:23
  50.6 3.4 %collective-permute-start.5 = (bf16[136,128]{1,0:T(8,128)(2,1)S(1)}, bf16[136,128]{1,0:T(8,128)(2,1)S(1)}, u32[]{:S(2)}, u32[]{:S(2)}) collective-permute-start(bf16[136,128]{1,0:T(8,128)(2,1)S(1)} %shard_map.121.total_ref), channel_id=1, source_target_pairs={{0,384},{16,400},{32,416},{48,432},{64,448},{80,464},{96,480},{112... | collective-permute-start | bytes 104456 | tf_op jit(solution)/shard_map/ppermute | solution.py:23
  51.9 2.1 %collective-permute-start.4 = (bf16[136,128]{1,0:T(8,128)(2,1)S(1)}, bf16[136,128]{1,0:T(8,128)(2,1)S(1)}, u32[]{:S(2)}, u32[]{:S(2)}) collective-permute-start(bf16[136,128]{1,0:T(8,128)(2,1)S(1)} %shard_map.121.total_ref), channel_id=1, source_target_pairs={{128,384},{144,400},{160,416},{176,432},{192,448},{208,464},{224,4... | collective-permute-start | bytes 104456 | tf_op jit(solution)/shard_map/ppermute | solution.py:23
  52.6 1.4 %collective-permute-start.2 = (bf16[136,128]{1,0:T(8,128)(2,1)S(1)}, bf16[136,128]{1,0:T(8,128)(2,1)S(1)}, u32[]{:S(2)}, u32[]{:S(2)}) collective-permute-start(bf16[136,128]{1,0:T(8,128)(2,1)S(1)} %get-tuple-element.45), channel_id=1, source_target_pairs={{128,256},{144,272},{160,288},{176,304},{192,320},{208,336},{224,3... | collective-permute-start | bytes 104456 | tf_op jit(solution)/shard_map/ppermute | solution.py:23
  53.2 0.7 collective-permute-start.3
  54.8 13.6 %all-to-all-start.2 = ((bf16[8,128,128]{2,1,0:T(8,128)(2,1)}), bf16[8,128,128]{2,1,0:T(8,128)(2,1)S(1)}, u32[]{:S(2)}, u32[]{:S(2)}) async-start(bf16[8,128,128]{2,1,0:T(8,128)(2,1)} %shard_map.123), calls=%async_computation.2 | async-start | bytes 524288 | tf_op jit(solution)/shard_map/all_to_all | solution.py:33

commit v9 on v8

--- a/solution.py
+++ b/solution.py
@@ -94,7 +94,7 @@
 
 def main_kernel(x_ref, vec_ref, w_xbc_ref, w_step_ref, head_ref, gaps_ref,
                 normed_ref, act_ref, dt_ref, cs_ref, state_ref, logs_ref, first_ref, coef_first_ref,
-                coef_ref, rows_ref, upright_ref, shift_ref):
+                coef_ref, rows_ref, upright_ref, shift_ref, weighted_ref):
     depth, length = x_ref.shape
     heads = dt_ref.shape[0]
     inner, state_width = state_ref.shape
@@ -132,21 +132,23 @@
         for tap in range(BIAS):
             first = EXTRA - (BIAS - 1 - tap)
             conv = conv + vec_ref[tap : tap + 1, cols] * shift_ref[first : first + length, cols]
-        act = (conv * jax.nn.sigmoid(conv)).T.astype(bf16)
-        act_ref[at : at + step, :] = act
-        return act
-
-    b = act_of(inner, state_width)
+        act = conv * jax.nn.sigmoid(conv)
+        turned = act.T.astype(bf16)
+        act_ref[at : at + step, :] = turned
+        return act.astype(bf16), turned
+
+    b, _ = act_of(inner, state_width)
     act_of(inner + state_width, state_width)
     step = 2 * head_dim
     for at in range(0, inner, step):
-        act = act_of(at, step).astype(f32)
+        act = act_of(at, step)[1].astype(f32)
         head = at // head_dim
         coef = jnp.concatenate(
             [jnp.broadcast_to(coef_ref[h : h + 1, :], (head_dim, length)) for h in (head, head + 1)],
             axis=0,
         )
-        state_ref[at : at + step, :] = contract((act * coef).astype(bf16), b, ((1,), (1,)))
+        weighted_ref[at : at + step, :] = (act * coef).astype(bf16)
+    state_ref[...] = jnp.dot(weighted_ref[...], b, preferred_element_type=f32)
     first_ref[...] = shift_ref[EXTRA : 2 * EXTRA, :]
 
 
@@ -172,10 +174,9 @@
     b = act[:, inner : inner + state_width]
     b = jnp.concatenate([b, jnp.zeros_like(b)], axis=0).astype(bf16)
     size = inner // GROUP
+    whole = state_ref[...] + contract(weighted, b, ((0,), (0,)))
     for part in range(GROUP):
-        rows = slice(part * size, (part + 1) * size)
-        late = contract(weighted[:, rows], b, ((0,), (0,)))
-        send_ref[part, 0:size, :] = (state_ref[rows, :] + late).astype(bf16)
+        send_ref[part, 0:size, :] = whole[part * size : (part + 1) * size, :].astype(bf16)
         send_ref[part, size : size + EXTRA, :] = logs_ref[part * EXTRA : (part + 1) * EXTRA, :]
 
 
@@ -217,7 +218,7 @@
     send_ref[size : size + EXTRA, :] = rows_ref[...].astype(bf16)
 
 
-def join_kernel(own, total_ref, earlier_ref, send_ref, same_ref):
+def join_kernel(own, total_ref, earlier_ref, send_ref):
     size = send_ref.shape[0] - EXTRA
     head_dim = size // own
     jumps = read_logs(total_ref[size:, :], own)
@@ -226,11 +227,9 @@
         state = jnp.exp(jumps[h]) * earlier_ref[rows, :].astype(f32)
         send_ref[rows, :] = (total_ref[rows, :].astype(f32) + state).astype(bf16)
     send_ref[size:, :] = jnp.zeros((EXTRA, send_ref.shape[1]), bf16)
-    same_ref[...] = total_ref[...]
-
-
-def combine_kernel(own, states_ref, *refs):
-    *whole, near_ref, middle_ref, far_ref, back_ref = refs
+
+
+def combine_kernel(own, states_ref, near_ref, after_ref, far_ref, middle_ref, back_ref):
     size = back_ref.shape[1]
     head_dim = size // own
     logs = [read_logs(states_ref[m, size : size + EXTRA, :], own) for m in range(GROUP)]
@@ -241,8 +240,7 @@
         state = middle_ref[rows, :].astype(f32)
         state = state + jnp.exp(middle_jumps[h]) * far_ref[rows, :].astype(f32)
         state = near_ref[rows, :].astype(f32) + jnp.exp(near_jumps[h]) * state
-        for ref in whole:
-            state = state + ref[rows, :].astype(f32)
+        state = state + after_ref[rows, :].astype(f32)
         for m in range(GROUP):
             back_ref[m, rows, :] = state.astype(bf16)
             state = jnp.exp(logs[m][h]) * state + states_ref[m, rows, :].astype(f32)
@@ -306,12 +304,11 @@
                   out_ref, gated_ref, normed_ref, weight_ref, sem):
     fetches = fetch_rows(w_out_ref, weight_ref, sem)
     inner, length = y_ref.shape
-    queries = query_ref[...]
+    gated_ref[...] = jnp.dot(carried_ref[...], query_ref[...], preferred_element_type=f32)
     total = jnp.zeros((1, length), f32)
     for at in range(0, inner, EDGE):
         rows = slice(at, at + EDGE)
-        picked = jnp.dot(carried_ref[rows, :], queries, preferred_element_type=f32)
-        gated = y_ref[rows, :] + grown_ref[rows, :] * picked
+        gated = y_ref[rows, :] + grown_ref[rows, :] * gated_ref[rows, :]
         gated_ref[rows, :] = gated
         total = total + jnp.sum(gated * gated, axis=0, keepdims=True)
     scale = lax.rsqrt(total / inner + epsilon)
@@ -399,6 +396,7 @@
             pltpu.VMEM((GROUP * EXTRA, state_width), f32),
             pltpu.VMEM((length, depth), bf16),
             pltpu.VMEM((EXTRA + length, width), f32),
+            pltpu.VMEM((inner, length), bf16),
         ],
         x, vec, w_xbc, w_step_t, head, gaps,
     )
@@ -416,22 +414,21 @@
         states,
     )
     assert lax.axis_size("seq") == 4 * GROUP
-    first = passed_along(total, "seq", GROUP, members(0))
+    near = passed_along(total, "seq", GROUP, members(0, 2))
     middle = passed_along(total, "seq", 2 * GROUP, members(1))
     far = passed_along(total, "seq", 3 * GROUP, members(0))
-    joined, same = call(
+    joined = call(
         functools.partial(join_kernel, own),
-        [shape((size + EXTRA, state_width), bf16)] * 2,
+        shape((size + EXTRA, state_width), bf16),
         [],
-        total, first,
+        total, near,
     )
     after = passed_along(joined, "seq", GROUP, members(1))
-    near = passed_along(same, "seq", GROUP, members(2))
     back = call(
         functools.partial(combine_kernel, own),
         shape((GROUP, size, state_width), bf16),
         [],
-        states, first, after, near, middle, far,
+        states, near, after, far, middle,
     )
     back, act = lax.optimization_barrier((back, act))
     carried = within_groups(back).reshape(inner, state_width)

time: 71.4 us -> 72.1 us (level)
  starting transfers between devices: 30.2 us -> 31.7 us
  Pallas kernels: 11.6 us -> 10.2 us
    pallas_call x8, Pallas kernels: 11.6 us -> 10.2 us  [call(): pl.pallas_call(kernel, out_shape=outs, in_specs=[left if at in fetched el...]
    ppermute x6 -> x5, starting transfers between devices: 17.6 us -> 18.4 us  [passed_along(): return lax.ppermute(block, axis, route)]
    all_to_all x1, starting transfers between devices: 4.86 us -> 5.61 us  [within_groups(): lax.all_to_all(blocks, 'seq', split_axis=0, concat_axis=0, tiled=True, ax...]
  transfers between devices with their start and end apart: 8 -> 7, of which waited for: 2 -> 3; matrix products, arithmetic and copies ran while one was open for 2% -> 2% of each run, Pallas kernels for 11% -> 8%
where the time goes in v9:
time: 72.1 us; the launch traced here: 71.6 us
  starting transfers between devices  31.7 us (44%)
  blocking collectives  16.6 us (23%)
  waiting for transfers between devices  11.3 us (16%)
  Pallas kernels  10.2 us (14%)
  local copies, waits for them, and re-layouts  0.81 us (1%)
  other arithmetic  0.79 us (1%)
    ppermute x5, starting transfers between devices, passed_along(): return lax.ppermute(block, axis, route)  18.4 us
    all_to_all x1, blocking collectives, within_groups(): lax.all_to_all(blocks, 'seq', split_axis=0, concat_axis=0, tiled=True, ax...  16.6 us
    pallas_call x8, Pallas kernels, call(): pl.pallas_call(kernel, out_shape=outs, in_specs=[left if at in fetched el...  10.2 us
    all_to_all x1, starting transfers between devices, local(): lax.all_to_all(columns, 'table', split_axis=0, concat_axis=2, tiled=True)  7.72 us
    all_to_all x1, waiting for transfers between devices, within_groups(): lax.all_to_all(blocks, 'seq', split_axis=0, concat_axis=0, tiled=True, ax...  6.17 us
    all_to_all x1, starting transfers between devices, within_groups(): lax.all_to_all(blocks, 'seq', split_axis=0, concat_axis=0, tiled=True, ax...  5.61 us
    all_to_all x1, waiting for transfers between devices, local(): lax.all_to_all(columns, 'table', split_axis=0, concat_axis=2, tiled=True)  4.5 us
  transfers between devices with their start and end apart: 7, of which 3 were waited for; matrix products, arithmetic and copies ran while one was open for 2% of the time, Pallas kernels for 8%

profile of v9, /device:TPU:1, one launch (start us, length us, event | category | flops | bytes accessed | tf_op | source)
XLA Modules:
  0.0 71.6 jit_solution(3503021555895626470)
XLA Ops:
  0.0 0.0 copy-start
  0.0 0.0 copy-start.1
  0.0 7.7 %all-to-all-start = ((bf16[16,256,32]{1,2,0:T(8,128)(2,1)}), bf16[16,256,32]{1,2,0:T(8,128)(2,1)S(1)}, u32[]{:S(2)}, u32[]{:S(2)}) async-start(bf16[16,256,32]{1,2,0:T(8,128)(2,1)} %param.12), calls=%async_computation | async-start | bytes 524288 | tf_op jit(solution)/shard_map/all_to_all | solution.py:369
  7.7 0.7 broadcast_in_dim.12
  8.4 0.8 %select_maximum_fusion = f32[7,1280]{1,0:T(8,128)S(1)} fusion(f32[1,1024]{1,0:T(1,128)} %bitcast.19, f32[1,512]{1,0:T(1,128)} %bitcast.20, f32[1,1280]{1,0:T(1,128)S(1)} %broadcast_in_dim.12, f32[4,1280]{1,0:T(4,128)} %param.19), kind=kLoop, calls=%fused_computation.2 | loop fusion | flops 80640 | bytes 67584 | tf_op jit(solution)/shard_map/concatenate | solution.py:365
  9.2 1.4 %shard_map.118 = (bf16[512,1280]{1,0:T(8,128)(2,1)S(1)}, bf16[16,512]{1,0:T(8,128)(2,1)S(1)}, f32[1,256]{1,0:T(1,128)S(1)}) custom-call(bf16[512,1280]{1,0:T(8,128)(2,1)} %refs_0_.1, bf16[16,512]{1,0:T(8,128)(2,1)} %bitcast.18, f32[1,256]{1,0:T(1,128)} %refs_2_.1), custom_call_target="tpu_custom_call" | custom-call | tf_op jit(solution)/shard_map/pallas_call | solution.py:331
  10.6 0.0 copy-done
  10.6 0.0 copy-done.1
  10.6 4.5 %all-to-all-done = bf16[16,256,32]{1,2,0:T(8,128)(2,1)S(1)} async-done(((bf16[16,256,32]{1,2,0:T(8,128)(2,1)}), bf16[16,256,32]{1,2,0:T(8,128)(2,1)S(1)}, u32[]{:S(2)}, u32[]{:S(2)}) %all-to-all-start) | async-done | bytes 262176 | tf_op jit(solution)/shard_map/all_to_all | solution.py:369
  15.1 5.5 %collective-permute-start = (bf16[512,128]{1,0:T(8,128)(2,1)S(1)}, bf16[512,128]{1,0:T(8,128)(2,1)S(1)}, u32[]{:S(2)}, u32[]{:S(2)}) collective-permute-start(bf16[512,128]{1,0:T(8,128)(2,1)S(1)} %slice.4), channel_id=1, source_target_pairs={{0,16},{16,32},{32,48},{48,64},{64,80},{80,96},{96,112},{112,128},... | collective-permute-start | bytes 393224 | tf_op jit(solution)/shard_map/ppermute | solution.py:23
  20.6 0.1 copy.15.head_ref
  20.7 2.1 %shard_map.119 = (bf16[512,256]{1,0:T(8,128)(2,1)S(1)}, bf16[1280,256]{1,0:T(8,128)(2,1)S(1)}, f32[16,256]{1,0:T(8,128)S(1)}, f32[16,256]{1,0:T(8,128)S(1)}, f32...) custom-call(bf16[512,256]{1,0:T(8,128)(2,1)S(1)} %bitcast.16, ...), custom_call_target="tpu_custom_call" | custom-call | tf_op jit(solution)/shard_map/pallas_call | solution.py:331
  22.9 0.0 collective-permute-done.edge_ref
  22.9 0.8 %shard_map.120 = (bf16[8,136,128]{2,1,0:T(8,128)(2,1)S(1)}, f32[8,1280]{1,0:T(8,128)S(1)}) custom-call(bf16[512,128]{1,0:T(8,128)(2,1)S(1)} %collective-permute-done.edge_ref, f32[8,1280]{1,0:T(8,128)S(1)} %get-tuple-element.38.first_ref, f32[8,1280]{1,0:T(8,128)S(1)} %pad.14.vec_ref, bf16[512,1280]{1,0:T(8,128)(2,1)S(1)} %get-tuple-element.34.w_xbc_ref, ...), custom_call_target="tpu_custom_call" | custom-call | tf_op jit(solution)/shard_map/pallas_call | solution.py:331
  23.7 16.6 %all_to_all.28.states_ref = bf16[8,136,128]{2,1,0:T(8,128)(2,1)S(1)} all-to-all(bf16[8,136,128]{2,1,0:T(8,128)(2,1)S(1)} %get-tuple-element.42), channel_id=1, replica_groups={{0,16,32,48,64,80,96,112},{128,144,160,176,192,208,224,240},{256,272,28..., dimensions={0} | all-to-all | bytes 557056 | tf_op jit(solution)/shard_map/all_to_all | solution.py:33
  40.3 0.1 shard_map.121.total_ref
  40.4 8.8 %collective-permute-start.1 = (bf16[136,128]{1,0:T(8,128)(2,1)S(1)}, bf16[136,128]{1,0:T(8,128)(2,1)S(1)}, u32[]{:S(2)}, u32[]{:S(2)}) collective-permute-start(bf16[136,128]{1,0:T(8,128)(2,1)S(1)} %shard_map.121.total_ref), channel_id=1, source_target_pairs={{0,128},{16,144},{32,160},{48,176},{64,192},{80,208},{96,224},{112... | collective-permute-start | bytes 104456 | tf_op jit(solution)/shard_map/ppermute | solution.py:23
  49.2 0.7 collective-permute-start.4
  49.9 2.8 %collective-permute-start.3 = (bf16[136,128]{1,0:T(8,128)(2,1)S(1)}, bf16[136,128]{1,0:T(8,128)(2,1)S(1)}, u32[]{:S(2)}, u32[]{:S(2)}) collective-permute-start(bf16[136,128]{1,0:T(8,128)(2,1)S(1)} %shard_map.121.total_ref), channel_id=1, source_target_pairs={{0,384},{16,400},{32,416},{48,432},{64,448},{80,464},{96,480},{112... | collective-permute-start | bytes 104456 | tf_op jit(solution)/shard_map/ppermute | solution.py:23
  52.7 0.0 collective-permute-done.1.earlier_ref.near_ref
  52.7 0.7 collective-permute-start.2
  53.4 0.0 collective-permute-done.4.middle_ref
  53.4 0.6 collective-permute-done.3.far_ref
  54.0 0.0 collective-permute-done.2.after_ref
  54.0 0.8 %shard_map.123 = bf16[8,128,128]{2,1,0:T(8,128)(2,1)} custom-call(bf16[8,136,128]{2,1,0:T(8,128)(2,1)S(1)} %all_to_all.28.states_ref, bf16[136,128]{1,0:T(8,128)(2,1)S(1)} %collective-permute-done.1.earlier_ref.near_ref, bf16[136,128]{1,0:T(8,128)(2,1)S(1)} %collective-permute-done.2.after_ref, bf16[136,128]{1,0:T(8,128)(2,1)S(1)} %collective-permute-done.3.far_ref, ...), custom_call_target="tpu_custom_call" | custom-call | tf_op jit(solution)/shard_map/pallas_call | solution.py:331
  54.8 5.6 %all-to-all-start.2 = ((bf16[8,128,128]{2,1,0:T(8,128)(2,1)}), bf16[8,128,128]{2,1,0:T(8,128)(2,1)S(1)}, u32[]{:S(2)}, u32[]{:S(2)}) async-start(bf16[8,128,128]{2,1,0:T(8,128)(2,1)} %shard_map.123), calls=%async_computation.2 | async-start | bytes 524288 | tf_op jit(solution)/shard_map/all_to_all | solution.py:33
  60.4 2.6 %shard_map.124 = (f32[1024,256]{1,0:T(8,128)S(1)}, f32[1024,256]{1,0:T(8,128)S(1)}, bf16[128,256]{1,0:T(8,128)(2,1)S(1)}) custom-call(bf16[512,256]{1,0:T(8,128)(2,1)S(1)} %get-tuple-element.45.normed_ref, bf16[512,1024]{1,0:T(8,128)(2,1)} %w_gate_ref.1, bf16[1280,256]{1,0:T(8,128)(2,1)S(1)} %get-tuple-element.46.main_ref, ...), custom_call_target="tpu_custom_call" | custom-call | tf_op jit(solution)/shard_map/pallas_call | solution.py:331
  63.0 6.2 %all-to-all-done.2 = bf16[8,128,128]{2,1,0:T(8,128)(2,1)S(1)} async-done(((bf16[8,128,128]{2,1,0:T(8,128)(2,1)}), bf16[8,128,128]{2,1,0:T(8,128)(2,1)S(1)}, u32[]{:S(2)}, u32[]{:S(2)}) %all-to-all-start.2) | async-done | bytes 262176 | tf_op jit(solution)/shard_map/all_to_all | solution.py:33
  69.1 2.4 %shard_map.125 = bf16[256,512]{1,0:T(8,128)(2,1)} custom-call(bf16[1024,128]{1,0:T(8,128)(2,1)S(1)} %bitcast.17, bf16[128,256]{1,0:T(8,128)(2,1)S(1)} %get-tuple-element.50.query_ref, f32[1024,256]{1,0:T(8,128)S(1)} %get-tuple-element.51.grown_ref, f32[1024,256]{1,0:T(8,128)S(1)} %get-tuple-element.52.y_ref, f32[8,1280]{1,0:T(8,128)S(1)} %pad.14.vec_ref, ...), custom_call_target="tpu_custom_call" | custom-call | tf_op jit(solution)/shard_map/pallas_call | solution.py:331
  (4 shorter events, 0.0 us)
Async XLA Ops:
  0.0 10.6 %copy-start = (f32[16]{0:T(128)S(1)}, f32[16]{0:T(128)}, u32[]{:S(2)}) copy-start(f32[16]{0:T(128)} %param.21) | copy-start | bytes 196
  0.0 10.6 %copy-start.1 = (f32[16]{0:T(128)S(1)}, f32[16]{0:T(128)}, u32[]{:S(2)}) copy-start(f32[16]{0:T(128)} %param.18) | copy-start | bytes 196
  0.0 15.1 %all-to-all-start = ((bf16[16,256,32]{1,2,0:T(8,128)(2,1)}), bf16[16,256,32]{1,2,0:T(8,128)(2,1)S(1)}, u32[]{:S(2)}, u32[]{:S(2)}) async-start(bf16[16,256,32]{1,2,0:T(8,128)(2,1)} %param.12), calls=%async_computation | async-start | bytes 524288 | tf_op jit(solution)/shard_map/all_to_all | solution.py:369
  15.1 7.7 %collective-permute-start = (bf16[512,128]{1,0:T(8,128)(2,1)S(1)}, bf16[512,128]{1,0:T(8,128)(2,1)S(1)}, u32[]{:S(2)}, u32[]{:S(2)}) collective-permute-start(bf16[512,128]{1,0:T(8,128)(2,1)S(1)} %slice.4), channel_id=1, source_target_pairs={{0,16},{16,32},{32,48},{48,64},{64,80},{80,96},{96,112},{112,128},... | collective-permute-start | bytes 393224 | tf_op jit(solution)/shard_map/ppermute | solution.py:23
  40.4 12.2 %collective-permute-start.1 = (bf16[136,128]{1,0:T(8,128)(2,1)S(1)}, bf16[136,128]{1,0:T(8,128)(2,1)S(1)}, u32[]{:S(2)}, u32[]{:S(2)}) collective-permute-start(bf16[136,128]{1,0:T(8,128)(2,1)S(1)} %shard_map.121.total_ref), channel_id=1, source_target_pairs={{0,128},{16,144},{32,160},{48,176},{64,192},{80,208},{96,224},{112... | collective-permute-start | bytes 104456 | tf_op jit(solution)/shard_map/ppermute | solution.py:23
  49.2 4.1 %collective-permute-start.4 = (bf16[136,128]{1,0:T(8,128)(2,1)S(1)}, bf16[136,128]{1,0:T(8,128)(2,1)S(1)}, u32[]{:S(2)}, u32[]{:S(2)}) collective-permute-start(bf16[136,128]{1,0:T(8,128)(2,1)S(1)} %shard_map.121.total_ref), channel_id=1, source_target_pairs={{128,384},{144,400},{160,416},{176,432},{192,448},{208,464},{224,4... | collective-permute-start | bytes 104456 | tf_op jit(solution)/shard_map/ppermute | solution.py:23
  49.9 4.1 %collective-permute-start.3 = (bf16[136,128]{1,0:T(8,128)(2,1)S(1)}, bf16[136,128]{1,0:T(8,128)(2,1)S(1)}, u32[]{:S(2)}, u32[]{:S(2)}) collective-permute-start(bf16[136,128]{1,0:T(8,128)(2,1)S(1)} %shard_map.121.total_ref), channel_id=1, source_target_pairs={{0,384},{16,400},{32,416},{48,432},{64,448},{80,464},{96,480},{112... | collective-permute-start | bytes 104456 | tf_op jit(solution)/shard_map/ppermute | solution.py:23
  52.7 1.3 %collective-permute-start.2 = (bf16[136,128]{1,0:T(8,128)(2,1)S(1)}, bf16[136,128]{1,0:T(8,128)(2,1)S(1)}, u32[]{:S(2)}, u32[]{:S(2)}) collective-permute-start(bf16[136,128]{1,0:T(8,128)(2,1)S(1)} %shard_map.122), channel_id=1, source_target_pairs={{128,256},{144,272},{160,288},{176,304},{192,320},{208,336},{224,3... | collective-permute-start | bytes 104456 | tf_op jit(solution)/shard_map/ppermute | solution.py:23
  54.8 14.3 %all-to-all-start.2 = ((bf16[8,128,128]{2,1,0:T(8,128)(2,1)}), bf16[8,128,128]{2,1,0:T(8,128)(2,1)S(1)}, u32[]{:S(2)}, u32[]{:S(2)}) async-start(bf16[8,128,128]{2,1,0:T(8,128)(2,1)} %shard_map.123), calls=%async_computation.2 | async-start | bytes 524288 | tf_op jit(solution)/shard_map/all_to_all | solution.py:33

commit v10 on v9

--- a/solution.py
+++ b/solution.py
@@ -229,7 +229,7 @@
     send_ref[size:, :] = jnp.zeros((EXTRA, send_ref.shape[1]), bf16)
 
 
-def combine_kernel(own, states_ref, near_ref, after_ref, far_ref, middle_ref, back_ref):
+def combine_kernel(own, states_ref, near_ref, after_ref, middle_ref, far_ref, back_ref):
     size = back_ref.shape[1]
     head_dim = size // own
     logs = [read_logs(states_ref[m, size : size + EXTRA, :], own) for m in range(GROUP)]
@@ -247,7 +247,7 @@
 
 
 def inside_kernel(normed_ref, w_gate_ref, main_ref, first_ref, dt_ref, cs_ref,
-                  grown_ref, y_ref, query_ref, act_ref, scores_ref, mix_ref, weight_ref, sem):
+                  gate_ref, y_ref, query_ref, act_ref, scores_ref, mix_ref, weight_ref, sem):
     fetches = fetch_rows(w_gate_ref, weight_ref, sem)
     heads, length = dt_ref.shape
     inner = y_ref.shape[0]
@@ -291,33 +291,29 @@
     step = 4 * head_dim
     for at in range(0, inner, step):
         gate = contract(weight_ref[:, at : at + step], normed, ((0,), (0,)))
-        gate = gate.astype(bf16).astype(f32)
-        gate = gate * jax.nn.sigmoid(gate)
-        for h in range(at // head_dim, (at + step) // head_dim):
-            rows = slice(h * head_dim, (h + 1) * head_dim)
-            own = gate[h * head_dim - at : (h + 1) * head_dim - at, :]
-            grown_ref[rows, :] = jnp.exp(cs_ref[h : h + 1, :]) * own
-            y_ref[rows, :] = y_ref[rows, :] * own
-
-
-def output_kernel(carried_ref, query_ref, grown_ref, y_ref, vec_ref, w_out_ref,
-                  out_ref, gated_ref, normed_ref, weight_ref, sem):
-    fetches = fetch_rows(w_out_ref, weight_ref, sem)
+        gate_ref[at : at + step, :] = gate.astype(bf16)
+
+
+def output_kernel(carried_ref, query_ref, cs_ref, gate_ref, y_ref, vec_ref, w_out_ref,
+                  out_ref, gated_ref, normed_ref):
     inner, length = y_ref.shape
     gated_ref[...] = jnp.dot(carried_ref[...], query_ref[...], preferred_element_type=f32)
+    heads = cs_ref.shape[0]
+    head_dim = inner // heads
+    grown = jnp.exp(cs_ref[...])
     total = jnp.zeros((1, length), f32)
-    for at in range(0, inner, EDGE):
-        rows = slice(at, at + EDGE)
-        gated = y_ref[rows, :] + grown_ref[rows, :] * gated_ref[rows, :]
+    for h in range(heads):
+        rows = slice(h * head_dim, (h + 1) * head_dim)
+        gate = gate_ref[rows, :].astype(f32)
+        gated = y_ref[rows, :] + grown[h : h + 1, :] * gated_ref[rows, :]
+        gated = gated * (gate * jax.nn.sigmoid(gate))
         gated_ref[rows, :] = gated
         total = total + jnp.sum(gated * gated, axis=0, keepdims=True)
     scale = lax.rsqrt(total / inner + epsilon)
     for at in range(0, inner, EDGE):
         gain = columns_of(vec_ref, at)[:, GAIN_OUT : GAIN_OUT + 1]
         normed_ref[at : at + EDGE, :] = (gated_ref[at : at + EDGE, :] * scale * gain).astype(bf16)
-    for fetch in fetches:
-        fetch.wait()
-    out_ref[...] = contract(normed_ref[...], weight_ref[...], ((0,), (0,))).astype(bf16)
+    out_ref[...] = contract(normed_ref[...], w_out_ref[...], ((0,), (0,))).astype(bf16)
 
 
 def call(kernel, outs, scratch, *args, fetched=()):
@@ -428,14 +424,14 @@
         functools.partial(combine_kernel, own),
         shape((GROUP, size, state_width), bf16),
         [],
-        states, near, after, far, middle,
+        states, near, after, middle, far,
     )
     back, act = lax.optimization_barrier((back, act))
     carried = within_groups(back).reshape(inner, state_width)
-    grown, y, query = call(
+    gate, y, query = call(
         inside_kernel,
         [
-            shape((inner, length), f32),
+            shape((inner, length), bf16),
             shape((inner, length), f32),
             shape((state_width, length), bf16),
         ],
@@ -449,17 +445,22 @@
         normed, w_gate, act, act_first, dt, cs,
         fetched=(1,),
     )
+    gate, y, query, w_out = lax.optimization_barrier((gate, y, query, w_out))
+    (w_out,) = call(
+        stage_kernel,
+        [shape(w_out.shape, w_out.dtype)],
+        [pltpu.SemaphoreType.DMA((1,))],
+        w_out,
+        fetched=(0,),
+    )
     out = call(
         output_kernel,
         shape((length, w_out.shape[1]), bf16),
         [
             pltpu.VMEM((inner, length), f32),
             pltpu.VMEM((inner, length), bf16),
-            pltpu.VMEM(w_out.shape, bf16),
-            pltpu.SemaphoreType.DMA((PARTS,)),
         ],
-        carried, query, grown, y, vec, w_out,
-        fetched=(5,),
+        carried, query, cs, gate, y, vec, w_out,
     )
     return out[None]
 

time: 72.1 us -> 70.9 us (0.983)
  waiting for transfers between devices: 11.3 us -> 7.67 us
  Pallas kernels: 10.2 us -> 11.9 us
  local copies, waits for them, and re-layouts: 0.81 us -> 1.6 us
    all_to_all x1, waiting for transfers between devices: 6.17 us -> 3.16 us  [within_groups(): lax.all_to_all(blocks, 'seq', split_axis=0, concat_axis=0, tiled=True, ax...]
    pallas_call x8 -> x9, Pallas kernels: 10.2 us -> 11.9 us  [call(): pl.pallas_call(kernel, out_shape=outs, in_specs=[left if at in fetched el...]
    unnamed x4 -> x8, local copies, waits for them, and re-layouts: 0.01 us -> 0.8 us
  transfers between devices with their start and end apart: 7 -> 7, of which waited for: 3 -> 2; matrix products, arithmetic and copies ran while one was open for 2% -> 2% of each run, Pallas kernels for 8% -> 12%
where the time goes in v10:
time: 70.9 us; the launch traced here: 69.8 us
  starting transfers between devices  31 us (44%)
  blocking collectives  16.6 us (23%)
  Pallas kernels  11.9 us (17%)
  waiting for transfers between devices  7.67 us (11%)
  local copies, waits for them, and re-layouts  1.6 us (2%)
  other arithmetic  0.79 us (1%)
    ppermute x5, starting transfers between devices, passed_along(): return lax.ppermute(block, axis, route)  17.8 us
    all_to_all x1, blocking collectives, within_groups(): lax.all_to_all(blocks, 'seq', split_axis=0, concat_axis=0, tiled=True, ax...  16.6 us
    pallas_call x9, Pallas kernels, call(): pl.pallas_call(kernel, out_shape=outs, in_specs=[left if at in fetched el...  11.9 us
    all_to_all x1, starting transfers between devices, local(): lax.all_to_all(columns, 'table', split_axis=0, concat_axis=2, tiled=True)  7.72 us
    all_to_all x1, starting transfers between devices, within_groups(): lax.all_to_all(blocks, 'seq', split_axis=0, concat_axis=0, tiled=True, ax...  5.54 us
    all_to_all x1, waiting for transfers between devices, local(): lax.all_to_all(columns, 'table', split_axis=0, concat_axis=2, tiled=True)  4.5 us
    all_to_all x1, waiting for transfers between devices, within_groups(): lax.all_to_all(blocks, 'seq', split_axis=0, concat_axis=0, tiled=True, ax...  3.16 us
  transfers between devices with their start and end apart: 7, of which 2 were waited for; matrix products, arithmetic and copies ran while one was open for 2% of the time, Pallas kernels for 12%

profile of v10, /device:TPU:1, one launch (start us, length us, event | category | flops | bytes accessed | tf_op | source)
XLA Modules:
  0.0 69.8 jit_solution(10696346542239804176)
XLA Ops:
  0.0 0.0 copy-start.2
  0.0 0.0 copy-start.3
  0.0 7.7 %all-to-all-start = ((bf16[16,256,32]{1,2,0:T(8,128)(2,1)}), bf16[16,256,32]{1,2,0:T(8,128)(2,1)S(1)}, u32[]{:S(2)}, u32[]{:S(2)}) async-start(bf16[16,256,32]{1,2,0:T(8,128)(2,1)} %param.12), calls=%async_computation | async-start | bytes 524288 | tf_op jit(solution)/shard_map/all_to_all | solution.py:365
  7.7 0.7 %broadcast_in_dim.12 = f32[1,1280]{1,0:T(1,128)S(1)} reshape(f32[1280]{0:T(1024)} %param.20) | data formatting | bytes 10240 | tf_op jit(solution)/shard_map/broadcast_in_dim | solution.py:360
  8.4 0.8 %select_maximum_fusion = f32[7,1280]{1,0:T(8,128)S(1)} fusion(f32[1,1024]{1,0:T(1,128)} %bitcast.19, f32[1,512]{1,0:T(1,128)} %bitcast.20, f32[1,1280]{1,0:T(1,128)S(1)} %broadcast_in_dim.12, f32[4,1280]{1,0:T(4,128)} %param.19), kind=kLoop, calls=%fused_computation.2 | loop fusion | flops 80640 | bytes 67584 | tf_op jit(solution)/shard_map/concatenate | solution.py:361
  9.2 1.4 %shard_map.118 = (bf16[512,1280]{1,0:T(8,128)(2,1)S(1)}, bf16[16,512]{1,0:T(8,128)(2,1)S(1)}, f32[1,256]{1,0:T(1,128)S(1)}) custom-call(bf16[512,1280]{1,0:T(8,128)(2,1)} %refs_0_.1, bf16[16,512]{1,0:T(8,128)(2,1)} %bitcast.18, f32[1,256]{1,0:T(1,128)} %refs_2_.1), custom_call_target="tpu_custom_call" | custom-call | tf_op jit(solution)/shard_map/pallas_call | solution.py:327
  10.6 0.0 copy-done.2
  10.6 0.0 copy-done.3
  10.6 4.5 %all-to-all-done = bf16[16,256,32]{1,2,0:T(8,128)(2,1)S(1)} async-done(((bf16[16,256,32]{1,2,0:T(8,128)(2,1)}), bf16[16,256,32]{1,2,0:T(8,128)(2,1)S(1)}, u32[]{:S(2)}, u32[]{:S(2)}) %all-to-all-start) | async-done | bytes 262176 | tf_op jit(solution)/shard_map/all_to_all | solution.py:365
  15.1 5.5 %collective-permute-start = (bf16[512,128]{1,0:T(8,128)(2,1)S(1)}, bf16[512,128]{1,0:T(8,128)(2,1)S(1)}, u32[]{:S(2)}, u32[]{:S(2)}) collective-permute-start(bf16[512,128]{1,0:T(8,128)(2,1)S(1)} %slice.4), channel_id=1, source_target_pairs={{0,16},{16,32},{32,48},{48,64},{64,80},{80,96},{96,112},{112,128},... | collective-permute-start | bytes 393224 | tf_op jit(solution)/shard_map/ppermute | solution.py:23
  20.6 0.1 copy.15.head_ref
  20.7 2.1 %shard_map.119 = (bf16[512,256]{1,0:T(8,128)(2,1)S(1)}, bf16[1280,256]{1,0:T(8,128)(2,1)S(1)}, f32[16,256]{1,0:T(8,128)S(1)}, f32[16,256]{1,0:T(8,128)S(1)}, f32...) custom-call(bf16[512,256]{1,0:T(8,128)(2,1)S(1)} %bitcast.16, ...), custom_call_target="tpu_custom_call" | custom-call | tf_op jit(solution)/shard_map/pallas_call | solution.py:327
  22.9 0.0 collective-permute-done.edge_ref
  22.9 0.8 %shard_map.120 = (bf16[8,136,128]{2,1,0:T(8,128)(2,1)S(1)}, f32[8,1280]{1,0:T(8,128)S(1)}) custom-call(bf16[512,128]{1,0:T(8,128)(2,1)S(1)} %collective-permute-done.edge_ref, f32[8,1280]{1,0:T(8,128)S(1)} %get-tuple-element.42.first_ref, f32[8,1280]{1,0:T(8,128)S(1)} %pad.14.vec_ref, bf16[512,1280]{1,0:T(8,128)(2,1)S(1)} %get-tuple-element.38.w_xbc_ref, ...), custom_call_target="tpu_custom_call" | custom-call | tf_op jit(solution)/shard_map/pallas_call | solution.py:327
  23.7 16.6 %all_to_all.28.states_ref = bf16[8,136,128]{2,1,0:T(8,128)(2,1)S(1)} all-to-all(bf16[8,136,128]{2,1,0:T(8,128)(2,1)S(1)} %get-tuple-element.46), channel_id=1, replica_groups={{0,16,32,48,64,80,96,112},{128,144,160,176,192,208,224,240},{256,272,28..., dimensions={0} | all-to-all | bytes 557056 | tf_op jit(solution)/shard_map/all_to_all | solution.py:33
  40.3 0.1 shard_map.121.total_ref
  40.4 8.8 %collective-permute-start.1 = (bf16[136,128]{1,0:T(8,128)(2,1)S(1)}, bf16[136,128]{1,0:T(8,128)(2,1)S(1)}, u32[]{:S(2)}, u32[]{:S(2)}) collective-permute-start(bf16[136,128]{1,0:T(8,128)(2,1)S(1)} %shard_map.121.total_ref), channel_id=1, source_target_pairs={{0,128},{16,144},{32,160},{48,176},{64,192},{80,208},{96,224},{112... | collective-permute-start | bytes 104456 | tf_op jit(solution)/shard_map/ppermute | solution.py:23
  49.2 2.1 %collective-permute-start.4 = (bf16[136,128]{1,0:T(8,128)(2,1)S(1)}, bf16[136,128]{1,0:T(8,128)(2,1)S(1)}, u32[]{:S(2)}, u32[]{:S(2)}) collective-permute-start(bf16[136,128]{1,0:T(8,128)(2,1)S(1)} %shard_map.121.total_ref), channel_id=1, source_target_pairs={{0,384},{16,400},{32,416},{48,432},{64,448},{80,464},{96,480},{112... | collective-permute-start | bytes 104456 | tf_op jit(solution)/shard_map/ppermute | solution.py:23
  51.4 0.7 collective-permute-start.3
  52.0 0.0 collective-permute-done.1.earlier_ref.near_ref
  52.1 0.7 collective-permute-start.2
  52.7 0.0 collective-permute-done.4.far_ref
  52.8 0.0 collective-permute-done.3.middle_ref
  52.8 0.0 collective-permute-done.2.after_ref
  52.8 0.8 %shard_map.123 = bf16[8,128,128]{2,1,0:T(8,128)(2,1)} custom-call(bf16[8,136,128]{2,1,0:T(8,128)(2,1)S(1)} %all_to_all.28.states_ref, bf16[136,128]{1,0:T(8,128)(2,1)S(1)} %collective-permute-done.1.earlier_ref.near_ref, bf16[136,128]{1,0:T(8,128)(2,1)S(1)} %collective-permute-done.2.after_ref, bf16[136,128]{1,0:T(8,128)(2,1)S(1)} %collective-permute-done.3.middle_ref, ...), custom_call_target="tpu_custom_call" | custom-call | tf_op jit(solution)/shard_map/pallas_call | solution.py:327
  53.6 5.5 %all-to-all-start.2 = ((bf16[8,128,128]{2,1,0:T(8,128)(2,1)}), bf16[8,128,128]{2,1,0:T(8,128)(2,1)S(1)}, u32[]{:S(2)}, u32[]{:S(2)}) async-start(bf16[8,128,128]{2,1,0:T(8,128)(2,1)} %shard_map.123), calls=%async_computation.2 | async-start | bytes 524288 | tf_op jit(solution)/shard_map/all_to_all | solution.py:33
  59.1 3.5 %shard_map.124 = (bf16[1024,256]{1,0:T(8,128)(2,1)S(1)}, f32[1024,256]{1,0:T(8,128)S(1)}, bf16[128,256]{1,0:T(8,128)(2,1)S(1)}) custom-call(bf16[512,256]{1,0:T(8,128)(2,1)S(1)} %get-tuple-element.49.normed_ref, bf16[512,1024]{1,0:T(8,128)(2,1)} %w_gate_ref.1, bf16[1280,256]{1,0:T(8,128)(2,1)S(1)} %get-tuple-element.50.main_ref, ...), custom_call_target="tpu_custom_call" | custom-call | tf_op jit(solution)/shard_map/pallas_call | solution.py:327
  62.6 0.0 copy-start
  62.6 0.8 %copy-done = bf16[1024,256]{1,0:T(8,128)(2,1)} copy-done((bf16[1024,256]{1,0:T(8,128)(2,1)}, bf16[1024,256]{1,0:T(8,128)(2,1)S(1)}, u32[]{:S(2)}) %copy-start) | copy-done | bytes 524312
  63.4 0.0 copy-start.1
  63.4 1.3 %shard_map.125.w_out_ref = bf16[1024,512]{1,0:T(8,128)(2,1)S(1)} custom-call(bf16[1024,512]{1,0:T(8,128)(2,1)} %refs_0_.2), custom_call_target="tpu_custom_call" | custom-call | tf_op jit(solution)/shard_map/pallas_call | solution.py:327
  64.7 3.2 %all-to-all-done.2 = bf16[8,128,128]{2,1,0:T(8,128)(2,1)S(1)} async-done(((bf16[8,128,128]{2,1,0:T(8,128)(2,1)}), bf16[8,128,128]{2,1,0:T(8,128)(2,1)S(1)}, u32[]{:S(2)}, u32[]{:S(2)}) %all-to-all-start.2) | async-done | bytes 262176 | tf_op jit(solution)/shard_map/all_to_all | solution.py:33
  67.8 0.0 copy-done.1
  67.8 2.0 %shard_map.126 = bf16[256,512]{1,0:T(8,128)(2,1)} custom-call(bf16[1024,128]{1,0:T(8,128)(2,1)S(1)} %bitcast.17, bf16[128,256]{1,0:T(8,128)(2,1)S(1)} %get-tuple-element.57.query_ref, f32[16,256]{1,0:T(8,128)S(1)} %get-tuple-element.53.cs_ref, bf16[1024,256]{1,0:T(8,128)(2,1)S(1)} %copy-done.1, f32[1024,256]{1,0:T(8,128)S(1)} %get-tuple-element.59.y_ref, ...), custom_call_target="tpu_custom_call" | custom-call | tf_op jit(solution)/shard_map/pallas_call | solution.py:327
  (4 shorter events, 0.0 us)
Async XLA Ops:
  0.0 10.6 %copy-start.2 = (f32[16]{0:T(128)S(1)}, f32[16]{0:T(128)}, u32[]{:S(2)}) copy-start(f32[16]{0:T(128)} %param.21) | copy-start | bytes 196
  0.0 10.6 %copy-start.3 = (f32[16]{0:T(128)S(1)}, f32[16]{0:T(128)}, u32[]{:S(2)}) copy-start(f32[16]{0:T(128)} %param.18) | copy-start | bytes 196
  0.0 15.1 %all-to-all-start = ((bf16[16,256,32]{1,2,0:T(8,128)(2,1)}), bf16[16,256,32]{1,2,0:T(8,128)(2,1)S(1)}, u32[]{:S(2)}, u32[]{:S(2)}) async-start(bf16[16,256,32]{1,2,0:T(8,128)(2,1)} %param.12), calls=%async_computation | async-start | bytes 524288 | tf_op jit(solution)/shard_map/all_to_all | solution.py:365
  15.1 7.7 %collective-permute-start = (bf16[512,128]{1,0:T(8,128)(2,1)S(1)}, bf16[512,128]{1,0:T(8,128)(2,1)S(1)}, u32[]{:S(2)}, u32[]{:S(2)}) collective-permute-start(bf16[512,128]{1,0:T(8,128)(2,1)S(1)} %slice.4), channel_id=1, source_target_pairs={{0,16},{16,32},{32,48},{48,64},{64,80},{80,96},{96,112},{112,128},... | collective-permute-start | bytes 393224 | tf_op jit(solution)/shard_map/ppermute | solution.py:23
  40.4 11.6 %collective-permute-start.1 = (bf16[136,128]{1,0:T(8,128)(2,1)S(1)}, bf16[136,128]{1,0:T(8,128)(2,1)S(1)}, u32[]{:S(2)}, u32[]{:S(2)}) collective-permute-start(bf16[136,128]{1,0:T(8,128)(2,1)S(1)} %shard_map.121.total_ref), channel_id=1, source_target_pairs={{0,128},{16,144},{32,160},{48,176},{64,192},{80,208},{96,224},{112... | collective-permute-start | bytes 104456 | tf_op jit(solution)/shard_map/ppermute | solution.py:23
  49.2 3.5 %collective-permute-start.4 = (bf16[136,128]{1,0:T(8,128)(2,1)S(1)}, bf16[136,128]{1,0:T(8,128)(2,1)S(1)}, u32[]{:S(2)}, u32[]{:S(2)}) collective-permute-start(bf16[136,128]{1,0:T(8,128)(2,1)S(1)} %shard_map.121.total_ref), channel_id=1, source_target_pairs={{0,384},{16,400},{32,416},{48,432},{64,448},{80,464},{96,480},{112... | collective-permute-start | bytes 104456 | tf_op jit(solution)/shard_map/ppermute | solution.py:23
  51.4 1.4 %collective-permute-start.3 = (bf16[136,128]{1,0:T(8,128)(2,1)S(1)}, bf16[136,128]{1,0:T(8,128)(2,1)S(1)}, u32[]{:S(2)}, u32[]{:S(2)}) collective-permute-start(bf16[136,128]{1,0:T(8,128)(2,1)S(1)} %shard_map.121.total_ref), channel_id=1, source_target_pairs={{128,384},{144,400},{160,416},{176,432},{192,448},{208,464},{224,4... | collective-permute-start | bytes 104456 | tf_op jit(solution)/shard_map/ppermute | solution.py:23
  52.1 0.7 collective-permute-start.2
  53.6 14.3 %all-to-all-start.2 = ((bf16[8,128,128]{2,1,0:T(8,128)(2,1)}), bf16[8,128,128]{2,1,0:T(8,128)(2,1)S(1)}, u32[]{:S(2)}, u32[]{:S(2)}) async-start(bf16[8,128,128]{2,1,0:T(8,128)(2,1)} %shard_map.123), calls=%async_computation.2 | async-start | bytes 524288 | tf_op jit(solution)/shard_map/all_to_all | solution.py:33
  62.6 0.8 %copy-start = (bf16[1024,256]{1,0:T(8,128)(2,1)}, bf16[1024,256]{1,0:T(8,128)(2,1)S(1)}, u32[]{:S(2)}) copy-start(bf16[1024,256]{1,0:T(8,128)(2,1)S(1)} %get-tuple-element.58.gate_ref) | copy-start | bytes 1572868
  63.4 4.5 %copy-start.1 = (bf16[1024,256]{1,0:T(8,128)(2,1)S(1)}, bf16[1024,256]{1,0:T(8,128)(2,1)}, u32[]{:S(2)}) copy-start(bf16[1024,256]{1,0:T(8,128)(2,1)} %copy-done) | copy-start | bytes 1572868

commit v11 on v10

--- a/solution.py
+++ b/solution.py
@@ -92,7 +92,16 @@
         copy.wait()
 
 
-def main_kernel(x_ref, vec_ref, w_xbc_ref, w_step_ref, head_ref, gaps_ref,
+def main_kernel(turn_ref, *refs, before):
+    outs = 8
+    operands, rest = refs[:6], refs[6 + (outs if before else 0) :]
+
+    @pl.when((turn_ref[0] == 0) == before)
+    def _():
+        project_and_sum(*operands, *rest)
+
+
+def project_and_sum(x_ref, vec_ref, w_xbc_ref, w_step_ref, head_ref, gaps_ref,
                 normed_ref, act_ref, dt_ref, cs_ref, state_ref, logs_ref, first_ref, coef_first_ref,
                 coef_ref, rows_ref, upright_ref, shift_ref, weighted_ref):
     depth, length = x_ref.shape
@@ -152,11 +161,11 @@
     first_ref[...] = shift_ref[EXTRA : 2 * EXTRA, :]
 
 
-def edge_kernel(edge_ref, first_ref, vec_ref, w_xbc_ref, coef_ref, state_ref, logs_ref,
+def edge_kernel(edge_a_ref, edge_b_ref, first_ref, vec_ref, w_xbc_ref, coef_ref, state_ref, logs_ref,
                 send_ref, act_ref, rows_ref):
     inner, state_width = state_ref.shape
-    depth = edge_ref.shape[0]
-    x = edge_ref[...].astype(f32).T[EDGE - EXTRA :, :]
+    depth = edge_a_ref.shape[0]
+    x = (edge_a_ref[...].astype(f32) + edge_b_ref[...].astype(f32)).T[EDGE - EXTRA :, :]
     scale = lax.rsqrt(jnp.mean(x * x, axis=1, keepdims=True) + epsilon)
     normed = (x * scale * vec_ref[GAIN_IN : GAIN_IN + 1, :depth]).astype(bf16)
     before = jnp.dot(normed, w_xbc_ref[...], preferred_element_type=f32)
@@ -316,7 +325,7 @@
     out_ref[...] = contract(normed_ref[...], w_out_ref[...], ((0,), (0,))).astype(bf16)
 
 
-def call(kernel, outs, scratch, *args, fetched=()):
+def call(kernel, outs, scratch, *args, fetched=(), scalars=0, aliases={}):
     vmem = pl.BlockSpec(memory_space=pltpu.VMEM)
     left = pl.BlockSpec(memory_space=pltpu.HBM)
     single = not isinstance(outs, list)
@@ -327,7 +336,15 @@
     return pl.pallas_call(
         kernel,
         out_shape=outs,
-        in_specs=[left if at in fetched else vmem for at in range(len(args))],
+        in_specs=[
+            pl.BlockSpec(memory_space=pltpu.SMEM)
+            if at < scalars
+            else left
+            if at in fetched
+            else vmem
+            for at in range(len(args))
+        ],
+        input_output_aliases=aliases,
         out_specs=vmem if single else [vmem] * len(outs),
         scratch_shapes=scratch,
         compiler_params=pltpu.CompilerParams(vmem_limit_bytes=12 << 20),
@@ -374,33 +391,48 @@
     whole, vec, head, *staged = lax.optimization_barrier((whole, vec, head, *staged))
     w_xbc, w_step_t, gaps = staged
     x = whole.reshape(length, depth).T
-    edge = passed_along(x[:, length - EDGE :], "seq", 1)
-    normed, act, dt, cs, state, logs, first, coef_first = call(
-        main_kernel,
-        [
-            shape((depth, length), bf16),
-            shape((width, length), bf16),
-            shape((heads, length), f32),
-            shape((heads, length), f32),
-            shape((inner, state_width), f32),
-            shape((GROUP * EXTRA, state_width), bf16),
-            shape((EXTRA, width), f32),
-            shape((EXTRA, inner), f32),
-        ],
-        [
-            pltpu.VMEM((heads, length), f32),
-            pltpu.VMEM((GROUP * EXTRA, state_width), f32),
-            pltpu.VMEM((length, depth), bf16),
-            pltpu.VMEM((EXTRA + length, width), f32),
-            pltpu.VMEM((inner, length), bf16),
-        ],
-        x, vec, w_xbc, w_step_t, head, gaps,
-    )
+    edge = x[:, length - EDGE :]
+    places = lax.axis_size("seq")
+    turn = (lax.axis_index("seq") % 2).astype(jnp.int32)[None]
+    shapes = [
+        shape((depth, length), bf16),
+        shape((width, length), bf16),
+        shape((heads, length), f32),
+        shape((heads, length), f32),
+        shape((inner, state_width), f32),
+        shape((GROUP * EXTRA, state_width), bf16),
+        shape((EXTRA, width), f32),
+        shape((EXTRA, inner), f32),
+    ]
+    scratch = [
+        pltpu.VMEM((heads, length), f32),
+        pltpu.VMEM((GROUP * EXTRA, state_width), f32),
+        pltpu.VMEM((length, depth), bf16),
+        pltpu.VMEM((EXTRA + length, width), f32),
+        pltpu.VMEM((inner, length), bf16),
+    ]
+    operands = [turn, x, vec, w_xbc, w_step_t, head, gaps]
+    results = call(
+        functools.partial(main_kernel, before=False), shapes, scratch, *operands, scalars=1
+    )
+    edge, *results = lax.optimization_barrier((edge, *results))
+    edge_a = passed_along(edge, "seq", 1, range(1, places, 2))
+    edge_b = passed_along(edge, "seq", 1, range(0, places, 2))
+    results = call(
+        functools.partial(main_kernel, before=True),
+        shapes,
+        scratch,
+        *operands,
+        *results,
+        scalars=1,
+        aliases={len(operands) + at: at for at in range(len(shapes))},
+    )
+    normed, act, dt, cs, state, logs, first, coef_first = results
     send, act_first = call(
         edge_kernel,
         [shape((GROUP, size + EXTRA, state_width), bf16), shape((EXTRA, width), f32)],
         [pltpu.VMEM((2 * EXTRA, width), f32)],
-        edge, first, vec, w_xbc, coef_first, state, logs,
+        edge_b, edge_a, first, vec, w_xbc, coef_first, state, logs,
     )
     states = within_groups(send)
     total = call(

time: 70.9 us -> 72.2 us (1.018)
  starting transfers between devices: 31 us -> 29.5 us
  blocking collectives: 16.6 us -> 17.9 us
  waiting for transfers between devices: 7.67 us -> 8.89 us
    ppermute x5 -> x6, waiting for transfers between devices: 0.01 us -> 1.92 us  [passed_along(): return lax.ppermute(block, axis, route)]
    ppermute x5 -> x6, starting transfers between devices: 17.8 us -> 16.2 us  [passed_along(): return lax.ppermute(block, axis, route)]
    all_to_all x1, blocking collectives: 16.6 us -> 17.9 us  [within_groups(): lax.all_to_all(blocks, 'seq', split_axis=0, concat_axis=0, tiled=True, ax...]
    unnamed x8 -> x20, local copies, waits for them, and re-layouts: 0.8 us -> 1.46 us
    pallas_call x9 -> x10, Pallas kernels: 11.9 us -> 12 us  [call(): pl.pallas_call(kernel, out_shape=outs, in_specs=[pl.BlockSpec(memory_spac...]
  transfers between devices with their start and end apart: 7 -> 8, of which waited for: 2 -> 4; matrix products, arithmetic and copies ran while one was open for 2% -> 2% of each run, Pallas kernels for 12% -> 9%
where the time goes in v11:
time: 72.2 us; the launch traced here: 71.6 us
  starting transfers between devices  29.5 us (41%)
  blocking collectives  17.9 us (25%)
  Pallas kernels  12 us (17%)
  waiting for transfers between devices  8.89 us (12%)
  local copies, waits for them, and re-layouts  2.27 us (3%)
  other arithmetic  0.79 us (1%)
    all_to_all x1, blocking collectives, within_groups(): lax.all_to_all(blocks, 'seq', split_axis=0, concat_axis=0, tiled=True, ax...  17.9 us
    ppermute x6, starting transfers between devices, passed_along(): return lax.ppermute(block, axis, route)  16.2 us
    pallas_call x10, Pallas kernels, call(): pl.pallas_call(kernel, out_shape=outs, in_specs=[pl.BlockSpec(memory_spac...  12 us
    all_to_all x1, starting transfers between devices, local(): lax.all_to_all(columns, 'table', split_axis=0, concat_axis=2, tiled=True)  7.72 us
    all_to_all x1, starting transfers between devices, within_groups(): lax.all_to_all(blocks, 'seq', split_axis=0, concat_axis=0, tiled=True, ax...  5.54 us
    all_to_all x1, waiting for transfers between devices, local(): lax.all_to_all(columns, 'table', split_axis=0, concat_axis=2, tiled=True)  4.47 us
    all_to_all x1, waiting for transfers between devices, within_groups(): lax.all_to_all(blocks, 'seq', split_axis=0, concat_axis=0, tiled=True, ax...  2.51 us
    ppermute x6, waiting for transfers between devices, passed_along(): return lax.ppermute(block, axis, route)  1.92 us
  transfers between devices with their start and end apart: 8, of which 4 were waited for; matrix products, arithmetic and copies ran while one was open for 2% of the time, Pallas kernels for 9%

profile of v11, /device:TPU:1, one launch (start us, length us, event | category | flops | bytes accessed | tf_op | source)
XLA Modules:
  0.0 71.6 jit_solution(2003808957365589049)
XLA Ops:
  0.0 0.0 copy-start.8
  0.0 0.0 copy-start.9
  0.0 7.7 %all-to-all-start = ((bf16[16,256,32]{1,2,0:T(8,128)(2,1)}), bf16[16,256,32]{1,2,0:T(8,128)(2,1)S(1)}, u32[]{:S(2)}, u32[]{:S(2)}) async-start(bf16[16,256,32]{1,2,0:T(8,128)(2,1)} %param.12), calls=%async_computation | async-start | bytes 524288 | tf_op jit(solution)/shard_map/all_to_all | solution.py:382
  7.7 0.7 broadcast_in_dim.15
  8.4 0.8 %select_maximum_fusion = f32[7,1280]{1,0:T(8,128)S(1)} fusion(f32[1,1024]{1,0:T(1,128)} %bitcast.21, f32[1,512]{1,0:T(1,128)} %bitcast.22, f32[1,1280]{1,0:T(1,128)S(1)} %broadcast_in_dim.15, f32[4,1280]{1,0:T(4,128)} %param.19), kind=kLoop, calls=%fused_computation.2 | loop fusion | flops 80640 | bytes 67584 | tf_op jit(solution)/shard_map/concatenate | solution.py:378
  9.2 0.0 copy-start
  9.3 1.4 %shard_map.118 = (bf16[512,1280]{1,0:T(8,128)(2,1)S(1)}, bf16[16,512]{1,0:T(8,128)(2,1)S(1)}, f32[1,256]{1,0:T(1,128)S(1)}) custom-call(bf16[512,1280]{1,0:T(8,128)(2,1)} %refs_0_.1, bf16[16,512]{1,0:T(8,128)(2,1)} %bitcast.20, f32[1,256]{1,0:T(1,128)} %refs_2_.1), custom_call_target="tpu_custom_call" | custom-call | tf_op jit(solution)/shard_map/pallas_call | solution.py:336
  10.6 0.0 copy-done.8
  10.6 0.0 copy-done.9
  10.7 4.5 %all-to-all-done = bf16[16,256,32]{1,2,0:T(8,128)(2,1)S(1)} async-done(((bf16[16,256,32]{1,2,0:T(8,128)(2,1)}), bf16[16,256,32]{1,2,0:T(8,128)(2,1)S(1)}, u32[]{:S(2)}, u32[]{:S(2)}) %all-to-all-start) | async-done | bytes 262176 | tf_op jit(solution)/shard_map/all_to_all | solution.py:382
  15.1 0.1 copy.23.refs_4_
  15.2 2.2 %shard_map.119 = (bf16[512,256]{1,0:T(8,128)(2,1)S(1)}, bf16[1280,256]{1,0:T(8,128)(2,1)S(1)}, f32[16,256]{1,0:T(8,128)S(1)}, f32[16,256]{1,0:T(8,128)S(1)}, f32...) custom-call(s32[1]{0:T(128)} %bitcast.10.turn_ref, ...), custom_call_target="tpu_custom_call" | custom-call | tf_op jit(solution)/shard_map/pallas_call | solution.py:336
  17.4 3.4 %collective-permute-start.1 = (bf16[512,128]{1,0:T(8,128)(2,1)S(1)}, bf16[512,128]{1,0:T(8,128)(2,1)S(1)}, u32[]{:S(2)}, u32[]{:S(2)}) collective-permute-start(bf16[512,128]{1,0:T(8,128)(2,1)S(1)} %slice.4), channel_id=1, source_target_pairs={{16,32},{48,64},{80,96},{112,128},{144,160},{176,192},{208,224},{2... | collective-permute-start | bytes 393224 | tf_op jit(solution)/shard_map/ppermute | solution.py:23
  20.8 1.3 %collective-permute-start = (bf16[512,128]{1,0:T(8,128)(2,1)S(1)}, bf16[512,128]{1,0:T(8,128)(2,1)S(1)}, u32[]{:S(2)}, u32[]{:S(2)}) collective-permute-start(bf16[512,128]{1,0:T(8,128)(2,1)S(1)} %slice.4), channel_id=1, source_target_pairs={{0,16},{32,48},{64,80},{96,112},{128,144},{160,176},{192,208},{224... | collective-permute-start | bytes 393224 | tf_op jit(solution)/shard_map/ppermute | solution.py:23
  22.1 0.0 copy-start.4
  22.1 0.6 collective-permute-done.1.edge_b_ref
  22.7 1.3 %collective-permute-done.edge_a_ref = bf16[512,128]{1,0:T(8,128)(2,1)S(1)} collective-permute-done((bf16[512,128]{1,0:T(8,128)(2,1)S(1)}, bf16[512,128]{1,0:T(8,128)(2,1)S(1)}, u32[]{:S(2)}, u32[]{:S(2)}) %collective-permute-start) | collective-permute-done | bytes 131104 | tf_op jit(solution)/shard_map/ppermute | solution.py:23
  24.0 0.0 copy-done
  24.0 0.8 %shard_map.121 = (bf16[8,136,128]{2,1,0:T(8,128)(2,1)S(1)}, f32[8,1280]{1,0:T(8,128)S(1)}) custom-call(bf16[512,128]{1,0:T(8,128)(2,1)S(1)} %collective-permute-done.edge_a_ref, bf16[512,128]{1,0:T(8,128)(2,1)S(1)} %collective-permute-done.1.edge_b_ref, f32[8,1280]{1,0:T(8,128)S(1)} %get-tuple-element.76.first_ref, f32[8,1280]{1,0:T(8,128)S(1)} %pad.14.refs_1_.vec_ref, ...), custom_call_target="tpu_custom_call" | custom-call | tf_op jit(solution)/shard_map/pallas_call | solution.py:336
  24.8 17.9 %all_to_all.28.states_ref = bf16[8,136,128]{2,1,0:T(8,128)(2,1)S(1)} all-to-all(bf16[8,136,128]{2,1,0:T(8,128)(2,1)S(1)} %get-tuple-element.80), channel_id=1, replica_groups={{0,16,32,48,64,80,96,112},{128,144,160,176,192,208,224,240},{256,272,28..., dimensions={0} | all-to-all | bytes 557056 | tf_op jit(solution)/shard_map/all_to_all | solution.py:33
  42.8 0.0 copy-done.4
  42.8 0.1 shard_map.122.total_ref
  42.8 0.0 copy-start.5
  42.9 8.9 %collective-permute-start.2 = (bf16[136,128]{1,0:T(8,128)(2,1)S(1)}, bf16[136,128]{1,0:T(8,128)(2,1)S(1)}, u32[]{:S(2)}, u32[]{:S(2)}) collective-permute-start(bf16[136,128]{1,0:T(8,128)(2,1)S(1)} %shard_map.122.total_ref), channel_id=1, source_target_pairs={{0,128},{16,144},{32,160},{48,176},{64,192},{80,208},{96,224},{112... | collective-permute-start | bytes 104456 | tf_op jit(solution)/shard_map/ppermute | solution.py:23
  51.8 1.3 %collective-permute-start.5 = (bf16[136,128]{1,0:T(8,128)(2,1)S(1)}, bf16[136,128]{1,0:T(8,128)(2,1)S(1)}, u32[]{:S(2)}, u32[]{:S(2)}) collective-permute-start(bf16[136,128]{1,0:T(8,128)(2,1)S(1)} %shard_map.122.total_ref), channel_id=1, source_target_pairs={{0,384},{16,400},{32,416},{48,432},{64,448},{80,464},{96,480},{112... | collective-permute-start | bytes 104456 | tf_op jit(solution)/shard_map/ppermute | solution.py:23
  53.1 0.7 collective-permute-start.4
  53.8 0.0 collective-permute-done.2.earlier_ref.near_ref
  53.8 0.7 collective-permute-start.3
  54.5 0.0 collective-permute-done.5.far_ref
  54.5 0.0 collective-permute-done.4.middle_ref
  54.5 0.0 collective-permute-done.3.after_ref
  54.5 0.8 %shard_map.124 = bf16[8,128,128]{2,1,0:T(8,128)(2,1)} custom-call(bf16[8,136,128]{2,1,0:T(8,128)(2,1)S(1)} %all_to_all.28.states_ref, bf16[136,128]{1,0:T(8,128)(2,1)S(1)} %collective-permute-done.2.earlier_ref.near_ref, bf16[136,128]{1,0:T(8,128)(2,1)S(1)} %collective-permute-done.3.after_ref, bf16[136,128]{1,0:T(8,128)(2,1)S(1)} %collective-permute-done.4.middle_ref, ...), custom_call_target="tpu_custom_call" | custom-call | tf_op jit(solution)/shard_map/pallas_call | solution.py:336
  55.3 5.5 %all-to-all-start.2 = ((bf16[8,128,128]{2,1,0:T(8,128)(2,1)}), bf16[8,128,128]{2,1,0:T(8,128)(2,1)S(1)}, u32[]{:S(2)}, u32[]{:S(2)}) async-start(bf16[8,128,128]{2,1,0:T(8,128)(2,1)} %shard_map.124), calls=%async_computation.2 | async-start | bytes 524288 | tf_op jit(solution)/shard_map/all_to_all | solution.py:33
  60.9 0.0 copy-done.5
  60.9 3.5 %shard_map.125 = (bf16[1024,256]{1,0:T(8,128)(2,1)S(1)}, f32[1024,256]{1,0:T(8,128)S(1)}, bf16[128,256]{1,0:T(8,128)(2,1)S(1)}) custom-call(bf16[512,256]{1,0:T(8,128)(2,1)S(1)} %get-tuple-element.83.normed_ref, bf16[512,1024]{1,0:T(8,128)(2,1)} %w_gate_ref.1, bf16[1280,256]{1,0:T(8,128)(2,1)S(1)} %get-tuple-element.84.main_ref, ...), custom_call_target="tpu_custom_call" | custom-call | tf_op jit(solution)/shard_map/pallas_call | solution.py:336
  64.3 0.0 copy-start.2
  64.3 0.8 %copy-done.2 = bf16[1024,256]{1,0:T(8,128)(2,1)} copy-done((bf16[1024,256]{1,0:T(8,128)(2,1)}, bf16[1024,256]{1,0:T(8,128)(2,1)S(1)}, u32[]{:S(2)}) %copy-start.2) | copy-done | bytes 524312
  65.1 0.0 copy-start.6
  65.1 0.6 copy-done.6
  65.8 0.0 copy-start.1
  65.8 0.0 copy-start.3
  65.8 0.0 copy-start.7
  65.8 1.3 %shard_map.126.w_out_ref = bf16[1024,512]{1,0:T(8,128)(2,1)S(1)} custom-call(bf16[1024,512]{1,0:T(8,128)(2,1)} %refs_0_.2), custom_call_target="tpu_custom_call" | custom-call | tf_op jit(solution)/shard_map/pallas_call | solution.py:336
  67.1 2.5 %all-to-all-done.2 = bf16[8,128,128]{2,1,0:T(8,128)(2,1)S(1)} async-done(((bf16[8,128,128]{2,1,0:T(8,128)(2,1)}), bf16[8,128,128]{2,1,0:T(8,128)(2,1)S(1)}, u32[]{:S(2)}, u32[]{:S(2)}) %all-to-all-start.2) | async-done | bytes 262176 | tf_op jit(solution)/shard_map/all_to_all | solution.py:33
  69.6 0.0 copy-done.1
  69.6 0.0 copy-done.3
  69.6 0.0 copy-done.7
  69.6 2.0 %shard_map.127 = bf16[256,512]{1,0:T(8,128)(2,1)} custom-call(bf16[1024,128]{1,0:T(8,128)(2,1)S(1)} %bitcast.19, bf16[128,256]{1,0:T(8,128)(2,1)S(1)} %copy-done.7, f32[16,256]{1,0:T(8,128)S(1)} %get-tuple-element.87.cs_ref, bf16[1024,256]{1,0:T(8,128)(2,1)S(1)} %copy-done.3, f32[1024,256]{1,0:T(8,128)S(1)} %get-tuple-element.93.y_ref, ...), custom_call_target="tpu_custom_call" | custom-call | tf_op jit(solution)/shard_map/pallas_call | solution.py:336
  (5 shorter events, 0.1 us)
Async XLA Ops:
  0.0 10.6 %copy-start.8 = (f32[16]{0:T(128)S(1)}, f32[16]{0:T(128)}, u32[]{:S(2)}) copy-start(f32[16]{0:T(128)} %param.21) | copy-start | bytes 196
  0.0 10.6 %copy-start.9 = (f32[16]{0:T(128)S(1)}, f32[16]{0:T(128)}, u32[]{:S(2)}) copy-start(f32[16]{0:T(128)} %param.18) | copy-start | bytes 196
  0.0 15.1 %all-to-all-start = ((bf16[16,256,32]{1,2,0:T(8,128)(2,1)}), bf16[16,256,32]{1,2,0:T(8,128)(2,1)S(1)}, u32[]{:S(2)}, u32[]{:S(2)}) async-start(bf16[16,256,32]{1,2,0:T(8,128)(2,1)} %param.12), calls=%async_computation | async-start | bytes 524288 | tf_op jit(solution)/shard_map/all_to_all | solution.py:382
  9.2 14.8 %copy-start = (f32[8,1280]{1,0:T(8,128)}, f32[8,1280]{1,0:T(8,128)S(1)}, u32[]{:S(2)}) copy-start(f32[8,1280]{1,0:T(8,128)S(1)} %pad.14.refs_1_.vec_ref) | copy-start | bytes 122884
  17.4 5.3 %collective-permute-start.1 = (bf16[512,128]{1,0:T(8,128)(2,1)S(1)}, bf16[512,128]{1,0:T(8,128)(2,1)S(1)}, u32[]{:S(2)}, u32[]{:S(2)}) collective-permute-start(bf16[512,128]{1,0:T(8,128)(2,1)S(1)} %slice.4), channel_id=1, source_target_pairs={{16,32},{48,64},{80,96},{112,128},{144,160},{176,192},{208,224},{2... | collective-permute-start | bytes 393224 | tf_op jit(solution)/shard_map/ppermute | solution.py:23
  20.8 3.2 %collective-permute-start = (bf16[512,128]{1,0:T(8,128)(2,1)S(1)}, bf16[512,128]{1,0:T(8,128)(2,1)S(1)}, u32[]{:S(2)}, u32[]{:S(2)}) collective-permute-start(bf16[512,128]{1,0:T(8,128)(2,1)S(1)} %slice.4), channel_id=1, source_target_pairs={{0,16},{32,48},{64,80},{96,112},{128,144},{160,176},{192,208},{224... | collective-permute-start | bytes 393224 | tf_op jit(solution)/shard_map/ppermute | solution.py:23
  22.1 20.7 %copy-start.4 = (f32[16,256]{1,0:T(8,128)}, f32[16,256]{1,0:T(8,128)S(1)}, u32[]{:S(2)}) copy-start(f32[16,256]{1,0:T(8,128)S(1)} %get-tuple-element.86.dt_ref) | copy-start | bytes 49156
  42.8 18.0 %copy-start.5 = (f32[16,256]{1,0:T(8,128)S(1)}, f32[16,256]{1,0:T(8,128)}, u32[]{:S(2)}) copy-start(f32[16,256]{1,0:T(8,128)} %copy-done.4) | copy-start | bytes 49156
  42.9 10.9 %collective-permute-start.2 = (bf16[136,128]{1,0:T(8,128)(2,1)S(1)}, bf16[136,128]{1,0:T(8,128)(2,1)S(1)}, u32[]{:S(2)}, u32[]{:S(2)}) collective-permute-start(bf16[136,128]{1,0:T(8,128)(2,1)S(1)} %shard_map.122.total_ref), channel_id=1, source_target_pairs={{0,128},{16,144},{32,160},{48,176},{64,192},{80,208},{96,224},{112... | collective-permute-start | bytes 104456 | tf_op jit(solution)/shard_map/ppermute | solution.py:23
  51.8 2.7 %collective-permute-start.5 = (bf16[136,128]{1,0:T(8,128)(2,1)S(1)}, bf16[136,128]{1,0:T(8,128)(2,1)S(1)}, u32[]{:S(2)}, u32[]{:S(2)}) collective-permute-start(bf16[136,128]{1,0:T(8,128)(2,1)S(1)} %shard_map.122.total_ref), channel_id=1, source_target_pairs={{0,384},{16,400},{32,416},{48,432},{64,448},{80,464},{96,480},{112... | collective-permute-start | bytes 104456 | tf_op jit(solution)/shard_map/ppermute | solution.py:23
  53.1 1.4 %collective-permute-start.4 = (bf16[136,128]{1,0:T(8,128)(2,1)S(1)}, bf16[136,128]{1,0:T(8,128)(2,1)S(1)}, u32[]{:S(2)}, u32[]{:S(2)}) collective-permute-start(bf16[136,128]{1,0:T(8,128)(2,1)S(1)} %shard_map.122.total_ref), channel_id=1, source_target_pairs={{128,384},{144,400},{160,416},{176,432},{192,448},{208,464},{224,4... | collective-permute-start | bytes 104456 | tf_op jit(solution)/shard_map/ppermute | solution.py:23
  53.8 0.7 collective-permute-start.3
  55.3 14.3 %all-to-all-start.2 = ((bf16[8,128,128]{2,1,0:T(8,128)(2,1)}), bf16[8,128,128]{2,1,0:T(8,128)(2,1)S(1)}, u32[]{:S(2)}, u32[]{:S(2)}) async-start(bf16[8,128,128]{2,1,0:T(8,128)(2,1)} %shard_map.124), calls=%async_computation.2 | async-start | bytes 524288 | tf_op jit(solution)/shard_map/all_to_all | solution.py:33
  64.3 0.8 %copy-start.2 = (bf16[1024,256]{1,0:T(8,128)(2,1)}, bf16[1024,256]{1,0:T(8,128)(2,1)S(1)}, u32[]{:S(2)}) copy-start(bf16[1024,256]{1,0:T(8,128)(2,1)S(1)} %get-tuple-element.92.gate_ref) | copy-start | bytes 1572868
  65.1 0.6 copy-start.6
  65.8 3.8 %copy-start.1 = (f32[8,1280]{1,0:T(8,128)S(1)}, f32[8,1280]{1,0:T(8,128)}, u32[]{:S(2)}) copy-start(f32[8,1280]{1,0:T(8,128)} %copy-done) | copy-start | bytes 122884
  65.8 3.8 %copy-start.3 = (bf16[1024,256]{1,0:T(8,128)(2,1)S(1)}, bf16[1024,256]{1,0:T(8,128)(2,1)}, u32[]{:S(2)}) copy-start(bf16[1024,256]{1,0:T(8,128)(2,1)} %copy-done.2) | copy-start | bytes 1572868
  65.8 3.8 %copy-start.7 = (bf16[128,256]{1,0:T(8,128)(2,1)S(1)}, bf16[128,256]{1,0:T(8,128)(2,1)}, u32[]{:S(2)}) copy-start(bf16[128,256]{1,0:T(8,128)(2,1)} %copy-done.6) | copy-start | bytes 196612

commit v12 on v9

--- a/solution.py
+++ b/solution.py
@@ -218,7 +218,8 @@
     send_ref[size : size + EXTRA, :] = rows_ref[...].astype(bf16)
 
 
-def join_kernel(own, total_ref, earlier_ref, send_ref):
+def join_kernel(own, total_ref, earlier_ref, send_ref, again_ref, same_ref):
+    same_ref[...] = total_ref[...]
     size = send_ref.shape[0] - EXTRA
     head_dim = size // own
     jumps = read_logs(total_ref[size:, :], own)
@@ -227,20 +228,19 @@
         state = jnp.exp(jumps[h]) * earlier_ref[rows, :].astype(f32)
         send_ref[rows, :] = (total_ref[rows, :].astype(f32) + state).astype(bf16)
     send_ref[size:, :] = jnp.zeros((EXTRA, send_ref.shape[1]), bf16)
-
-
-def combine_kernel(own, states_ref, near_ref, after_ref, far_ref, middle_ref, back_ref):
+    again_ref[...] = send_ref[...]
+
+
+def combine_kernel(own, states_ref, first_ref, after_b_ref, after_a_ref, near_ref, back_ref):
     size = back_ref.shape[1]
     head_dim = size // own
     logs = [read_logs(states_ref[m, size : size + EXTRA, :], own) for m in range(GROUP)]
-    near_jumps = read_logs(near_ref[size:, :], own)
-    middle_jumps = read_logs(middle_ref[size:, :], own)
+    jumps = read_logs(near_ref[size:, :], own)
     for h in range(own):
         rows = slice(h * head_dim, (h + 1) * head_dim)
-        state = middle_ref[rows, :].astype(f32)
-        state = state + jnp.exp(middle_jumps[h]) * far_ref[rows, :].astype(f32)
-        state = near_ref[rows, :].astype(f32) + jnp.exp(near_jumps[h]) * state
-        state = state + after_ref[rows, :].astype(f32)
+        after = after_a_ref[rows, :].astype(f32) + after_b_ref[rows, :].astype(f32)
+        state = first_ref[rows, :].astype(f32) + near_ref[rows, :].astype(f32)
+        state = state + jnp.exp(jumps[h]) * after
         for m in range(GROUP):
             back_ref[m, rows, :] = state.astype(bf16)
             state = jnp.exp(logs[m][h]) * state + states_ref[m, rows, :].astype(f32)
@@ -296,28 +296,25 @@
         for h in range(at // head_dim, (at + step) // head_dim):
             rows = slice(h * head_dim, (h + 1) * head_dim)
             own = gate[h * head_dim - at : (h + 1) * head_dim - at, :]
-            grown_ref[rows, :] = jnp.exp(cs_ref[h : h + 1, :]) * own
+            grown_ref[rows, :] = (jnp.exp(cs_ref[h : h + 1, :]) * own).astype(bf16)
             y_ref[rows, :] = y_ref[rows, :] * own
 
 
 def output_kernel(carried_ref, query_ref, grown_ref, y_ref, vec_ref, w_out_ref,
-                  out_ref, gated_ref, normed_ref, weight_ref, sem):
-    fetches = fetch_rows(w_out_ref, weight_ref, sem)
+                  out_ref, gated_ref, normed_ref):
     inner, length = y_ref.shape
     gated_ref[...] = jnp.dot(carried_ref[...], query_ref[...], preferred_element_type=f32)
     total = jnp.zeros((1, length), f32)
     for at in range(0, inner, EDGE):
         rows = slice(at, at + EDGE)
-        gated = y_ref[rows, :] + grown_ref[rows, :] * gated_ref[rows, :]
+        gated = y_ref[rows, :] + grown_ref[rows, :].astype(f32) * gated_ref[rows, :]
         gated_ref[rows, :] = gated
         total = total + jnp.sum(gated * gated, axis=0, keepdims=True)
     scale = lax.rsqrt(total / inner + epsilon)
     for at in range(0, inner, EDGE):
         gain = columns_of(vec_ref, at)[:, GAIN_OUT : GAIN_OUT + 1]
         normed_ref[at : at + EDGE, :] = (gated_ref[at : at + EDGE, :] * scale * gain).astype(bf16)
-    for fetch in fetches:
-        fetch.wait()
-    out_ref[...] = contract(normed_ref[...], weight_ref[...], ((0,), (0,))).astype(bf16)
+    out_ref[...] = contract(normed_ref[...], w_out_ref[...], ((0,), (0,))).astype(bf16)
 
 
 def call(kernel, outs, scratch, *args, fetched=()):
@@ -414,28 +411,28 @@
         states,
     )
     assert lax.axis_size("seq") == 4 * GROUP
-    near = passed_along(total, "seq", GROUP, members(0, 2))
-    middle = passed_along(total, "seq", 2 * GROUP, members(1))
-    far = passed_along(total, "seq", 3 * GROUP, members(0))
-    joined = call(
+    first = passed_along(total, "seq", GROUP, members(0))
+    joined, again, same = call(
         functools.partial(join_kernel, own),
-        shape((size + EXTRA, state_width), bf16),
+        [shape((size + EXTRA, state_width), bf16)] * 3,
         [],
-        total, near,
-    )
-    after = passed_along(joined, "seq", GROUP, members(1))
+        total, first,
+    )
+    after_b = passed_along(joined, "seq", 2 * GROUP, members(1))
+    after_a = passed_along(again, "seq", GROUP, members(1))
+    near = passed_along(same, "seq", GROUP, members(2))
     back = call(
         functools.partial(combine_kernel, own),
         shape((GROUP, size, state_width), bf16),
         [],
-        states, near, after, far, middle,
+        states, first, after_b, after_a, near,
     )
     back, act = lax.optimization_barrier((back, act))
     carried = within_groups(back).reshape(inner, state_width)
     grown, y, query = call(
         inside_kernel,
         [
-            shape((inner, length), f32),
+            shape((inner, length), bf16),
             shape((inner, length), f32),
             shape((state_width, length), bf16),
         ],
@@ -449,17 +446,22 @@
         normed, w_gate, act, act_first, dt, cs,
         fetched=(1,),
     )
+    grown, y, query, w_out = lax.optimization_barrier((grown, y, query, w_out))
+    (w_out,) = call(
+        stage_kernel,
+        [shape(w_out.shape, w_out.dtype)],
+        [pltpu.SemaphoreType.DMA((1,))],
+        w_out,
+        fetched=(0,),
+    )
     out = call(
         output_kernel,
         shape((length, w_out.shape[1]), bf16),
         [
             pltpu.VMEM((inner, length), f32),
             pltpu.VMEM((inner, length), bf16),
-            pltpu.VMEM(w_out.shape, bf16),
-            pltpu.SemaphoreType.DMA((PARTS,)),
         ],
         carried, query, grown, y, vec, w_out,
-        fetched=(5,),
     )
     return out[None]
 

time: 72.1 us -> 70.4 us (0.976)
  starting transfers between devices: 31.7 us -> 28.7 us
  waiting for transfers between devices: 11.3 us -> 10.4 us
  local copies, waits for them, and re-layouts: 0.81 us -> 1.6 us
    ppermute x5, starting transfers between devices: 18.4 us -> 16.3 us  [passed_along(): return lax.ppermute(block, axis, route)]
    all_to_all x1, waiting for transfers between devices: 6.17 us -> 4.91 us  [within_groups(): lax.all_to_all(blocks, 'seq', split_axis=0, concat_axis=0, tiled=True, ax...]
    all_to_all x1, starting transfers between devices: 5.61 us -> 4.65 us  [within_groups(): lax.all_to_all(blocks, 'seq', split_axis=0, concat_axis=0, tiled=True, ax...]
    unnamed x4 -> x8, local copies, waits for them, and re-layouts: 0.01 us -> 0.79 us
    pallas_call x8 -> x9, Pallas kernels: 10.2 us -> 10.9 us  [call(): pl.pallas_call(kernel, out_shape=outs, in_specs=[left if at in fetched el...]
  transfers between devices with their start and end apart: 7 -> 7, of which waited for: 3 -> 3; matrix products, arithmetic and copies ran while one was open for 2% -> 2% of each run, Pallas kernels for 8% -> 11%
where the time goes in v12:
time: 70.4 us; the launch traced here: 69.2 us
  starting transfers between devices  28.7 us (41%)
  blocking collectives  16.6 us (24%)
  Pallas kernels  10.9 us (15%)
  waiting for transfers between devices  10.4 us (15%)
  local copies, waits for them, and re-layouts  1.6 us (2%)
  other arithmetic  0.79 us (1%)
    all_to_all x1, blocking collectives, within_groups(): lax.all_to_all(blocks, 'seq', split_axis=0, concat_axis=0, tiled=True, ax...  16.6 us
    ppermute x5, starting transfers between devices, passed_along(): return lax.ppermute(block, axis, route)  16.3 us
    pallas_call x9, Pallas kernels, call(): pl.pallas_call(kernel, out_shape=outs, in_specs=[left if at in fetched el...  10.9 us
    all_to_all x1, starting transfers between devices, local(): lax.all_to_all(columns, 'table', split_axis=0, concat_axis=2, tiled=True)  7.72 us
    all_to_all x1, waiting for transfers between devices, within_groups(): lax.all_to_all(blocks, 'seq', split_axis=0, concat_axis=0, tiled=True, ax...  4.91 us
    all_to_all x1, starting transfers between devices, within_groups(): lax.all_to_all(blocks, 'seq', split_axis=0, concat_axis=0, tiled=True, ax...  4.65 us
    all_to_all x1, waiting for transfers between devices, local(): lax.all_to_all(columns, 'table', split_axis=0, concat_axis=2, tiled=True)  4.5 us
  transfers between devices with their start and end apart: 7, of which 3 were waited for; matrix products, arithmetic and copies ran while one was open for 2% of the time, Pallas kernels for 11%

profile of v12, /device:TPU:1, one launch (start us, length us, event | category | flops | bytes accessed | tf_op | source)
XLA Modules:
  0.0 69.2 jit_solution(17233708834983453669)
XLA Ops:
  0.0 0.0 copy-start.2
  0.0 0.0 copy-start.3
  0.0 7.7 %all-to-all-start = ((bf16[16,256,32]{1,2,0:T(8,128)(2,1)}), bf16[16,256,32]{1,2,0:T(8,128)(2,1)S(1)}, u32[]{:S(2)}, u32[]{:S(2)}) async-start(bf16[16,256,32]{1,2,0:T(8,128)(2,1)} %param.12), calls=%async_computation | async-start | bytes 524288 | tf_op jit(solution)/shard_map/all_to_all | solution.py:366
  7.7 0.7 %broadcast_in_dim.12 = f32[1,1280]{1,0:T(1,128)S(1)} reshape(f32[1280]{0:T(1024)} %param.20) | data formatting | bytes 10240 | tf_op jit(solution)/shard_map/broadcast_in_dim | solution.py:361
  8.4 0.8 %select_maximum_fusion = f32[7,1280]{1,0:T(8,128)S(1)} fusion(f32[1,1024]{1,0:T(1,128)} %bitcast.19, f32[1,512]{1,0:T(1,128)} %bitcast.20, f32[1,1280]{1,0:T(1,128)S(1)} %broadcast_in_dim.12, f32[4,1280]{1,0:T(4,128)} %param.19), kind=kLoop, calls=%fused_computation.2 | loop fusion | flops 80640 | bytes 67584 | tf_op jit(solution)/shard_map/concatenate | solution.py:362
  9.2 1.4 %shard_map.118 = (bf16[512,1280]{1,0:T(8,128)(2,1)S(1)}, bf16[16,512]{1,0:T(8,128)(2,1)S(1)}, f32[1,256]{1,0:T(1,128)S(1)}) custom-call(bf16[512,1280]{1,0:T(8,128)(2,1)} %refs_0_.1, bf16[16,512]{1,0:T(8,128)(2,1)} %bitcast.18, f32[1,256]{1,0:T(1,128)} %refs_2_.1), custom_call_target="tpu_custom_call" | custom-call | tf_op jit(solution)/shard_map/pallas_call | solution.py:328
  10.6 0.0 copy-done.2
  10.6 0.0 copy-done.3
  10.6 4.5 %all-to-all-done = bf16[16,256,32]{1,2,0:T(8,128)(2,1)S(1)} async-done(((bf16[16,256,32]{1,2,0:T(8,128)(2,1)}), bf16[16,256,32]{1,2,0:T(8,128)(2,1)S(1)}, u32[]{:S(2)}, u32[]{:S(2)}) %all-to-all-start) | async-done | bytes 262176 | tf_op jit(solution)/shard_map/all_to_all | solution.py:366
  15.1 5.5 %collective-permute-start = (bf16[512,128]{1,0:T(8,128)(2,1)S(1)}, bf16[512,128]{1,0:T(8,128)(2,1)S(1)}, u32[]{:S(2)}, u32[]{:S(2)}) collective-permute-start(bf16[512,128]{1,0:T(8,128)(2,1)S(1)} %slice.4), channel_id=1, source_target_pairs={{0,16},{16,32},{32,48},{48,64},{64,80},{80,96},{96,112},{112,128},... | collective-permute-start | bytes 393224 | tf_op jit(solution)/shard_map/ppermute | solution.py:23
  20.6 0.1 copy.15.head_ref
  20.7 2.1 %shard_map.119 = (bf16[512,256]{1,0:T(8,128)(2,1)S(1)}, bf16[1280,256]{1,0:T(8,128)(2,1)S(1)}, f32[16,256]{1,0:T(8,128)S(1)}, f32[16,256]{1,0:T(8,128)S(1)}, f32...) custom-call(bf16[512,256]{1,0:T(8,128)(2,1)S(1)} %bitcast.16, ...), custom_call_target="tpu_custom_call" | custom-call | tf_op jit(solution)/shard_map/pallas_call | solution.py:328
  22.9 0.0 collective-permute-done.edge_ref
  22.9 0.8 %shard_map.120 = (bf16[8,136,128]{2,1,0:T(8,128)(2,1)S(1)}, f32[8,1280]{1,0:T(8,128)S(1)}) custom-call(bf16[512,128]{1,0:T(8,128)(2,1)S(1)} %collective-permute-done.edge_ref, f32[8,1280]{1,0:T(8,128)S(1)} %get-tuple-element.45.first_ref, f32[8,1280]{1,0:T(8,128)S(1)} %pad.14.vec_ref, bf16[512,1280]{1,0:T(8,128)(2,1)S(1)} %get-tuple-element.41.w_xbc_ref, ...), custom_call_target="tpu_custom_call" | custom-call | tf_op jit(solution)/shard_map/pallas_call | solution.py:328
  23.7 16.6 %all_to_all.28.states_ref = bf16[8,136,128]{2,1,0:T(8,128)(2,1)S(1)} all-to-all(bf16[8,136,128]{2,1,0:T(8,128)(2,1)S(1)} %get-tuple-element.49), channel_id=1, replica_groups={{0,16,32,48,64,80,96,112},{128,144,160,176,192,208,224,240},{256,272,28..., dimensions={0} | all-to-all | bytes 557056 | tf_op jit(solution)/shard_map/all_to_all | solution.py:33
  40.3 0.1 shard_map.121.total_ref
  40.4 8.8 %collective-permute-start.1 = (bf16[136,128]{1,0:T(8,128)(2,1)S(1)}, bf16[136,128]{1,0:T(8,128)(2,1)S(1)}, u32[]{:S(2)}, u32[]{:S(2)}) collective-permute-start(bf16[136,128]{1,0:T(8,128)(2,1)S(1)} %shard_map.121.total_ref), channel_id=1, source_target_pairs={{0,128},{16,144},{32,160},{48,176},{64,192},{80,208},{96,224},{112... | collective-permute-start | bytes 104456 | tf_op jit(solution)/shard_map/ppermute | solution.py:23
  49.2 1.0 %collective-permute-done.1.earlier_ref.first_ref = bf16[136,128]{1,0:T(8,128)(2,1)S(1)} collective-permute-done((bf16[136,128]{1,0:T(8,128)(2,1)S(1)}, bf16[136,128]{1,0:T(8,128)(2,1)S(1)}, u32[]{:S(2)}, u32[]{:S(2)}) %collective-permute-start.1) | collective-permute-done | bytes 34848 | tf_op jit(solution)/shard_map/ppermute | solution.py:23
  50.3 0.7 collective-permute-start.2
  50.9 0.7 collective-permute-start.3
  51.6 0.7 collective-permute-start.4
  52.3 0.0 collective-permute-done.2.after_b_ref
  52.3 0.0 collective-permute-done.3.after_a_ref
  52.3 0.0 collective-permute-done.4.near_ref
  52.3 0.8 %shard_map.123 = bf16[8,128,128]{2,1,0:T(8,128)(2,1)} custom-call(bf16[8,136,128]{2,1,0:T(8,128)(2,1)S(1)} %all_to_all.28.states_ref, bf16[136,128]{1,0:T(8,128)(2,1)S(1)} %collective-permute-done.1.earlier_ref.first_ref, bf16[136,128]{1,0:T(8,128)(2,1)S(1)} %collective-permute-done.2.after_b_ref, bf16[136,128]{1,0:T(8,128)(2,1)S(1)} %collective-permute-done.3.after_a_ref, ...), custom_call_target="tpu_custom_call" | custom-call | tf_op jit(solution)/shard_map/pallas_call | solution.py:328
  53.1 4.7 %all-to-all-start.2 = ((bf16[8,128,128]{2,1,0:T(8,128)(2,1)}), bf16[8,128,128]{2,1,0:T(8,128)(2,1)S(1)}, u32[]{:S(2)}, u32[]{:S(2)}) async-start(bf16[8,128,128]{2,1,0:T(8,128)(2,1)} %shard_map.123), calls=%async_computation.2 | async-start | bytes 524288 | tf_op jit(solution)/shard_map/all_to_all | solution.py:33
  57.7 2.6 %shard_map.124 = (bf16[1024,256]{1,0:T(8,128)(2,1)S(1)}, f32[1024,256]{1,0:T(8,128)S(1)}, bf16[128,256]{1,0:T(8,128)(2,1)S(1)}) custom-call(bf16[512,256]{1,0:T(8,128)(2,1)S(1)} %get-tuple-element.55.normed_ref, bf16[512,1024]{1,0:T(8,128)(2,1)} %w_gate_ref.1, bf16[1280,256]{1,0:T(8,128)(2,1)S(1)} %get-tuple-element.56.main_ref, ...), custom_call_target="tpu_custom_call" | custom-call | tf_op jit(solution)/shard_map/pallas_call | solution.py:328
  60.3 0.0 copy-start
  60.3 0.8 %copy-done = bf16[1024,256]{1,0:T(8,128)(2,1)} copy-done((bf16[1024,256]{1,0:T(8,128)(2,1)}, bf16[1024,256]{1,0:T(8,128)(2,1)S(1)}, u32[]{:S(2)}) %copy-start) | copy-done | bytes 524312
  61.1 0.0 copy-start.1
  61.1 1.3 %shard_map.125.w_out_ref = bf16[1024,512]{1,0:T(8,128)(2,1)S(1)} custom-call(bf16[1024,512]{1,0:T(8,128)(2,1)} %refs_0_.2), custom_call_target="tpu_custom_call" | custom-call | tf_op jit(solution)/shard_map/pallas_call | solution.py:328
  62.4 4.9 %all-to-all-done.2 = bf16[8,128,128]{2,1,0:T(8,128)(2,1)S(1)} async-done(((bf16[8,128,128]{2,1,0:T(8,128)(2,1)}), bf16[8,128,128]{2,1,0:T(8,128)(2,1)S(1)}, u32[]{:S(2)}, u32[]{:S(2)}) %all-to-all-start.2) | async-done | bytes 262176 | tf_op jit(solution)/shard_map/all_to_all | solution.py:33
  67.3 0.0 copy-done.1
  67.3 1.9 %shard_map.126 = bf16[256,512]{1,0:T(8,128)(2,1)} custom-call(bf16[1024,128]{1,0:T(8,128)(2,1)S(1)} %bitcast.17, bf16[128,256]{1,0:T(8,128)(2,1)S(1)} %get-tuple-element.63.query_ref, bf16[1024,256]{1,0:T(8,128)(2,1)S(1)} %copy-done.1, f32[1024,256]{1,0:T(8,128)S(1)} %get-tuple-element.65.y_ref, f32[8,1280]{1,0:T(8,128)S(1)} %pad.14.vec_ref, ...), custom_call_target="tpu_custom_call" | custom-call | tf_op jit(solution)/shard_map/pallas_call | solution.py:328
  (4 shorter events, 0.1 us)
Async XLA Ops:
  0.0 10.6 %copy-start.2 = (f32[16]{0:T(128)S(1)}, f32[16]{0:T(128)}, u32[]{:S(2)}) copy-start(f32[16]{0:T(128)} %param.21) | copy-start | bytes 196
  0.0 10.6 %copy-start.3 = (f32[16]{0:T(128)S(1)}, f32[16]{0:T(128)}, u32[]{:S(2)}) copy-start(f32[16]{0:T(128)} %param.18) | copy-start | bytes 196
  0.0 15.1 %all-to-all-start = ((bf16[16,256,32]{1,2,0:T(8,128)(2,1)}), bf16[16,256,32]{1,2,0:T(8,128)(2,1)S(1)}, u32[]{:S(2)}, u32[]{:S(2)}) async-start(bf16[16,256,32]{1,2,0:T(8,128)(2,1)} %param.12), calls=%async_computation | async-start | bytes 524288 | tf_op jit(solution)/shard_map/all_to_all | solution.py:366
  15.1 7.7 %collective-permute-start = (bf16[512,128]{1,0:T(8,128)(2,1)S(1)}, bf16[512,128]{1,0:T(8,128)(2,1)S(1)}, u32[]{:S(2)}, u32[]{:S(2)}) collective-permute-start(bf16[512,128]{1,0:T(8,128)(2,1)S(1)} %slice.4), channel_id=1, source_target_pairs={{0,16},{16,32},{32,48},{48,64},{64,80},{80,96},{96,112},{112,128},... | collective-permute-start | bytes 393224 | tf_op jit(solution)/shard_map/ppermute | solution.py:23
  40.4 9.8 %collective-permute-start.1 = (bf16[136,128]{1,0:T(8,128)(2,1)S(1)}, bf16[136,128]{1,0:T(8,128)(2,1)S(1)}, u32[]{:S(2)}, u32[]{:S(2)}) collective-permute-start(bf16[136,128]{1,0:T(8,128)(2,1)S(1)} %shard_map.121.total_ref), channel_id=1, source_target_pairs={{0,128},{16,144},{32,160},{48,176},{64,192},{80,208},{96,224},{112... | collective-permute-start | bytes 104456 | tf_op jit(solution)/shard_map/ppermute | solution.py:23
  50.3 2.0 %collective-permute-start.2 = (bf16[136,128]{1,0:T(8,128)(2,1)S(1)}, bf16[136,128]{1,0:T(8,128)(2,1)S(1)}, u32[]{:S(2)}, u32[]{:S(2)}) collective-permute-start(bf16[136,128]{1,0:T(8,128)(2,1)S(1)} %get-tuple-element.50), channel_id=1, source_target_pairs={{128,384},{144,400},{160,416},{176,432},{192,448},{208,464},{224,4... | collective-permute-start | bytes 104456 | tf_op jit(solution)/shard_map/ppermute | solution.py:23
  50.9 1.4 %collective-permute-start.3 = (bf16[136,128]{1,0:T(8,128)(2,1)S(1)}, bf16[136,128]{1,0:T(8,128)(2,1)S(1)}, u32[]{:S(2)}, u32[]{:S(2)}) collective-permute-start(bf16[136,128]{1,0:T(8,128)(2,1)S(1)} %get-tuple-element.51), channel_id=1, source_target_pairs={{128,256},{144,272},{160,288},{176,304},{192,320},{208,336},{224,3... | collective-permute-start | bytes 104456 | tf_op jit(solution)/shard_map/ppermute | solution.py:23
  51.6 0.7 %collective-permute-start.4 = (bf16[136,128]{1,0:T(8,128)(2,1)S(1)}, bf16[136,128]{1,0:T(8,128)(2,1)S(1)}, u32[]{:S(2)}, u32[]{:S(2)}) collective-permute-start(bf16[136,128]{1,0:T(8,128)(2,1)S(1)} %get-tuple-element.52), channel_id=1, source_target_pairs={{256,384},{272,400},{288,416},{304,432},{320,448},{336,464},{352,4... | collective-permute-start | bytes 104456 | tf_op jit(solution)/shard_map/ppermute | solution.py:23
  53.1 14.2 %all-to-all-start.2 = ((bf16[8,128,128]{2,1,0:T(8,128)(2,1)}), bf16[8,128,128]{2,1,0:T(8,128)(2,1)S(1)}, u32[]{:S(2)}, u32[]{:S(2)}) async-start(bf16[8,128,128]{2,1,0:T(8,128)(2,1)} %shard_map.123), calls=%async_computation.2 | async-start | bytes 524288 | tf_op jit(solution)/shard_map/all_to_all | solution.py:33
  60.3 0.8 %copy-start = (bf16[1024,256]{1,0:T(8,128)(2,1)}, bf16[1024,256]{1,0:T(8,128)(2,1)S(1)}, u32[]{:S(2)}) copy-start(bf16[1024,256]{1,0:T(8,128)(2,1)S(1)} %get-tuple-element.64.grown_ref) | copy-start | bytes 1572868
  61.1 6.2 %copy-start.1 = (bf16[1024,256]{1,0:T(8,128)(2,1)S(1)}, bf16[1024,256]{1,0:T(8,128)(2,1)}, u32[]{:S(2)}) copy-start(bf16[1024,256]{1,0:T(8,128)(2,1)} %copy-done) | copy-start | bytes 1572868

commit v13 on v12

--- a/solution.py
+++ b/solution.py
@@ -152,11 +152,17 @@
     first_ref[...] = shift_ref[EXTRA : 2 * EXTRA, :]
 
 
+def last_kernel(x_ref, last_ref):
+    length = x_ref.shape[1]
+    last = x_ref[:, length - EDGE :].astype(f32).T
+    last_ref[...] = last[EDGE - EXTRA :, :].astype(bf16)
+
+
 def edge_kernel(edge_ref, first_ref, vec_ref, w_xbc_ref, coef_ref, state_ref, logs_ref,
                 send_ref, act_ref, rows_ref):
     inner, state_width = state_ref.shape
-    depth = edge_ref.shape[0]
-    x = edge_ref[...].astype(f32).T[EDGE - EXTRA :, :]
+    depth = edge_ref.shape[1]
+    x = edge_ref[...].astype(f32)
     scale = lax.rsqrt(jnp.mean(x * x, axis=1, keepdims=True) + epsilon)
     normed = (x * scale * vec_ref[GAIN_IN : GAIN_IN + 1, :depth]).astype(bf16)
     before = jnp.dot(normed, w_xbc_ref[...], preferred_element_type=f32)
@@ -375,7 +381,7 @@
     whole, vec, head, *staged = lax.optimization_barrier((whole, vec, head, *staged))
     w_xbc, w_step_t, gaps = staged
     x = whole.reshape(length, depth).T
-    edge = passed_along(x[:, length - EDGE :], "seq", 1)
+    edge = passed_along(call(last_kernel, shape((EXTRA, depth), bf16), [], x), "seq", 1)
     normed, act, dt, cs, state, logs, first, coef_first = call(
         main_kernel,
         [

time: 70.4 us -> 70.4 us (level)
    pallas_call x9 -> x10, Pallas kernels: 10.9 us -> 10.9 us  [call(): pl.pallas_call(kernel, out_shape=outs, in_specs=[left if at in fetched el...]
where the time goes in v13:
time: 70.4 us; the launch traced here: 69.2 us
  starting transfers between devices  28.7 us (41%)
  blocking collectives  16.6 us (24%)
  Pallas kernels  10.9 us (15%)
  waiting for transfers between devices  10.4 us (15%)
  local copies, waits for them, and re-layouts  1.59 us (2%)
  other arithmetic  0.79 us (1%)
    all_to_all x1, blocking collectives, within_groups(): lax.all_to_all(blocks, 'seq', split_axis=0, concat_axis=0, tiled=True, ax...  16.6 us
    ppermute x5, starting transfers between devices, passed_along(): return lax.ppermute(block, axis, route)  16.3 us
    pallas_call x10, Pallas kernels, call(): pl.pallas_call(kernel, out_shape=outs, in_specs=[left if at in fetched el...  10.9 us
    all_to_all x1, starting transfers between devices, local(): lax.all_to_all(columns, 'table', split_axis=0, concat_axis=2, tiled=True)  7.72 us
    all_to_all x1, waiting for transfers between devices, within_groups(): lax.all_to_all(blocks, 'seq', split_axis=0, concat_axis=0, tiled=True, ax...  4.91 us
    all_to_all x1, starting transfers between devices, within_groups(): lax.all_to_all(blocks, 'seq', split_axis=0, concat_axis=0, tiled=True, ax...  4.65 us
    all_to_all x1, waiting for transfers between devices, local(): lax.all_to_all(columns, 'table', split_axis=0, concat_axis=2, tiled=True)  4.5 us
  transfers between devices with their start and end apart: 7, of which 3 were waited for; matrix products, arithmetic and copies ran while one was open for 2% of the time, Pallas kernels for 11%

profile of v13, /device:TPU:1, one launch (start us, length us, event | category | flops | bytes accessed | tf_op | source)
XLA Modules:
  0.0 69.2 jit_solution(17723299060130574366)
XLA Ops:
  0.0 0.0 copy-start.2
  0.0 0.0 copy-start.3
  0.0 7.7 %all-to-all-start = ((bf16[16,256,32]{1,2,0:T(8,128)(2,1)}), bf16[16,256,32]{1,2,0:T(8,128)(2,1)S(1)}, u32[]{:S(2)}, u32[]{:S(2)}) async-start(bf16[16,256,32]{1,2,0:T(8,128)(2,1)} %param.12), calls=%async_computation | async-start | bytes 524288 | tf_op jit(solution)/shard_map/all_to_all | solution.py:372
  7.7 0.7 %broadcast_in_dim.12 = f32[1,1280]{1,0:T(1,128)S(1)} reshape(f32[1280]{0:T(1024)} %param.20) | data formatting | bytes 10240 | tf_op jit(solution)/shard_map/broadcast_in_dim | solution.py:367
  8.4 0.8 %select_maximum_fusion = f32[7,1280]{1,0:T(8,128)S(1)} fusion(f32[1,1024]{1,0:T(1,128)} %bitcast.19, f32[1,512]{1,0:T(1,128)} %bitcast.20, f32[1,1280]{1,0:T(1,128)S(1)} %broadcast_in_dim.12, f32[4,1280]{1,0:T(4,128)} %param.19), kind=kLoop, calls=%fused_computation.2 | loop fusion | flops 80640 | bytes 67584 | tf_op jit(solution)/shard_map/concatenate | solution.py:368
  9.2 1.4 %shard_map.118 = (bf16[512,1280]{1,0:T(8,128)(2,1)S(1)}, bf16[16,512]{1,0:T(8,128)(2,1)S(1)}, f32[1,256]{1,0:T(1,128)S(1)}) custom-call(bf16[512,1280]{1,0:T(8,128)(2,1)} %refs_0_.1, bf16[16,512]{1,0:T(8,128)(2,1)} %bitcast.18, f32[1,256]{1,0:T(1,128)} %refs_2_.1), custom_call_target="tpu_custom_call" | custom-call | tf_op jit(solution)/shard_map/pallas_call | solution.py:334
  10.6 0.0 copy-done.2
  10.6 0.0 copy-done.3
  10.6 4.5 %all-to-all-done = bf16[16,256,32]{1,2,0:T(8,128)(2,1)S(1)} async-done(((bf16[16,256,32]{1,2,0:T(8,128)(2,1)}), bf16[16,256,32]{1,2,0:T(8,128)(2,1)S(1)}, u32[]{:S(2)}, u32[]{:S(2)}) %all-to-all-start) | async-done | bytes 262176 | tf_op jit(solution)/shard_map/all_to_all | solution.py:372
  15.1 0.1 shard_map.119
  15.2 5.5 %collective-permute-start = (bf16[8,512]{1,0:T(8,128)(2,1)S(1)}, bf16[8,512]{1,0:T(8,128)(2,1)S(1)}, u32[]{:S(2)}, u32[]{:S(2)}) collective-permute-start(bf16[8,512]{1,0:T(8,128)(2,1)S(1)} %shard_map.119), channel_id=1, source_target_pairs={{0,16},{16,32},{32,48},{48,64},{64,80},{80,96},{96,112},{112,128},... | collective-permute-start | bytes 24584 | tf_op jit(solution)/shard_map/ppermute | solution.py:23
  20.7 0.1 copy.15.head_ref
  20.8 2.1 %shard_map.120 = (bf16[512,256]{1,0:T(8,128)(2,1)S(1)}, bf16[1280,256]{1,0:T(8,128)(2,1)S(1)}, f32[16,256]{1,0:T(8,128)S(1)}, f32[16,256]{1,0:T(8,128)S(1)}, f32...) custom-call(bf16[512,256]{1,0:T(8,128)(2,1)S(1)} %bitcast.16, ...), custom_call_target="tpu_custom_call" | custom-call | tf_op jit(solution)/shard_map/pallas_call | solution.py:334
  22.9 0.0 collective-permute-done.edge_ref
  23.0 0.7 %shard_map.121 = (bf16[8,136,128]{2,1,0:T(8,128)(2,1)S(1)}, f32[8,1280]{1,0:T(8,128)S(1)}) custom-call(bf16[8,512]{1,0:T(8,128)(2,1)S(1)} %collective-permute-done.edge_ref, f32[8,1280]{1,0:T(8,128)S(1)} %get-tuple-element.45.first_ref, f32[8,1280]{1,0:T(8,128)S(1)} %pad.14.vec_ref, bf16[512,1280]{1,0:T(8,128)(2,1)S(1)} %get-tuple-element.41.w_xbc_ref, ...), custom_call_target="tpu_custom_call" | custom-call | tf_op jit(solution)/shard_map/pallas_call | solution.py:334
  23.6 16.6 %all_to_all.28.states_ref = bf16[8,136,128]{2,1,0:T(8,128)(2,1)S(1)} all-to-all(bf16[8,136,128]{2,1,0:T(8,128)(2,1)S(1)} %get-tuple-element.49), channel_id=1, replica_groups={{0,16,32,48,64,80,96,112},{128,144,160,176,192,208,224,240},{256,272,28..., dimensions={0} | all-to-all | bytes 557056 | tf_op jit(solution)/shard_map/all_to_all | solution.py:33
  40.3 0.1 shard_map.122.total_ref
  40.4 8.8 %collective-permute-start.1 = (bf16[136,128]{1,0:T(8,128)(2,1)S(1)}, bf16[136,128]{1,0:T(8,128)(2,1)S(1)}, u32[]{:S(2)}, u32[]{:S(2)}) collective-permute-start(bf16[136,128]{1,0:T(8,128)(2,1)S(1)} %shard_map.122.total_ref), channel_id=1, source_target_pairs={{0,128},{16,144},{32,160},{48,176},{64,192},{80,208},{96,224},{112... | collective-permute-start | bytes 104456 | tf_op jit(solution)/shard_map/ppermute | solution.py:23
  49.2 1.0 %collective-permute-done.1.earlier_ref.first_ref = bf16[136,128]{1,0:T(8,128)(2,1)S(1)} collective-permute-done((bf16[136,128]{1,0:T(8,128)(2,1)S(1)}, bf16[136,128]{1,0:T(8,128)(2,1)S(1)}, u32[]{:S(2)}, u32[]{:S(2)}) %collective-permute-start.1) | collective-permute-done | bytes 34848 | tf_op jit(solution)/shard_map/ppermute | solution.py:23
  50.2 0.7 collective-permute-start.2
  50.9 0.7 collective-permute-start.3
  51.6 0.7 collective-permute-start.4
  52.3 0.0 collective-permute-done.2.after_b_ref
  52.3 0.0 collective-permute-done.3.after_a_ref
  52.3 0.0 collective-permute-done.4.near_ref
  52.3 0.8 %shard_map.124 = bf16[8,128,128]{2,1,0:T(8,128)(2,1)} custom-call(bf16[8,136,128]{2,1,0:T(8,128)(2,1)S(1)} %all_to_all.28.states_ref, bf16[136,128]{1,0:T(8,128)(2,1)S(1)} %collective-permute-done.1.earlier_ref.first_ref, bf16[136,128]{1,0:T(8,128)(2,1)S(1)} %collective-permute-done.2.after_b_ref, bf16[136,128]{1,0:T(8,128)(2,1)S(1)} %collective-permute-done.3.after_a_ref, ...), custom_call_target="tpu_custom_call" | custom-call | tf_op jit(solution)/shard_map/pallas_call | solution.py:334
  53.1 4.7 %all-to-all-start.2 = ((bf16[8,128,128]{2,1,0:T(8,128)(2,1)}), bf16[8,128,128]{2,1,0:T(8,128)(2,1)S(1)}, u32[]{:S(2)}, u32[]{:S(2)}) async-start(bf16[8,128,128]{2,1,0:T(8,128)(2,1)} %shard_map.124), calls=%async_computation.2 | async-start | bytes 524288 | tf_op jit(solution)/shard_map/all_to_all | solution.py:33
  57.7 2.6 %shard_map.125 = (bf16[1024,256]{1,0:T(8,128)(2,1)S(1)}, f32[1024,256]{1,0:T(8,128)S(1)}, bf16[128,256]{1,0:T(8,128)(2,1)S(1)}) custom-call(bf16[512,256]{1,0:T(8,128)(2,1)S(1)} %get-tuple-element.55.normed_ref, bf16[512,1024]{1,0:T(8,128)(2,1)} %w_gate_ref.1, bf16[1280,256]{1,0:T(8,128)(2,1)S(1)} %get-tuple-element.56.main_ref, ...), custom_call_target="tpu_custom_call" | custom-call | tf_op jit(solution)/shard_map/pallas_call | solution.py:334
  60.3 0.0 copy-start
  60.3 0.8 %copy-done = bf16[1024,256]{1,0:T(8,128)(2,1)} copy-done((bf16[1024,256]{1,0:T(8,128)(2,1)}, bf16[1024,256]{1,0:T(8,128)(2,1)S(1)}, u32[]{:S(2)}) %copy-start) | copy-done | bytes 524312
  61.1 0.0 copy-start.1
  61.1 1.3 %shard_map.126.w_out_ref = bf16[1024,512]{1,0:T(8,128)(2,1)S(1)} custom-call(bf16[1024,512]{1,0:T(8,128)(2,1)} %refs_0_.2), custom_call_target="tpu_custom_call" | custom-call | tf_op jit(solution)/shard_map/pallas_call | solution.py:334
  62.4 4.9 %all-to-all-done.2 = bf16[8,128,128]{2,1,0:T(8,128)(2,1)S(1)} async-done(((bf16[8,128,128]{2,1,0:T(8,128)(2,1)}), bf16[8,128,128]{2,1,0:T(8,128)(2,1)S(1)}, u32[]{:S(2)}, u32[]{:S(2)}) %all-to-all-start.2) | async-done | bytes 262176 | tf_op jit(solution)/shard_map/all_to_all | solution.py:33
  67.3 0.0 copy-done.1
  67.3 1.8 %shard_map.127 = bf16[256,512]{1,0:T(8,128)(2,1)} custom-call(bf16[1024,128]{1,0:T(8,128)(2,1)S(1)} %bitcast.17, bf16[128,256]{1,0:T(8,128)(2,1)S(1)} %get-tuple-element.63.query_ref, bf16[1024,256]{1,0:T(8,128)(2,1)S(1)} %copy-done.1, f32[1024,256]{1,0:T(8,128)S(1)} %get-tuple-element.65.y_ref, f32[8,1280]{1,0:T(8,128)S(1)} %pad.14.vec_ref, ...), custom_call_target="tpu_custom_call" | custom-call | tf_op jit(solution)/shard_map/pallas_call | solution.py:334
  (3 shorter events, 0.0 us)
Async XLA Ops:
  0.0 10.6 %copy-start.2 = (f32[16]{0:T(128)S(1)}, f32[16]{0:T(128)}, u32[]{:S(2)}) copy-start(f32[16]{0:T(128)} %param.21) | copy-start | bytes 196
  0.0 10.6 %copy-start.3 = (f32[16]{0:T(128)S(1)}, f32[16]{0:T(128)}, u32[]{:S(2)}) copy-start(f32[16]{0:T(128)} %param.18) | copy-start | bytes 196
  0.0 15.1 %all-to-all-start = ((bf16[16,256,32]{1,2,0:T(8,128)(2,1)}), bf16[16,256,32]{1,2,0:T(8,128)(2,1)S(1)}, u32[]{:S(2)}, u32[]{:S(2)}) async-start(bf16[16,256,32]{1,2,0:T(8,128)(2,1)} %param.12), calls=%async_computation | async-start | bytes 524288 | tf_op jit(solution)/shard_map/all_to_all | solution.py:372
  15.2 7.7 %collective-permute-start = (bf16[8,512]{1,0:T(8,128)(2,1)S(1)}, bf16[8,512]{1,0:T(8,128)(2,1)S(1)}, u32[]{:S(2)}, u32[]{:S(2)}) collective-permute-start(bf16[8,512]{1,0:T(8,128)(2,1)S(1)} %shard_map.119), channel_id=1, source_target_pairs={{0,16},{16,32},{32,48},{48,64},{64,80},{80,96},{96,112},{112,128},... | collective-permute-start | bytes 24584 | tf_op jit(solution)/shard_map/ppermute | solution.py:23
  40.4 9.8 %collective-permute-start.1 = (bf16[136,128]{1,0:T(8,128)(2,1)S(1)}, bf16[136,128]{1,0:T(8,128)(2,1)S(1)}, u32[]{:S(2)}, u32[]{:S(2)}) collective-permute-start(bf16[136,128]{1,0:T(8,128)(2,1)S(1)} %shard_map.122.total_ref), channel_id=1, source_target_pairs={{0,128},{16,144},{32,160},{48,176},{64,192},{80,208},{96,224},{112... | collective-permute-start | bytes 104456 | tf_op jit(solution)/shard_map/ppermute | solution.py:23
  50.2 2.0 %collective-permute-start.2 = (bf16[136,128]{1,0:T(8,128)(2,1)S(1)}, bf16[136,128]{1,0:T(8,128)(2,1)S(1)}, u32[]{:S(2)}, u32[]{:S(2)}) collective-permute-start(bf16[136,128]{1,0:T(8,128)(2,1)S(1)} %get-tuple-element.50), channel_id=1, source_target_pairs={{128,384},{144,400},{160,416},{176,432},{192,448},{208,464},{224,4... | collective-permute-start | bytes 104456 | tf_op jit(solution)/shard_map/ppermute | solution.py:23
  50.9 1.4 %collective-permute-start.3 = (bf16[136,128]{1,0:T(8,128)(2,1)S(1)}, bf16[136,128]{1,0:T(8,128)(2,1)S(1)}, u32[]{:S(2)}, u32[]{:S(2)}) collective-permute-start(bf16[136,128]{1,0:T(8,128)(2,1)S(1)} %get-tuple-element.51), channel_id=1, source_target_pairs={{128,256},{144,272},{160,288},{176,304},{192,320},{208,336},{224,3... | collective-permute-start | bytes 104456 | tf_op jit(solution)/shard_map/ppermute | solution.py:23
  51.6 0.7 %collective-permute-start.4 = (bf16[136,128]{1,0:T(8,128)(2,1)S(1)}, bf16[136,128]{1,0:T(8,128)(2,1)S(1)}, u32[]{:S(2)}, u32[]{:S(2)}) collective-permute-start(bf16[136,128]{1,0:T(8,128)(2,1)S(1)} %get-tuple-element.52), channel_id=1, source_target_pairs={{256,384},{272,400},{288,416},{304,432},{320,448},{336,464},{352,4... | collective-permute-start | bytes 104456 | tf_op jit(solution)/shard_map/ppermute | solution.py:23
  53.1 14.2 %all-to-all-start.2 = ((bf16[8,128,128]{2,1,0:T(8,128)(2,1)}), bf16[8,128,128]{2,1,0:T(8,128)(2,1)S(1)}, u32[]{:S(2)}, u32[]{:S(2)}) async-start(bf16[8,128,128]{2,1,0:T(8,128)(2,1)} %shard_map.124), calls=%async_computation.2 | async-start | bytes 524288 | tf_op jit(solution)/shard_map/all_to_all | solution.py:33
  60.3 0.8 %copy-start = (bf16[1024,256]{1,0:T(8,128)(2,1)}, bf16[1024,256]{1,0:T(8,128)(2,1)S(1)}, u32[]{:S(2)}) copy-start(bf16[1024,256]{1,0:T(8,128)(2,1)S(1)} %get-tuple-element.64.grown_ref) | copy-start | bytes 1572868
  61.1 6.2 %copy-start.1 = (bf16[1024,256]{1,0:T(8,128)(2,1)S(1)}, bf16[1024,256]{1,0:T(8,128)(2,1)}, u32[]{:S(2)}) copy-start(bf16[1024,256]{1,0:T(8,128)(2,1)} %copy-done) | copy-start | bytes 1572868

commit v14 on v13

--- a/solution.py
+++ b/solution.py
@@ -139,12 +139,12 @@
 
     b, _ = act_of(inner, state_width)
     act_of(inner + state_width, state_width)
-    step = 2 * head_dim
+    step = 4 * head_dim
     for at in range(0, inner, step):
         act = act_of(at, step)[1].astype(f32)
         head = at // head_dim
         coef = jnp.concatenate(
-            [jnp.broadcast_to(coef_ref[h : h + 1, :], (head_dim, length)) for h in (head, head + 1)],
+            [jnp.broadcast_to(coef_ref[h : h + 1, :], (head_dim, length)) for h in range(head, head + 4)],
             axis=0,
         )
         weighted_ref[at : at + step, :] = (act * coef).astype(bf16)

time: 70.4 us -> 70.3 us (level)
  no operation moved by 1% of the time
where the time goes in v14:
time: 70.3 us; the launch traced here: 69.1 us
  starting transfers between devices  28.7 us (41%)
  blocking collectives  16.6 us (24%)
  Pallas kernels  10.9 us (16%)
  waiting for transfers between devices  10.4 us (15%)
  local copies, waits for them, and re-layouts  1.59 us (2%)
  other arithmetic  0.79 us (1%)
    all_to_all x1, blocking collectives, within_groups(): lax.all_to_all(blocks, 'seq', split_axis=0, concat_axis=0, tiled=True, ax...  16.6 us
    ppermute x5, starting transfers between devices, passed_along(): return lax.ppermute(block, axis, route)  16.3 us
    pallas_call x10, Pallas kernels, call(): pl.pallas_call(kernel, out_shape=outs, in_specs=[left if at in fetched el...  10.9 us
    all_to_all x1, starting transfers between devices, local(): lax.all_to_all(columns, 'table', split_axis=0, concat_axis=2, tiled=True)  7.72 us
    all_to_all x1, waiting for transfers between devices, within_groups(): lax.all_to_all(blocks, 'seq', split_axis=0, concat_axis=0, tiled=True, ax...  4.9 us
    all_to_all x1, starting transfers between devices, within_groups(): lax.all_to_all(blocks, 'seq', split_axis=0, concat_axis=0, tiled=True, ax...  4.65 us
    all_to_all x1, waiting for transfers between devices, local(): lax.all_to_all(columns, 'table', split_axis=0, concat_axis=2, tiled=True)  4.5 us
  transfers between devices with their start and end apart: 7, of which 3 were waited for; matrix products, arithmetic and copies ran while one was open for 2% of the time, Pallas kernels for 11%

profile of v14, /device:TPU:1, one launch (start us, length us, event | category | flops | bytes accessed | tf_op | source)
XLA Modules:
  0.0 69.1 jit_solution(1030229764636404445)
XLA Ops:
  0.0 0.0 copy-start.2
  0.0 0.0 copy-start.3
  0.0 7.7 %all-to-all-start = ((bf16[16,256,32]{1,2,0:T(8,128)(2,1)}), bf16[16,256,32]{1,2,0:T(8,128)(2,1)S(1)}, u32[]{:S(2)}, u32[]{:S(2)}) async-start(bf16[16,256,32]{1,2,0:T(8,128)(2,1)} %param.12), calls=%async_computation | async-start | bytes 524288 | tf_op jit(solution)/shard_map/all_to_all | solution.py:372
  7.7 0.7 %broadcast_in_dim.12 = f32[1,1280]{1,0:T(1,128)S(1)} reshape(f32[1280]{0:T(1024)} %param.20) | data formatting | bytes 10240 | tf_op jit(solution)/shard_map/broadcast_in_dim | solution.py:367
  8.4 0.8 %select_maximum_fusion = f32[7,1280]{1,0:T(8,128)S(1)} fusion(f32[1,1024]{1,0:T(1,128)} %bitcast.19, f32[1,512]{1,0:T(1,128)} %bitcast.20, f32[1,1280]{1,0:T(1,128)S(1)} %broadcast_in_dim.12, f32[4,1280]{1,0:T(4,128)} %param.19), kind=kLoop, calls=%fused_computation.2 | loop fusion | flops 80640 | bytes 67584 | tf_op jit(solution)/shard_map/concatenate | solution.py:368
  9.2 1.4 %shard_map.118 = (bf16[512,1280]{1,0:T(8,128)(2,1)S(1)}, bf16[16,512]{1,0:T(8,128)(2,1)S(1)}, f32[1,256]{1,0:T(1,128)S(1)}) custom-call(bf16[512,1280]{1,0:T(8,128)(2,1)} %refs_0_.1, bf16[16,512]{1,0:T(8,128)(2,1)} %bitcast.18, f32[1,256]{1,0:T(1,128)} %refs_2_.1), custom_call_target="tpu_custom_call" | custom-call | tf_op jit(solution)/shard_map/pallas_call | solution.py:334
  10.6 0.0 copy-done.2
  10.6 0.0 copy-done.3
  10.6 4.5 %all-to-all-done = bf16[16,256,32]{1,2,0:T(8,128)(2,1)S(1)} async-done(((bf16[16,256,32]{1,2,0:T(8,128)(2,1)}), bf16[16,256,32]{1,2,0:T(8,128)(2,1)S(1)}, u32[]{:S(2)}, u32[]{:S(2)}) %all-to-all-start) | async-done | bytes 262176 | tf_op jit(solution)/shard_map/all_to_all | solution.py:372
  15.1 0.1 shard_map.119
  15.2 5.5 %collective-permute-start = (bf16[8,512]{1,0:T(8,128)(2,1)S(1)}, bf16[8,512]{1,0:T(8,128)(2,1)S(1)}, u32[]{:S(2)}, u32[]{:S(2)}) collective-permute-start(bf16[8,512]{1,0:T(8,128)(2,1)S(1)} %shard_map.119), channel_id=1, source_target_pairs={{0,16},{16,32},{32,48},{48,64},{64,80},{80,96},{96,112},{112,128},... | collective-permute-start | bytes 24584 | tf_op jit(solution)/shard_map/ppermute | solution.py:23
  20.7 0.1 copy.15.head_ref
  20.8 2.1 %shard_map.120 = (bf16[512,256]{1,0:T(8,128)(2,1)S(1)}, bf16[1280,256]{1,0:T(8,128)(2,1)S(1)}, f32[16,256]{1,0:T(8,128)S(1)}, f32[16,256]{1,0:T(8,128)S(1)}, f32...) custom-call(bf16[512,256]{1,0:T(8,128)(2,1)S(1)} %bitcast.16, ...), custom_call_target="tpu_custom_call" | custom-call | tf_op jit(solution)/shard_map/pallas_call | solution.py:334
  22.9 0.0 collective-permute-done.edge_ref
  22.9 0.7 %shard_map.121 = (bf16[8,136,128]{2,1,0:T(8,128)(2,1)S(1)}, f32[8,1280]{1,0:T(8,128)S(1)}) custom-call(bf16[8,512]{1,0:T(8,128)(2,1)S(1)} %collective-permute-done.edge_ref, f32[8,1280]{1,0:T(8,128)S(1)} %get-tuple-element.45.first_ref, f32[8,1280]{1,0:T(8,128)S(1)} %pad.14.vec_ref, bf16[512,1280]{1,0:T(8,128)(2,1)S(1)} %get-tuple-element.41.w_xbc_ref, ...), custom_call_target="tpu_custom_call" | custom-call | tf_op jit(solution)/shard_map/pallas_call | solution.py:334
  23.6 16.6 %all_to_all.28.states_ref = bf16[8,136,128]{2,1,0:T(8,128)(2,1)S(1)} all-to-all(bf16[8,136,128]{2,1,0:T(8,128)(2,1)S(1)} %get-tuple-element.49), channel_id=1, replica_groups={{0,16,32,48,64,80,96,112},{128,144,160,176,192,208,224,240},{256,272,28..., dimensions={0} | all-to-all | bytes 557056 | tf_op jit(solution)/shard_map/all_to_all | solution.py:33
  40.3 0.1 shard_map.122.total_ref
  40.4 8.8 %collective-permute-start.1 = (bf16[136,128]{1,0:T(8,128)(2,1)S(1)}, bf16[136,128]{1,0:T(8,128)(2,1)S(1)}, u32[]{:S(2)}, u32[]{:S(2)}) collective-permute-start(bf16[136,128]{1,0:T(8,128)(2,1)S(1)} %shard_map.122.total_ref), channel_id=1, source_target_pairs={{0,128},{16,144},{32,160},{48,176},{64,192},{80,208},{96,224},{112... | collective-permute-start | bytes 104456 | tf_op jit(solution)/shard_map/ppermute | solution.py:23
  49.2 1.0 %collective-permute-done.1.earlier_ref.first_ref = bf16[136,128]{1,0:T(8,128)(2,1)S(1)} collective-permute-done((bf16[136,128]{1,0:T(8,128)(2,1)S(1)}, bf16[136,128]{1,0:T(8,128)(2,1)S(1)}, u32[]{:S(2)}, u32[]{:S(2)}) %collective-permute-start.1) | collective-permute-done | bytes 34848 | tf_op jit(solution)/shard_map/ppermute | solution.py:23
  50.2 0.7 collective-permute-start.2
  50.9 0.7 collective-permute-start.3
  51.6 0.7 collective-permute-start.4
  52.2 0.0 collective-permute-done.2.after_b_ref
  52.3 0.0 collective-permute-done.3.after_a_ref
  52.3 0.0 collective-permute-done.4.near_ref
  52.3 0.8 %shard_map.124 = bf16[8,128,128]{2,1,0:T(8,128)(2,1)} custom-call(bf16[8,136,128]{2,1,0:T(8,128)(2,1)S(1)} %all_to_all.28.states_ref, bf16[136,128]{1,0:T(8,128)(2,1)S(1)} %collective-permute-done.1.earlier_ref.first_ref, bf16[136,128]{1,0:T(8,128)(2,1)S(1)} %collective-permute-done.2.after_b_ref, bf16[136,128]{1,0:T(8,128)(2,1)S(1)} %collective-permute-done.3.after_a_ref, ...), custom_call_target="tpu_custom_call" | custom-call | tf_op jit(solution)/shard_map/pallas_call | solution.py:334
  53.1 4.7 %all-to-all-start.2 = ((bf16[8,128,128]{2,1,0:T(8,128)(2,1)}), bf16[8,128,128]{2,1,0:T(8,128)(2,1)S(1)}, u32[]{:S(2)}, u32[]{:S(2)}) async-start(bf16[8,128,128]{2,1,0:T(8,128)(2,1)} %shard_map.124), calls=%async_computation.2 | async-start | bytes 524288 | tf_op jit(solution)/shard_map/all_to_all | solution.py:33
  57.7 2.6 %shard_map.125 = (bf16[1024,256]{1,0:T(8,128)(2,1)S(1)}, f32[1024,256]{1,0:T(8,128)S(1)}, bf16[128,256]{1,0:T(8,128)(2,1)S(1)}) custom-call(bf16[512,256]{1,0:T(8,128)(2,1)S(1)} %get-tuple-element.55.normed_ref, bf16[512,1024]{1,0:T(8,128)(2,1)} %w_gate_ref.1, bf16[1280,256]{1,0:T(8,128)(2,1)S(1)} %get-tuple-element.56.main_ref, ...), custom_call_target="tpu_custom_call" | custom-call | tf_op jit(solution)/shard_map/pallas_call | solution.py:334
  60.3 0.0 copy-start
  60.3 0.8 %copy-done = bf16[1024,256]{1,0:T(8,128)(2,1)} copy-done((bf16[1024,256]{1,0:T(8,128)(2,1)}, bf16[1024,256]{1,0:T(8,128)(2,1)S(1)}, u32[]{:S(2)}) %copy-start) | copy-done | bytes 524312
  61.1 0.0 copy-start.1
  61.1 1.3 %shard_map.126.w_out_ref = bf16[1024,512]{1,0:T(8,128)(2,1)S(1)} custom-call(bf16[1024,512]{1,0:T(8,128)(2,1)} %refs_0_.2), custom_call_target="tpu_custom_call" | custom-call | tf_op jit(solution)/shard_map/pallas_call | solution.py:334
  62.4 4.9 %all-to-all-done.2 = bf16[8,128,128]{2,1,0:T(8,128)(2,1)S(1)} async-done(((bf16[8,128,128]{2,1,0:T(8,128)(2,1)}), bf16[8,128,128]{2,1,0:T(8,128)(2,1)S(1)}, u32[]{:S(2)}, u32[]{:S(2)}) %all-to-all-start.2) | async-done | bytes 262176 | tf_op jit(solution)/shard_map/all_to_all | solution.py:33
  67.3 0.0 copy-done.1
  67.3 1.8 %shard_map.127 = bf16[256,512]{1,0:T(8,128)(2,1)} custom-call(bf16[1024,128]{1,0:T(8,128)(2,1)S(1)} %bitcast.17, bf16[128,256]{1,0:T(8,128)(2,1)S(1)} %get-tuple-element.63.query_ref, bf16[1024,256]{1,0:T(8,128)(2,1)S(1)} %copy-done.1, f32[1024,256]{1,0:T(8,128)S(1)} %get-tuple-element.65.y_ref, f32[8,1280]{1,0:T(8,128)S(1)} %pad.14.vec_ref, ...), custom_call_target="tpu_custom_call" | custom-call | tf_op jit(solution)/shard_map/pallas_call | solution.py:334
  (3 shorter events, 0.0 us)
Async XLA Ops:
  0.0 10.6 %copy-start.2 = (f32[16]{0:T(128)S(1)}, f32[16]{0:T(128)}, u32[]{:S(2)}) copy-start(f32[16]{0:T(128)} %param.21) | copy-start | bytes 196
  0.0 10.6 %copy-start.3 = (f32[16]{0:T(128)S(1)}, f32[16]{0:T(128)}, u32[]{:S(2)}) copy-start(f32[16]{0:T(128)} %param.18) | copy-start | bytes 196
  0.0 15.1 %all-to-all-start = ((bf16[16,256,32]{1,2,0:T(8,128)(2,1)}), bf16[16,256,32]{1,2,0:T(8,128)(2,1)S(1)}, u32[]{:S(2)}, u32[]{:S(2)}) async-start(bf16[16,256,32]{1,2,0:T(8,128)(2,1)} %param.12), calls=%async_computation | async-start | bytes 524288 | tf_op jit(solution)/shard_map/all_to_all | solution.py:372
  15.2 7.7 %collective-permute-start = (bf16[8,512]{1,0:T(8,128)(2,1)S(1)}, bf16[8,512]{1,0:T(8,128)(2,1)S(1)}, u32[]{:S(2)}, u32[]{:S(2)}) collective-permute-start(bf16[8,512]{1,0:T(8,128)(2,1)S(1)} %shard_map.119), channel_id=1, source_target_pairs={{0,16},{16,32},{32,48},{48,64},{64,80},{80,96},{96,112},{112,128},... | collective-permute-start | bytes 24584 | tf_op jit(solution)/shard_map/ppermute | solution.py:23
  40.4 9.8 %collective-permute-start.1 = (bf16[136,128]{1,0:T(8,128)(2,1)S(1)}, bf16[136,128]{1,0:T(8,128)(2,1)S(1)}, u32[]{:S(2)}, u32[]{:S(2)}) collective-permute-start(bf16[136,128]{1,0:T(8,128)(2,1)S(1)} %shard_map.122.total_ref), channel_id=1, source_target_pairs={{0,128},{16,144},{32,160},{48,176},{64,192},{80,208},{96,224},{112... | collective-permute-start | bytes 104456 | tf_op jit(solution)/shard_map/ppermute | solution.py:23
  50.2 2.0 %collective-permute-start.2 = (bf16[136,128]{1,0:T(8,128)(2,1)S(1)}, bf16[136,128]{1,0:T(8,128)(2,1)S(1)}, u32[]{:S(2)}, u32[]{:S(2)}) collective-permute-start(bf16[136,128]{1,0:T(8,128)(2,1)S(1)} %get-tuple-element.50), channel_id=1, source_target_pairs={{128,384},{144,400},{160,416},{176,432},{192,448},{208,464},{224,4... | collective-permute-start | bytes 104456 | tf_op jit(solution)/shard_map/ppermute | solution.py:23
  50.9 1.4 %collective-permute-start.3 = (bf16[136,128]{1,0:T(8,128)(2,1)S(1)}, bf16[136,128]{1,0:T(8,128)(2,1)S(1)}, u32[]{:S(2)}, u32[]{:S(2)}) collective-permute-start(bf16[136,128]{1,0:T(8,128)(2,1)S(1)} %get-tuple-element.51), channel_id=1, source_target_pairs={{128,256},{144,272},{160,288},{176,304},{192,320},{208,336},{224,3... | collective-permute-start | bytes 104456 | tf_op jit(solution)/shard_map/ppermute | solution.py:23
  51.6 0.7 %collective-permute-start.4 = (bf16[136,128]{1,0:T(8,128)(2,1)S(1)}, bf16[136,128]{1,0:T(8,128)(2,1)S(1)}, u32[]{:S(2)}, u32[]{:S(2)}) collective-permute-start(bf16[136,128]{1,0:T(8,128)(2,1)S(1)} %get-tuple-element.52), channel_id=1, source_target_pairs={{256,384},{272,400},{288,416},{304,432},{320,448},{336,464},{352,4... | collective-permute-start | bytes 104456 | tf_op jit(solution)/shard_map/ppermute | solution.py:23
  53.1 14.2 %all-to-all-start.2 = ((bf16[8,128,128]{2,1,0:T(8,128)(2,1)}), bf16[8,128,128]{2,1,0:T(8,128)(2,1)S(1)}, u32[]{:S(2)}, u32[]{:S(2)}) async-start(bf16[8,128,128]{2,1,0:T(8,128)(2,1)} %shard_map.124), calls=%async_computation.2 | async-start | bytes 524288 | tf_op jit(solution)/shard_map/all_to_all | solution.py:33
  60.3 0.8 %copy-start = (bf16[1024,256]{1,0:T(8,128)(2,1)}, bf16[1024,256]{1,0:T(8,128)(2,1)S(1)}, u32[]{:S(2)}) copy-start(bf16[1024,256]{1,0:T(8,128)(2,1)S(1)} %get-tuple-element.64.grown_ref) | copy-start | bytes 1572868
  61.1 6.2 %copy-start.1 = (bf16[1024,256]{1,0:T(8,128)(2,1)S(1)}, bf16[1024,256]{1,0:T(8,128)(2,1)}, u32[]{:S(2)}) copy-start(bf16[1024,256]{1,0:T(8,128)(2,1)} %copy-done) | copy-start | bytes 1572868
